TPU v7x, 32 devices: a whole 2x2x4 slice. The times are simulated.
32 devices in a mesh: tm: 8 (over y, x, core), lat: 4 (over z).
Axes of the slice: x: 2, y: 2, z: 4, core: 2. Of those that a mesh axis runs over, the one named last changes fastest.
Arguments:
- noisy_state: float32 [16, 8, 64, 1024], P(None, 'tm', None, 'lat'), may hold values from -6 to 6
- w_in: bfloat16 [128, 320], replicated, may hold values from -0.3125 to 0.3125
- w_mid: bfloat16 [128, 128], replicated, may hold values from -0.5 to 0.5
- w_out: bfloat16 [320, 128], replicated, may hold values from -0.5 to 0.5
- obs_pick: int32 [8, 4, 4, 2, 128], P('tm', 'lat'), may hold values from 0 to 16383, as said below
- obs_slot: int32 [8, 4, 4, 2], P('tm', 'lat'), may hold values from 0 to 7, as said below
- observed: float32 [8, 4, 1024], P('tm', 'lat'), may hold values from -6 to 6
- precision: bfloat16 [8, 4, 1024, 1024], P('tm', 'lat'), may hold values from -1 to 9, as said below
Outputs:
- updated: float32 [16, 8, 64, 1024], P(None, 'tm', None, 'lat')
Inputs may be any that keep to these rules, and one draw needn't show every extreme that they name: `obs_pick`: within one time and band all entries are distinct; entry q names variable q // 256 at pixel q % 256 of that band. `obs_slot`: for each time, band and owner either all 2 entries are instrument positions or all equal 8 (nothing for that owner). For each time and owner, every position 0 to 7 appears exactly once over all bands, from exactly 4 bands. `precision`: Symmetric.
All inputs are finite; a program needn't handle non-finite values.
Results may differ from a plain program's by a relative error of at most 0.0053.
Values may be sent and summed in bfloat16 or wider, within the bound.
No kernel may reach another device: no remote copies, remote signals or barrier semaphores. Data moves between devices by JAX's collectives and lax.ppermute only.
A program may use at most 64 MiB of HBM per device.

v0:
```python
import jax
import jax.numpy as jnp
from jax import lax
from jax.sharding import PartitionSpec as P

WIN = 5
INST_BLOCKS = 8


def from_behind(block, axis, distance):
    devices = range(lax.axis_size(axis))
    route = [(i - distance, i) for i in devices if i - distance in devices]
    return lax.ppermute(block, axis, route)


def silu_grad(values):
    sigma = jax.nn.sigmoid(values)
    return sigma * (1.0 + values * (1.0 - sigma))


def window_of(piece):
    radius = WIN // 2
    pieces = {0: piece}
    for offset in [shift_by for shift_by in range(-radius, radius + 1) if shift_by != 0]:
        pieces[offset] = from_behind(piece, "tm", -offset)
    return jnp.concatenate([pieces[offset] for offset in range(-radius, radius + 1)], axis=1)


def window_sum(blocks):
    radius = WIN // 2
    members, width, pixels = blocks.shape
    split_blocks = blocks.reshape(members, WIN, width // WIN, pixels)
    totals = split_blocks[:, radius].astype(jnp.float32)
    for offset in [shift_by for shift_by in range(-radius, radius + 1) if shift_by != 0]:
        arrived = from_behind(split_blocks[:, offset + radius], "tm", offset)
        totals = totals + arrived.astype(jnp.float32)
    return totals


def owner_weights(arrived, observed, precision, members):
    positions = arrived.shape[0]
    vector = arrived.reshape(positions, members, -1).transpose(1, 0, 2).reshape(members, -1)
    innovation = (observed[0, 0][None, :] - vector).astype(jnp.bfloat16)
    weighted = jnp.einsum(
        "ij,mj->mi", precision[0, 0], innovation, preferred_element_type=jnp.float32
    )
    return weighted.reshape(members, positions, -1).transpose(1, 0, 2).reshape(positions, -1)


def body(noisy_state, w_in, w_mid, w_out, obs_pick, obs_slot, observed, precision):
    current = noisy_state[:, 0]
    members, channels, pixels = current.shape
    window = window_of(current.astype(jnp.bfloat16))
    pre_one = jnp.einsum("hc,mcp->mhp", w_in, window, preferred_element_type=jnp.float32)
    hidden_one = jax.nn.silu(pre_one).astype(jnp.bfloat16)
    pre_two = jnp.einsum("gh,mhp->mgp", w_mid, hidden_one, preferred_element_type=jnp.float32)
    hidden_two = jax.nn.silu(pre_two).astype(jnp.bfloat16)
    blocks = jnp.einsum(
        "ch,mhp->mcp", w_out, hidden_two, preferred_element_type=jnp.float32
    ).astype(jnp.bfloat16)
    denoised = current + window_sum(blocks)
    lanes = obs_pick.shape[2]
    pairs = obs_pick.shape[3]
    rows_block = obs_pick.shape[4]
    indices = obs_pick[0, 0].reshape(-1)
    predicted = jnp.take(denoised.reshape(members, -1), indices, axis=1)
    outgoing = (
        predicted.reshape(members, lanes * pairs, rows_block)
        .transpose(1, 0, 2)
        .reshape(lanes * pairs, members * rows_block)
    )
    packed = outgoing.reshape(lanes, pairs, members * rows_block)
    slot_values = obs_slot[0, 0].astype(jnp.float32)
    received, received_slot = (
        lax.all_to_all(packed, "lat", split_axis=0, concat_axis=0, tiled=True),
        lax.all_to_all(slot_values, "lat", split_axis=0, concat_axis=0, tiled=True),
    )
    selector = (
        jnp.arange(INST_BLOCKS, dtype=jnp.float32)[:, None] == received_slot.reshape(-1)[None, :]
    ).astype(jnp.float32)
    arrived = jnp.dot(
        selector, received.reshape(lanes * pairs, -1), precision=lax.Precision.HIGHEST
    )
    weighted = owner_weights(arrived, observed, precision, members)
    answer = jnp.dot(selector.T, weighted, precision=lax.Precision.HIGHEST).reshape(
        lanes, pairs, -1
    )
    returned = (
        lax.all_to_all(answer.astype(jnp.bfloat16), "lat", split_axis=0, concat_axis=0, tiled=True)
        .astype(answer.dtype)
        .reshape(lanes * pairs, -1)
    )
    returned_rows = (
        returned.reshape(lanes * pairs, members, rows_block).transpose(1, 0, 2).reshape(members, -1)
    )
    guidance = (
        jnp.zeros((members, channels * pixels), jnp.float32).at[:, indices].add(returned_rows)
    )
    guidance = guidance.reshape(members, channels, pixels)
    cotangent = window_of(guidance.astype(jnp.bfloat16))
    slope_one = silu_grad(pre_one)
    slope_two = silu_grad(pre_two)
    grad_two = (
        jnp.einsum("ch,mcp->mhp", w_out, cotangent, preferred_element_type=jnp.float32) * slope_two
    ).astype(jnp.bfloat16)
    grad_one = (
        jnp.einsum("gh,mgp->mhp", w_mid, grad_two, preferred_element_type=jnp.float32) * slope_one
    ).astype(jnp.bfloat16)
    back_blocks = jnp.einsum(
        "hc,mhp->mcp", w_in, grad_one, preferred_element_type=jnp.float32
    ).astype(jnp.bfloat16)
    updated = denoised + guidance + window_sum(back_blocks)
    return updated[:, None]


def solution(mesh):
    in_specs = (
        P(None, "tm", None, "lat"),
        P(),
        P(),
        P(),
        P("tm", "lat", None, None, None),
        P("tm", "lat", None, None),
        P("tm", "lat", None),
        P("tm", "lat", None, None),
    )
    out_specs = P(None, "tm", None, "lat")
    return jax.shard_map(body, mesh=mesh, in_specs=in_specs, out_specs=out_specs, check_vma=False)
```

profile of v0, /device:TPU:4, one launch (start us, length us, event | category | flops | bytes accessed | tf_op | source)
XLA Modules:
  0.0 223.6 jit_solution(16691318211252722654)
XLA Ops:
  0.0 2.2 %bitcast_convert_fusion = bf16[16,64,256]{2,1,0:T(8,128)(2,1)} fusion(f32[16,1,64,256]{3,2,1,0:T(8,128)} %param.8), kind=kLoop, calls=%fused_computation.44 | loop fusion | flops 262144 | bytes 1572864 | tf_op jit(solution)/shard_map/convert_element_type | solution.py:53
  2.2 3.4 %collective-permute-start = (bf16[16,64,256]{2,1,0:T(8,128)(2,1)}, bf16[16,64,256]{2,1,0:T(8,128)(2,1)}, u32[]{:S(2)}, u32[]{:S(2)}) collective-permute-start(bf16[16,64,256]{2,1,0:T(8,128)(2,1)} %bitcast_convert_fusion), channel_id=1, source_target_pairs={{0,8},{4,12},{8,16},{12,20},{16,24},{20,28},{1,9},{5,13},{9,17},{1... | collective-permute-start | bytes 1572872 | tf_op jit(solution)/shard_map/ppermute | solution.py:13
  5.6 1.9 collective-permute-start.1
  7.6 3.3 %collective-permute-start.3 = (bf16[16,64,256]{2,1,0:T(8,128)(2,1)}, bf16[16,64,256]{2,1,0:T(8,128)(2,1)}, u32[]{:S(2)}, u32[]{:S(2)}) collective-permute-start(bf16[16,64,256]{2,1,0:T(8,128)(2,1)} %bitcast_convert_fusion), channel_id=1, source_target_pairs={{8,0},{12,4},{16,8},{20,12},{24,16},{28,20},{9,1},{13,5},{17,9},{2... | collective-permute-start | bytes 1572872 | tf_op jit(solution)/shard_map/ppermute | solution.py:13
  10.9 3.4 %collective-permute-start.2 = (bf16[16,64,256]{2,1,0:T(8,128)(2,1)}, bf16[16,64,256]{2,1,0:T(8,128)(2,1)}, u32[]{:S(2)}, u32[]{:S(2)}) collective-permute-start(bf16[16,64,256]{2,1,0:T(8,128)(2,1)} %bitcast_convert_fusion), channel_id=1, source_target_pairs={{4,0},{8,4},{12,8},{16,12},{20,16},{24,20},{28,24},{5,1},{9,5},{13... | collective-permute-start | bytes 1572872 | tf_op jit(solution)/shard_map/ppermute | solution.py:13
  15.6 4.9 %all-to-all-start = ((f32[4,1,2]{2,1,0:T(1,128)}), f32[4,1,2]{2,1,0:T(1,128)S(1)}, u32[]{:S(2)}, u32[]{:S(2)}) async-start(f32[4,1,2]{2,1,0:T(1,128)} %copy.62), calls=%async_computation | async-start | bytes 4096 | tf_op jit(solution)/shard_map/all_to_all | solution.py:76
  20.5 1.1 constant_dynamic-update-slice_fusion.4
  21.6 7.5 %collective-permute-done.1 = bf16[16,64,256]{2,1,0:T(8,128)(2,1)} collective-permute-done((bf16[16,64,256]{2,1,0:T(8,128)(2,1)}, bf16[16,64,256]{2,1,0:T(8,128)(2,1)}, u32[]{:S(2)}, u32[]{:S(2)}) %collective-permute-start.1) | collective-permute-done | bytes 524320 | tf_op jit(solution)/shard_map/ppermute | solution.py:13
  30.3 9.3 %collective-permute-done.2 = bf16[16,64,256]{2,1,0:T(8,128)(2,1)} collective-permute-done((bf16[16,64,256]{2,1,0:T(8,128)(2,1)}, bf16[16,64,256]{2,1,0:T(8,128)(2,1)}, u32[]{:S(2)}, u32[]{:S(2)}) %collective-permute-start.2) | collective-permute-done | bytes 524320 | tf_op jit(solution)/shard_map/ppermute | solution.py:13
  40.7 1.1 constant_dynamic-update-slice_fusion
  42.9 1.4 copy-done.4
  46.5 1.5 copy-done.3
  48.0 1.4 slice_bitcast_fusion.8
  49.4 3.3 %collective-permute-start.4 = (bf16[16,64,256]{2,1,0:T(8,128)(2,1)}, bf16[16,64,256]{2,1,0:T(8,128)(2,1)}, u32[]{:S(2)}, u32[]{:S(2)}) collective-permute-start(bf16[16,64,256]{2,1,0:T(8,128)(2,1)} %get-tuple-element.9), channel_id=1, source_target_pairs={{8,0},{12,4},{16,8},{20,12},{24,16},{28,20},{9,1},{13,5},{17,9},{2... | collective-permute-start | bytes 1572872 | tf_op jit(solution)/shard_map/ppermute | solution.py:13
  52.7 3.4 %collective-permute-start.6 = (bf16[16,64,256]{2,1,0:T(8,128)(2,1)}, bf16[16,64,256]{2,1,0:T(8,128)(2,1)}, u32[]{:S(2)}, u32[]{:S(2)}) collective-permute-start(bf16[16,64,256]{2,1,0:T(8,128)(2,1)} %get-tuple-element.10), channel_id=1, source_target_pairs={{0,4},{4,8},{8,12},{12,16},{16,20},{20,24},{24,28},{1,5},{5,9},{9,... | collective-permute-start | bytes 1572872 | tf_op jit(solution)/shard_map/ppermute | solution.py:13
  56.1 3.1 %collective-permute-start.5 = (bf16[16,64,256]{2,1,0:T(8,128)(2,1)}, bf16[16,64,256]{2,1,0:T(8,128)(2,1)}, u32[]{:S(2)}, u32[]{:S(2)}) collective-permute-start(bf16[16,64,256]{2,1,0:T(8,128)(2,1)} %get-tuple-element.11), channel_id=1, source_target_pairs={{4,0},{8,4},{12,8},{16,12},{20,16},{24,20},{28,24},{5,1},{9,5},{13... | collective-permute-start | bytes 1572872 | tf_op jit(solution)/shard_map/ppermute | solution.py:13
  59.2 2.4 %collective-permute-start.7 = (bf16[16,64,256]{2,1,0:T(8,128)(2,1)}, bf16[16,64,256]{2,1,0:T(8,128)(2,1)}, u32[]{:S(2)}, u32[]{:S(2)}) collective-permute-start(bf16[16,64,256]{2,1,0:T(8,128)(2,1)} %get-tuple-element.12), channel_id=1, source_target_pairs={{0,8},{4,12},{8,16},{12,20},{16,24},{20,28},{1,9},{5,13},{9,17},{1... | collective-permute-start | bytes 1572872 | tf_op jit(solution)/shard_map/ppermute | solution.py:13
  63.0 1.5 collective-permute-done.4
  64.5 13.8 %collective-permute-done.6 = bf16[16,64,256]{2,1,0:T(8,128)(2,1)} collective-permute-done((bf16[16,64,256]{2,1,0:T(8,128)(2,1)}, bf16[16,64,256]{2,1,0:T(8,128)(2,1)}, u32[]{:S(2)}, u32[]{:S(2)}) %collective-permute-start.6) | collective-permute-done | bytes 524320 | tf_op jit(solution)/shard_map/ppermute | solution.py:13
  78.3 8.6 %collective-permute-done.7 = bf16[16,64,256]{2,1,0:T(8,128)(2,1)} collective-permute-done((bf16[16,64,256]{2,1,0:T(8,128)(2,1)}, bf16[16,64,256]{2,1,0:T(8,128)(2,1)}, u32[]{:S(2)}, u32[]{:S(2)}) %collective-permute-start.7) | collective-permute-done | bytes 524320 | tf_op jit(solution)/shard_map/ppermute | solution.py:13
  87.0 3.1 %fusion.27 = f32[16,64,256]{2,1,0:T(8,128)} fusion(f32[16,1,64,256]{3,2,1,0:T(8,128)S(1)} %copy-done.1, bf16[16,64,256]{2,1,0:T(8,128)(2,1)} %collective-permute-done.7, bf16[16,64,256]{2,1,0:T(8,128)(2,1)} %collective-permute-done.6, bf16[16,64,256]{2,1,0:T(8,128)(2,1)} %collective-permute-done.5, bf16[16,64,256]{2,1,0:T(8,128)(2,1)} %collective-permute-done.4, ...), kind=kLoop, calls=%fused_computation.43 | loop fusion | flops 2621440 | bytes 4718592 | tf_op jit(solution)/shard_map/add | solution.py:61
  90.1 6.1 %copy.79 = f32[16,64,256]{0,2,1:T(8,128)} copy(f32[16,64,256]{2,1,0:T(8,128)} %fusion.27) | data formatting | bytes 2097152 | tf_op jit(solution)/shard_map/reshape | solution.py:66
  96.1 6.2 %gather_fusion = f32[1024,16]{1,0:T(8,128)S(1)} fusion(f32[16,16384]{0,1:T(8,128)} %bitcast.177, s32[1024]{0:T(1024)S(1)} %broadcast_clamp_fusion), kind=kCustom, calls=%fused_computation | custom fusion | bytes 135168 | tf_op jit(solution)/shard_map/jit(_take)/gather | solution.py:66
  103.2 4.9 %all-to-all-start.1 = ((f32[4,2,2048]{2,1,0:T(2,128)}), f32[4,2,2048]{2,1,0:T(2,128)S(1)}, u32[]{:S(2)}, u32[]{:S(2)}) async-start(f32[4,2,2048]{2,1,0:T(2,128)} %reshape_reshape.7), calls=%async_computation.1 | async-start | bytes 131072 | tf_op jit(solution)/shard_map/all_to_all | solution.py:75
  108.1 5.8 %all-to-all-done.1 = f32[4,2,2048]{2,1,0:T(2,128)S(1)} async-done(((f32[4,2,2048]{2,1,0:T(2,128)}), f32[4,2,2048]{2,1,0:T(2,128)S(1)}, u32[]{:S(2)}, u32[]{:S(2)}) %all-to-all-start.1) | async-done | bytes 65568 | tf_op jit(solution)/shard_map/all_to_all | solution.py:75
  115.1 8.1 %all_to_all.16 = bf16[4,2,2048]{2,1,0:T(2,128)(2,1)S(1)} all-to-all(bf16[4,2,2048]{2,1,0:T(2,128)(2,1)S(1)} %copy.66), channel_id=1, replica_groups=mesh['tm'=8,'lat'=4] {'lat'}, dimensions={0} | all-to-all | bytes 65536 | tf_op jit(solution)/shard_map/all_to_all | solution.py:89
  123.5 9.8 %scatter_custom_fusion = f32[16,16384]{0,1:T(8,128)} fusion(s32[1024]{0:T(1024)S(1)} %bitcast.186, f32[1024,16]{1,0:T(8,128)S(1)} %copy.68, f32[]{:T(128)} %constant.10.clone.1), kind=kCustom, calls=%fused_computation.2 | custom fusion | flops 16384 | bytes 1048580 | tf_op jit(solution)/shard_map/scatter-add | solution.py:97
  133.3 5.3 %copy.80 = f32[16,64,256]{2,1,0:T(8,128)S(1)} copy(f32[16,64,256]{0,2,1:T(8,128)} %bitcast.176) | data formatting | bytes 2097152 | tf_op jit(solution)/shard_map/reshape | solution.py:99
  138.6 4.1 %collective-permute-start.8 = (bf16[16,64,256]{2,1,0:T(8,128)(2,1)S(1)}, bf16[16,64,256]{2,1,0:T(8,128)(2,1)S(1)}, u32[]{:S(2)}, u32[]{:S(2)}) collective-permute-start(bf16[16,64,256]{2,1,0:T(8,128)(2,1)S(1)} %convert_element_type.110), channel_id=1, source_target_pairs={{0,8},{4,12},{8,16},{12,20},{16,24},{20,28},{1,9},{5,13},{9,17},{1... | collective-permute-start | bytes 1572872 | tf_op jit(solution)/shard_map/ppermute | solution.py:13
  142.7 1.9 collective-permute-start.9
  144.7 4.5 %collective-permute-start.10 = (bf16[16,64,256]{2,1,0:T(8,128)(2,1)S(1)}, bf16[16,64,256]{2,1,0:T(8,128)(2,1)S(1)}, u32[]{:S(2)}, u32[]{:S(2)}) collective-permute-start(bf16[16,64,256]{2,1,0:T(8,128)(2,1)S(1)} %convert_element_type.110), channel_id=1, source_target_pairs={{4,0},{8,4},{12,8},{16,12},{20,16},{24,20},{28,24},{5,1},{9,5},{13... | collective-permute-start | bytes 1572872 | tf_op jit(solution)/shard_map/ppermute | solution.py:13
  149.2 2.1 collective-permute-start.11
  151.3 4.9 %collective-permute-done.8 = bf16[16,64,256]{2,1,0:T(8,128)(2,1)S(1)} collective-permute-done((bf16[16,64,256]{2,1,0:T(8,128)(2,1)S(1)}, bf16[16,64,256]{2,1,0:T(8,128)(2,1)S(1)}, u32[]{:S(2)}, u32[]{:S(2)}) %collective-permute-start.8) | collective-permute-done | bytes 524320 | tf_op jit(solution)/shard_map/ppermute | solution.py:13
  156.2 6.4 %collective-permute-done.9 = bf16[16,64,256]{2,1,0:T(8,128)(2,1)S(1)} collective-permute-done((bf16[16,64,256]{2,1,0:T(8,128)(2,1)S(1)}, bf16[16,64,256]{2,1,0:T(8,128)(2,1)S(1)}, u32[]{:S(2)}, u32[]{:S(2)}) %collective-permute-start.9) | collective-permute-done | bytes 524320 | tf_op jit(solution)/shard_map/ppermute | solution.py:13
  162.7 3.5 %collective-permute-done.10 = bf16[16,64,256]{2,1,0:T(8,128)(2,1)S(1)} collective-permute-done((bf16[16,64,256]{2,1,0:T(8,128)(2,1)S(1)}, bf16[16,64,256]{2,1,0:T(8,128)(2,1)S(1)}, u32[]{:S(2)}, u32[]{:S(2)}) %collective-permute-start.10) | collective-permute-done | bytes 524320 | tf_op jit(solution)/shard_map/ppermute | solution.py:13
  166.3 8.4 %collective-permute-done.11 = bf16[16,64,256]{2,1,0:T(8,128)(2,1)S(1)} collective-permute-done((bf16[16,64,256]{2,1,0:T(8,128)(2,1)S(1)}, bf16[16,64,256]{2,1,0:T(8,128)(2,1)S(1)}, u32[]{:S(2)}, u32[]{:S(2)}) %collective-permute-start.11) | collective-permute-done | bytes 524320 | tf_op jit(solution)/shard_map/ppermute | solution.py:13
  174.7 2.3 %fusion.3 = bf16[16,128,256]{1,2,0:T(8,128)(2,1)} fusion(f32[16,256,128]{2,1,0:T(8,128)S(1)} %copy-done.11, bf16[16,320,256]{2,1,0:T(8,128)(2,1)S(1)} %constant_dynamic-update-slice_fusion.5, bf16[320,128]{1,0:T(8,128)(2,1)S(1)} %copy-done.8), kind=kOutput, calls=%fused_computation.8 | convolution fusion | flops 340262912 | bytes 5849088 | tf_op jit(solution)/shard_map/ch,mcp->mhp/dot_general | solution.py:104
  177.0 4.7 %convolution_convert_fusion.1 = bf16[16,256,320]{1,2,0:T(8,128)(2,1)} fusion(f32[16,256,128]{2,1,0:T(8,128)} %copy-done.4, bf16[16,128,256]{1,2,0:T(8,128)(2,1)} %fusion.3, bf16[128,320]{0,1:T(8,128)(2,1)S(1)} %copy-done.5, bf16[128,128]{1,0:T(8,128)(2,1)S(1)} %copy-done.9), kind=kOutput, calls=%fused_computation.27 | convolution fusion | flops 475791360 | bytes 5881856 | tf_op jit(solution)/shard_map/hc,mhp->mcp/dot_general | solution.py:109
  181.7 1.7 slice_bitcast_fusion.3
  183.5 5.3 %collective-permute-start.12 = (bf16[16,64,256]{2,1,0:T(8,128)(2,1)S(1)}, bf16[16,64,256]{2,1,0:T(8,128)(2,1)S(1)}, u32[]{:S(2)}, u32[]{:S(2)}) collective-permute-start(bf16[16,64,256]{2,1,0:T(8,128)(2,1)S(1)} %get-tuple-element.5), channel_id=1, source_target_pairs={{8,0},{12,4},{16,8},{20,12},{24,16},{28,20},{9,1},{13,5},{17,9},{2... | collective-permute-start | bytes 1572872 | tf_op jit(solution)/shard_map/ppermute | solution.py:13
  188.8 1.9 collective-permute-start.14
  190.7 4.5 %collective-permute-start.13 = (bf16[16,64,256]{2,1,0:T(8,128)(2,1)S(1)}, bf16[16,64,256]{2,1,0:T(8,128)(2,1)S(1)}, u32[]{:S(2)}, u32[]{:S(2)}) collective-permute-start(bf16[16,64,256]{2,1,0:T(8,128)(2,1)S(1)} %get-tuple-element.7), channel_id=1, source_target_pairs={{4,0},{8,4},{12,8},{16,12},{20,16},{24,20},{28,24},{5,1},{9,5},{13... | collective-permute-start | bytes 1572872 | tf_op jit(solution)/shard_map/ppermute | solution.py:13
  195.2 1.9 collective-permute-start.15
  197.2 3.9 %collective-permute-done.12 = bf16[16,64,256]{2,1,0:T(8,128)(2,1)S(1)} collective-permute-done((bf16[16,64,256]{2,1,0:T(8,128)(2,1)S(1)}, bf16[16,64,256]{2,1,0:T(8,128)(2,1)S(1)}, u32[]{:S(2)}, u32[]{:S(2)}) %collective-permute-start.12) | collective-permute-done | bytes 524320 | tf_op jit(solution)/shard_map/ppermute | solution.py:13
  201.1 5.4 %collective-permute-done.14 = bf16[16,64,256]{2,1,0:T(8,128)(2,1)S(1)} collective-permute-done((bf16[16,64,256]{2,1,0:T(8,128)(2,1)S(1)}, bf16[16,64,256]{2,1,0:T(8,128)(2,1)S(1)}, u32[]{:S(2)}, u32[]{:S(2)}) %collective-permute-start.14) | collective-permute-done | bytes 524320 | tf_op jit(solution)/shard_map/ppermute | solution.py:13
  206.5 5.8 %collective-permute-done.13 = bf16[16,64,256]{2,1,0:T(8,128)(2,1)S(1)} collective-permute-done((bf16[16,64,256]{2,1,0:T(8,128)(2,1)S(1)}, bf16[16,64,256]{2,1,0:T(8,128)(2,1)S(1)}, u32[]{:S(2)}, u32[]{:S(2)}) %collective-permute-start.13) | collective-permute-done | bytes 524320 | tf_op jit(solution)/shard_map/ppermute | solution.py:13
  212.3 8.7 %collective-permute-done.15 = bf16[16,64,256]{2,1,0:T(8,128)(2,1)S(1)} collective-permute-done((bf16[16,64,256]{2,1,0:T(8,128)(2,1)S(1)}, bf16[16,64,256]{2,1,0:T(8,128)(2,1)S(1)}, u32[]{:S(2)}, u32[]{:S(2)}) %collective-permute-start.15) | collective-permute-done | bytes 524320 | tf_op jit(solution)/shard_map/ppermute | solution.py:13
  221.0 2.6 %fusion.23 = f32[16,1,64,256]{3,2,1,0:T(8,128)} fusion(bf16[16,64,256]{2,1,0:T(8,128)(2,1)S(1)} %collective-permute-done.15, bf16[16,64,256]{2,1,0:T(8,128)(2,1)S(1)} %collective-permute-done.14, bf16[16,64,256]{2,1,0:T(8,128)(2,1)S(1)} %collective-permute-done.13, bf16[16,64,256]{2,1,0:T(8,128)(2,1)S(1)} %collective-permute-done.12, ...), kind=kLoop, calls=%fused_computation.38 | loop fusion | flops 2883584 | bytes 5767168 | tf_op jit(solution)/shard_map/broadcast_in_dim | solution.py:113
  (61 shorter events, 10.8 us)
Async XLA Ops:
  0.0 114.2 %copy-start = (bf16[1,1,1024,1024]{3,2,1,0:T(8,128)(2,1)S(1)}, bf16[1,1,1024,1024]{3,2,1,0:T(8,128)(2,1)}, u32[]{:S(2)}) copy-start(bf16[1,1,1024,1024]{3,2,1,0:T(8,128)(2,1)} %param.15) | copy-start | bytes 6291460
  0.0 30.2 %copy-start.1 = (f32[16,1,64,256]{3,2,1,0:T(8,128)S(1)}, f32[16,1,64,256]{3,2,1,0:T(8,128)}, u32[]{:S(2)}) copy-start(f32[16,1,64,256]{3,2,1,0:T(8,128)} %param.8) | copy-start | bytes 3145732
  2.2 18.3 %collective-permute-start = (bf16[16,64,256]{2,1,0:T(8,128)(2,1)}, bf16[16,64,256]{2,1,0:T(8,128)(2,1)}, u32[]{:S(2)}, u32[]{:S(2)}) collective-permute-start(bf16[16,64,256]{2,1,0:T(8,128)(2,1)} %bitcast_convert_fusion), channel_id=1, source_target_pairs={{0,8},{4,12},{8,16},{12,20},{16,24},{20,28},{1,9},{5,13},{9,17},{1... | collective-permute-start | bytes 1572872 | tf_op jit(solution)/shard_map/ppermute | solution.py:13
  5.6 23.5 %collective-permute-start.1 = (bf16[16,64,256]{2,1,0:T(8,128)(2,1)}, bf16[16,64,256]{2,1,0:T(8,128)(2,1)}, u32[]{:S(2)}, u32[]{:S(2)}) collective-permute-start(bf16[16,64,256]{2,1,0:T(8,128)(2,1)} %bitcast_convert_fusion), channel_id=1, source_target_pairs={{0,4},{4,8},{8,12},{12,16},{16,20},{20,24},{24,28},{1,5},{5,9},{9,... | collective-permute-start | bytes 1572872 | tf_op jit(solution)/shard_map/ppermute | solution.py:13
  7.6 33.1 %collective-permute-start.3 = (bf16[16,64,256]{2,1,0:T(8,128)(2,1)}, bf16[16,64,256]{2,1,0:T(8,128)(2,1)}, u32[]{:S(2)}, u32[]{:S(2)}) collective-permute-start(bf16[16,64,256]{2,1,0:T(8,128)(2,1)} %bitcast_convert_fusion), channel_id=1, source_target_pairs={{8,0},{12,4},{16,8},{20,12},{24,16},{28,20},{9,1},{13,5},{17,9},{2... | collective-permute-start | bytes 1572872 | tf_op jit(solution)/shard_map/ppermute | solution.py:13
  10.9 28.7 %collective-permute-start.2 = (bf16[16,64,256]{2,1,0:T(8,128)(2,1)}, bf16[16,64,256]{2,1,0:T(8,128)(2,1)}, u32[]{:S(2)}, u32[]{:S(2)}) collective-permute-start(bf16[16,64,256]{2,1,0:T(8,128)(2,1)} %bitcast_convert_fusion), channel_id=1, source_target_pairs={{4,0},{8,4},{12,8},{16,12},{20,16},{24,20},{28,24},{5,1},{9,5},{13... | collective-permute-start | bytes 1572872 | tf_op jit(solution)/shard_map/ppermute | solution.py:13
  15.6 46.0 %all-to-all-start = ((f32[4,1,2]{2,1,0:T(1,128)}), f32[4,1,2]{2,1,0:T(1,128)S(1)}, u32[]{:S(2)}, u32[]{:S(2)}) async-start(f32[4,1,2]{2,1,0:T(1,128)} %copy.62), calls=%async_computation | async-start | bytes 4096 | tf_op jit(solution)/shard_map/all_to_all | solution.py:76
  20.5 21.3 %copy-start.5 = (bf16[128,320]{0,1:T(8,128)(2,1)S(1)}, bf16[128,320]{0,1:T(8,128)(2,1)}, u32[]{:S(2)}) copy-start(bf16[128,320]{0,1:T(8,128)(2,1)} %param.9) | copy-start | bytes 245764
  41.8 2.5 %copy-start.9 = (bf16[128,128]{1,0:T(8,128)(2,1)S(1)}, bf16[128,128]{1,0:T(8,128)(2,1)}, u32[]{:S(2)}) copy-start(bf16[128,128]{1,0:T(8,128)(2,1)} %param.10) | copy-start | bytes 98308
  42.9 1.4 copy-start.4
  44.2 0.9 copy-start.8
  45.1 1.3 copy-start.10
  46.5 1.5 copy-start.3
  46.5 15.1 %copy-start.6 = (s32[1,1,4,2,128]{4,3,2,1,0:T(2,128)S(1)}, s32[1,1,4,2,128]{4,3,2,1,0:T(2,128)}, u32[]{:S(2)}) copy-start(s32[1,1,4,2,128]{4,3,2,1,0:T(2,128)} %param.12) | copy-start | bytes 12292
  49.4 15.2 %collective-permute-start.4 = (bf16[16,64,256]{2,1,0:T(8,128)(2,1)}, bf16[16,64,256]{2,1,0:T(8,128)(2,1)}, u32[]{:S(2)}, u32[]{:S(2)}) collective-permute-start(bf16[16,64,256]{2,1,0:T(8,128)(2,1)} %get-tuple-element.9), channel_id=1, source_target_pairs={{8,0},{12,4},{16,8},{20,12},{24,16},{28,20},{9,1},{13,5},{17,9},{2... | collective-permute-start | bytes 1572872 | tf_op jit(solution)/shard_map/ppermute | solution.py:13
  52.7 25.6 %collective-permute-start.6 = (bf16[16,64,256]{2,1,0:T(8,128)(2,1)}, bf16[16,64,256]{2,1,0:T(8,128)(2,1)}, u32[]{:S(2)}, u32[]{:S(2)}) collective-permute-start(bf16[16,64,256]{2,1,0:T(8,128)(2,1)} %get-tuple-element.10), channel_id=1, source_target_pairs={{0,4},{4,8},{8,12},{12,16},{16,20},{20,24},{24,28},{1,5},{5,9},{9,... | collective-permute-start | bytes 1572872 | tf_op jit(solution)/shard_map/ppermute | solution.py:13
  56.1 22.2 %collective-permute-start.5 = (bf16[16,64,256]{2,1,0:T(8,128)(2,1)}, bf16[16,64,256]{2,1,0:T(8,128)(2,1)}, u32[]{:S(2)}, u32[]{:S(2)}) collective-permute-start(bf16[16,64,256]{2,1,0:T(8,128)(2,1)} %get-tuple-element.11), channel_id=1, source_target_pairs={{4,0},{8,4},{12,8},{16,12},{20,16},{24,20},{28,24},{5,1},{9,5},{13... | collective-permute-start | bytes 1572872 | tf_op jit(solution)/shard_map/ppermute | solution.py:13
  59.2 27.8 %collective-permute-start.7 = (bf16[16,64,256]{2,1,0:T(8,128)(2,1)}, bf16[16,64,256]{2,1,0:T(8,128)(2,1)}, u32[]{:S(2)}, u32[]{:S(2)}) collective-permute-start(bf16[16,64,256]{2,1,0:T(8,128)(2,1)} %get-tuple-element.12), channel_id=1, source_target_pairs={{0,8},{4,12},{8,16},{12,20},{16,24},{20,28},{1,9},{5,13},{9,17},{1... | collective-permute-start | bytes 1572872 | tf_op jit(solution)/shard_map/ppermute | solution.py:13
  90.1 23.9 %copy-start.7 = (f32[1,1,1024]{2,1,0:T(1,128)S(1)}, f32[1,1,1024]{2,1,0:T(1,128)}, u32[]{:S(2)}) copy-start(f32[1,1,1024]{2,1,0:T(1,128)} %param.14) | copy-start | bytes 12292
  103.2 10.8 %all-to-all-start.1 = ((f32[4,2,2048]{2,1,0:T(2,128)}), f32[4,2,2048]{2,1,0:T(2,128)S(1)}, u32[]{:S(2)}, u32[]{:S(2)}) async-start(f32[4,2,2048]{2,1,0:T(2,128)} %reshape_reshape.7), calls=%async_computation.1 | async-start | bytes 131072 | tf_op jit(solution)/shard_map/all_to_all | solution.py:75
  138.6 17.6 %collective-permute-start.8 = (bf16[16,64,256]{2,1,0:T(8,128)(2,1)S(1)}, bf16[16,64,256]{2,1,0:T(8,128)(2,1)S(1)}, u32[]{:S(2)}, u32[]{:S(2)}) collective-permute-start(bf16[16,64,256]{2,1,0:T(8,128)(2,1)S(1)} %convert_element_type.110), channel_id=1, source_target_pairs={{0,8},{4,12},{8,16},{12,20},{16,24},{20,28},{1,9},{5,13},{9,17},{1... | collective-permute-start | bytes 1572872 | tf_op jit(solution)/shard_map/ppermute | solution.py:13
  142.7 19.9 %collective-permute-start.9 = (bf16[16,64,256]{2,1,0:T(8,128)(2,1)S(1)}, bf16[16,64,256]{2,1,0:T(8,128)(2,1)S(1)}, u32[]{:S(2)}, u32[]{:S(2)}) collective-permute-start(bf16[16,64,256]{2,1,0:T(8,128)(2,1)S(1)} %convert_element_type.110), channel_id=1, source_target_pairs={{0,4},{4,8},{8,12},{12,16},{16,20},{20,24},{24,28},{1,5},{5,9},{9,... | collective-permute-start | bytes 1572872 | tf_op jit(solution)/shard_map/ppermute | solution.py:13
  144.7 21.6 %collective-permute-start.10 = (bf16[16,64,256]{2,1,0:T(8,128)(2,1)S(1)}, bf16[16,64,256]{2,1,0:T(8,128)(2,1)S(1)}, u32[]{:S(2)}, u32[]{:S(2)}) collective-permute-start(bf16[16,64,256]{2,1,0:T(8,128)(2,1)S(1)} %convert_element_type.110), channel_id=1, source_target_pairs={{4,0},{8,4},{12,8},{16,12},{20,16},{24,20},{28,24},{5,1},{9,5},{13... | collective-permute-start | bytes 1572872 | tf_op jit(solution)/shard_map/ppermute | solution.py:13
  149.2 25.4 %collective-permute-start.11 = (bf16[16,64,256]{2,1,0:T(8,128)(2,1)S(1)}, bf16[16,64,256]{2,1,0:T(8,128)(2,1)S(1)}, u32[]{:S(2)}, u32[]{:S(2)}) collective-permute-start(bf16[16,64,256]{2,1,0:T(8,128)(2,1)S(1)} %convert_element_type.110), channel_id=1, source_target_pairs={{8,0},{12,4},{16,8},{20,12},{24,16},{28,20},{9,1},{13,5},{17,9},{2... | collective-permute-start | bytes 1572872 | tf_op jit(solution)/shard_map/ppermute | solution.py:13
  156.2 18.5 %copy-start.11 = (f32[16,256,128]{2,1,0:T(8,128)S(1)}, f32[16,256,128]{2,1,0:T(8,128)}, u32[]{:S(2)}) copy-start(f32[16,256,128]{2,1,0:T(8,128)} %copy-done.10) | copy-start | bytes 6291460
  181.7 39.2 %copy-start.2 = (f32[16,64,256]{2,1,0:T(8,128)S(1)}, f32[16,64,256]{2,1,0:T(8,128)}, u32[]{:S(2)}) copy-start(f32[16,64,256]{2,1,0:T(8,128)} %fusion.27) | copy-start | bytes 3145732
  183.5 17.6 %collective-permute-start.12 = (bf16[16,64,256]{2,1,0:T(8,128)(2,1)S(1)}, bf16[16,64,256]{2,1,0:T(8,128)(2,1)S(1)}, u32[]{:S(2)}, u32[]{:S(2)}) collective-permute-start(bf16[16,64,256]{2,1,0:T(8,128)(2,1)S(1)} %get-tuple-element.5), channel_id=1, source_target_pairs={{8,0},{12,4},{16,8},{20,12},{24,16},{28,20},{9,1},{13,5},{17,9},{2... | collective-permute-start | bytes 1572872 | tf_op jit(solution)/shard_map/ppermute | solution.py:13
  188.8 17.7 %collective-permute-start.14 = (bf16[16,64,256]{2,1,0:T(8,128)(2,1)S(1)}, bf16[16,64,256]{2,1,0:T(8,128)(2,1)S(1)}, u32[]{:S(2)}, u32[]{:S(2)}) collective-permute-start(bf16[16,64,256]{2,1,0:T(8,128)(2,1)S(1)} %get-tuple-element.6), channel_id=1, source_target_pairs={{0,4},{4,8},{8,12},{12,16},{16,20},{20,24},{24,28},{1,5},{5,9},{9,... | collective-permute-start | bytes 1572872 | tf_op jit(solution)/shard_map/ppermute | solution.py:13
  190.7 21.6 %collective-permute-start.13 = (bf16[16,64,256]{2,1,0:T(8,128)(2,1)S(1)}, bf16[16,64,256]{2,1,0:T(8,128)(2,1)S(1)}, u32[]{:S(2)}, u32[]{:S(2)}) collective-permute-start(bf16[16,64,256]{2,1,0:T(8,128)(2,1)S(1)} %get-tuple-element.7), channel_id=1, source_target_pairs={{4,0},{8,4},{12,8},{16,12},{20,16},{24,20},{28,24},{5,1},{9,5},{13... | collective-permute-start | bytes 1572872 | tf_op jit(solution)/shard_map/ppermute | solution.py:13
  195.2 25.7 %collective-permute-start.15 = (bf16[16,64,256]{2,1,0:T(8,128)(2,1)S(1)}, bf16[16,64,256]{2,1,0:T(8,128)(2,1)S(1)}, u32[]{:S(2)}, u32[]{:S(2)}) collective-permute-start(bf16[16,64,256]{2,1,0:T(8,128)(2,1)S(1)} %get-tuple-element.8), channel_id=1, source_target_pairs={{0,8},{4,12},{8,16},{12,20},{16,24},{20,28},{1,9},{5,13},{9,17},{1... | collective-permute-start | bytes 1572872 | tf_op jit(solution)/shard_map/ppermute | solution.py:13
where the time goes:
time: 225 us; the launch traced here: 224 us
  waiting for transfers between devices  93.5 us (42%)
  starting transfers between devices  60.3 us (27%)
  local copies, waits for them, and re-layouts  31.2 us (14%)
  other arithmetic  19.4 us (9%)
  matrix products  10.6 us (5%)
  blocking collectives  8.1 us (4%)
    ppermute x16, waiting for transfers between devices, from_behind(): return lax.ppermute(block, axis, route)  87.7 us
    ppermute x16, starting transfers between devices, from_behind(): return lax.ppermute(block, axis, route)  50.6 us
    scatter-add x1, other arithmetic, body(): jnp.zeros((members, channels * pixels), jnp.float32).at[:, indices]  9.79 us
    all_to_all x1, blocking collectives, body(): lax.all_to_all(answer.astype(jnp.bfloat16), 'lat', split_axis=0, concat_a...  8.1 us
    unnamed x30, local copies, waits for them, and re-layouts  6.92 us
    gather x2, local copies, waits for them, and re-layouts, body(): predicted = jnp.take(denoised.reshape(members, -1), indices, axis=1)  6.35 us
    reshape x1, local copies, waits for them, and re-layouts, body(): predicted = jnp.take(denoised.reshape(members, -1), indices, axis=1)  6.05 us
    all_to_all x1, waiting for transfers between devices, body(): lax.all_to_all(packed, 'lat', split_axis=0, concat_axis=0, tiled=True)  5.83 us
  transfers between devices with their start and end apart: 18, of which 14 were waited for; matrix products, arithmetic and copies ran while one was open for 5% of the time, Pallas kernels for 0%

commit v1 on v0

v1 whole, which is shorter than its diff:
```python
import functools

import jax
import jax.numpy as jnp
from jax import lax
from jax.experimental import pallas as pl
from jax.experimental.pallas import tpu as pltpu
from jax.sharding import PartitionSpec as P

WIN = 5
LANES = 128
BF = jnp.bfloat16
F32 = jnp.float32


def ceil_to(value, step):
    return -(-value // step) * step


def silu_and_slope(values):
    sigma = 0.5 * jnp.tanh(0.5 * values) + 0.5
    silu = values * sigma
    return silu, sigma + silu - silu * sigma


def one_hot_rows(ref, time, base, block, count, dtype):
    width = ref.shape[2]
    per_row = width // LANES
    row = base + block // per_row
    start = (block % per_row) * LANES
    entry = ref[time, row : row + 1, start : start + LANES].astype(F32)
    index = lax.broadcasted_iota(jnp.int32, (count, LANES), 0).astype(F32)
    return index == entry


def forward_kernel(
    dims, offset_ref, recv_ref, win_ref, wmid_ref, wout_ref,
    send_ref, total_ref, slope_one_ref, slope_two_ref, padded, sums
):
    times, members, chan, width, owners, pairs, extra = dims
    radius = WIN // 2
    rows = members * chan
    blocks_obs = owners * pairs
    rows_each = blocks_obs * LANES // width
    zero_state = jnp.zeros((radius, members, chan, width), BF)
    padded[0:radius] = zero_state
    padded[radius + times :] = zero_state
    padded[radius : radius + times] = recv_ref[:, 0:rows, :].reshape(times, members, chan, width)
    sums[...] = jnp.zeros_like(sums)

    def window_step(s, carry):
        for m in range(members):
            window = padded[pl.ds(s, WIN), m].reshape(WIN * chan, width)
            pre_one = jnp.dot(win_ref[...], window, preferred_element_type=F32)
            hidden_one, slope_one = silu_and_slope(pre_one)
            pre_two = jnp.dot(wmid_ref[...], hidden_one.astype(BF), preferred_element_type=F32)
            hidden_two, slope_two = silu_and_slope(pre_two)
            blocks = jnp.dot(wout_ref[...], hidden_two.astype(BF), preferred_element_type=F32)
            sums[pl.ds(s, WIN), m] += blocks.reshape(WIN, chan, width)
            slope_one_ref[s, m] = slope_one.astype(slope_one_ref.dtype)
            slope_two_ref[s, m] = slope_two.astype(slope_two_ref.dtype)
        return carry

    lax.fori_loop(0, times, window_step, 0, unroll=times <= 8)
    offset = offset_ref[0]

    def gather_step(t, carry):
        field = sums[t + radius].reshape(rows, width)
        total_ref[t] = field
        state = (padded[t + radius].reshape(rows, width).astype(F32) + field).astype(BF)
        for o in range(owners):
            pieces = []
            for r in range(pairs):
                block = o * pairs + r
                place_row = rows + rows_each + block // (width // LANES)
                place_at = (block % (width // LANES)) * LANES
                place = recv_ref[t, place_row : place_row + 1, place_at : place_at + LANES].astype(F32)
                index = (lax.broadcasted_iota(jnp.int32, (width, LANES), 0) + offset).astype(F32)
                at_pixel = jnp.where(index == place, 1.0, 0.0).astype(BF)
                found = jnp.dot(state, at_pixel, preferred_element_type=F32)
                at_chan = one_hot_rows(recv_ref, t, rows, block, chan, F32)
                for m in range(members):
                    piece = found[m * chan : (m + 1) * chan]
                    pieces.append(jnp.sum(jnp.where(at_chan, piece, 0.0), axis=0, keepdims=True))
            for r in range(pairs):
                block = o * pairs + r
                slot_row = rows + 2 * rows_each + block // (width // LANES)
                slot_at = (block % (width // LANES)) * LANES
                pieces.append(recv_ref[t, slot_row : slot_row + 1, slot_at : slot_at + LANES].astype(F32))
            spare = send_ref.shape[1] - len(pieces)
            if spare:
                pieces.append(jnp.zeros((spare, LANES), F32))
            send_ref[t * owners + o] = jnp.concatenate(pieces, axis=0).astype(BF)
        return carry

    lax.fori_loop(0, times, gather_step, 0, unroll=times <= 8)


def owner_kernel(dims, recv_ref, observed_ref, precision_ref, send_ref, arrived, slots):
    groups, parts, members, bands, pairs, positions = dims
    for b in range(bands):
        for g in range(groups):
            tile = recv_ref[(g * parts) * bands + b].astype(F32)
            for part in range(1, parts):
                other = recv_ref[(g * parts + part) * bands + b].astype(F32)
                tile = tile + other
            for r in range(pairs):
                arrived[b * pairs + r, g * members : (g + 1) * members] = tile[r * members : (r + 1) * members]
        first = recv_ref[b].astype(F32)
        for r in range(pairs):
            row = pairs * members + r
            slots[b * pairs + r] = jnp.broadcast_to(first[row : row + 1], slots.shape[1:])
    innovation = []
    for n in range(positions):
        vector = jnp.zeros(arrived.shape[1:], F32)
        for k in range(bands * pairs):
            vector = vector + jnp.where(slots[k] == float(n), arrived[k], 0.0)
        innovation.append((observed_ref[n : n + 1] - vector).astype(BF))
    innovation = jnp.concatenate(innovation, axis=1)
    weighted = jnp.dot(innovation, precision_ref[...], preferred_element_type=F32)
    for b in range(bands):
        answers = []
        for r in range(pairs):
            slot = slots[b * pairs + r]
            answer = jnp.zeros(arrived.shape[1:], F32)
            for n in range(positions):
                answer = answer + jnp.where(slot == float(n), weighted[:, n * LANES : (n + 1) * LANES], 0.0)
            answers.append(answer)
        for g in range(groups):
            pieces = [answer[g * members : (g + 1) * members] for answer in answers]
            spare = send_ref.shape[1] - pairs * members
            if spare:
                pieces.append(jnp.zeros((spare, LANES), F32))
            tile = jnp.concatenate(pieces, axis=0).astype(BF)
            for part in range(parts):
                send_ref[(g * parts + part) * bands + b] = tile


def backward_kernel(
    dims, offset_ref, recv_ref, picks_ref, win_ref, wmid_ref, wout_ref, total_ref, slope_one_ref, slope_two_ref,
    out_ref, padded, sums
):
    times, members, chan, width, owners, pairs, extra = dims
    radius = WIN // 2
    rows = members * chan
    blocks_obs = owners * pairs
    rows_each = blocks_obs * LANES // width
    per_row = width // LANES
    zero_state = jnp.zeros((radius, members, chan, width), BF)
    padded[0:radius] = zero_state
    padded[radius + times :] = zero_state
    sums[0:radius] = jnp.zeros((radius, members, chan, width), F32)
    sums[radius + times :] = jnp.zeros((radius, members, chan, width), F32)
    offset = offset_ref[0]

    def scatter_step(t, carry):
        guidance = jnp.zeros((rows, width), F32)
        for o in range(owners):
            tile = recv_ref[t * owners + o].astype(F32)
            for r in range(pairs):
                block = o * pairs + r
                at = (block % per_row) * LANES
                chan_row = rows + block // per_row
                place_row = chan_row + rows_each
                place = picks_ref[t, place_row : place_row + 1, at : at + LANES].astype(F32)
                index = (lax.broadcasted_iota(jnp.int32, (width, LANES), 0) + offset).astype(F32)
                at_pixel = jnp.where(index == place, 1.0, 0.0).astype(BF)
                where_chan = picks_ref[t, chan_row : chan_row + 1, at : at + LANES].astype(F32)
                at_chan = lax.broadcasted_iota(jnp.int32, (chan, LANES), 0).astype(F32) == where_chan
                spread = []
                for m in range(members):
                    row = r * members + m
                    spread.append(jnp.where(at_chan, tile[row : row + 1], 0.0))
                spread = jnp.concatenate(spread, axis=0).astype(BF)
                guidance = guidance + lax.dot_general(
                    spread, at_pixel, (((1,), (1,)), ((), ())), preferred_element_type=F32
                )
        padded[t + radius] = guidance.astype(BF).reshape(members, chan, width)
        sums[t + radius] = (guidance + total_ref[t]).reshape(members, chan, width)
        return carry

    lax.fori_loop(0, times, scatter_step, 0, unroll=times <= 8)
    turned = (((0,), (0,)), ((), ()))

    def window_step(s, carry):
        for m in range(members):
            window = padded[pl.ds(s, WIN), m].reshape(WIN * chan, width)
            grad_two = lax.dot_general(wout_ref[...], window, turned, preferred_element_type=F32)
            grad_two = (grad_two * slope_two_ref[s, m].astype(F32)).astype(BF)
            grad_one = lax.dot_general(wmid_ref[...], grad_two, turned, preferred_element_type=F32)
            grad_one = (grad_one * slope_one_ref[s, m].astype(F32)).astype(BF)
            blocks = lax.dot_general(win_ref[...], grad_one, turned, preferred_element_type=F32)
            sums[pl.ds(s, WIN), m] += blocks.reshape(WIN, chan, width)
        return carry

    lax.fori_loop(0, times, window_step, 0, unroll=times <= 8)
    for t in range(times):
        out_ref[t] = sums[t + radius].reshape(rows, width).astype(BF)


def body(noisy_state, w_in, w_mid, w_out, obs_pick, obs_slot, observed, precision):
    current = noisy_state[:, 0]
    all_members, chan, pixels = current.shape
    times = lax.axis_size("tm")
    bands = lax.axis_size("lat")
    owners, pairs, block_rows = obs_pick.shape[2:]
    positions = observed.shape[2] // block_rows
    parts = max(1, times // all_members)
    groups = times // parts
    members = all_members // groups
    width = pixels // parts
    radius = WIN // 2
    rows = members * chan
    hidden = w_mid.shape[0]
    pick = obs_pick[0, 0].reshape(-1)
    slot = jnp.broadcast_to(obs_slot[0, 0][:, :, None], (owners, pairs, block_rows)).reshape(-1)
    extras = jnp.stack([pick // pixels, pick % pixels, slot]).astype(BF)
    rows_each = extras.shape[1] // width
    extra = ceil_to(3 * rows_each, 16)
    extras = extras.reshape(3 * rows_each, width)
    extras = jnp.pad(extras, ((0, extra - 3 * rows_each), (0, 0)))
    state = current.astype(BF).reshape(groups, rows, parts, width)
    state = state.transpose(0, 2, 1, 3).reshape(times, rows, width)
    payload = jnp.concatenate([state, jnp.broadcast_to(extras[None], (times, extra, width))], axis=1)
    received = lax.all_to_all(payload, "tm", split_axis=0, concat_axis=0, tiled=True)

    offset = ((lax.axis_index("tm") % parts) * width).astype(jnp.int32).reshape(1)
    dims = (times, members, chan, width, owners, pairs, extra)
    smem = pl.BlockSpec(memory_space=pltpu.SMEM)
    vmem = pl.BlockSpec(memory_space=pltpu.VMEM)
    rows_two = ceil_to(members * pairs + pairs, 8)
    packed, total, slope_one, slope_two = pl.pallas_call(
        functools.partial(forward_kernel, dims),
        out_shape=(
            jax.ShapeDtypeStruct((times * owners, rows_two, LANES), BF),
            jax.ShapeDtypeStruct((times, rows, width), F32),
            jax.ShapeDtypeStruct((times, members, hidden, width), F32),
            jax.ShapeDtypeStruct((times, members, hidden, width), F32),
        ),
        in_specs=[smem, vmem, vmem, vmem, vmem],
        out_specs=(vmem,) * 4,
        scratch_shapes=[
            pltpu.VMEM((times + 2 * radius, members, chan, width), BF),
            pltpu.VMEM((times + 2 * radius, members, chan, width), F32),
        ],
        name="forward",
    )(offset, received, w_in, w_mid, w_out)
    arrived = lax.all_to_all(packed, ("tm", "lat"), split_axis=0, concat_axis=0, tiled=True)
    rows_three = ceil_to(members * pairs, 2)
    answer = pl.pallas_call(
        functools.partial(owner_kernel, (groups, parts, members, bands, pairs, positions)),
        out_shape=jax.ShapeDtypeStruct((times * bands, rows_three, LANES), BF),
        in_specs=[vmem, vmem, vmem],
        out_specs=vmem,
        scratch_shapes=[
            pltpu.VMEM((bands * pairs, all_members, LANES), F32),
            pltpu.VMEM((bands * pairs, all_members, LANES), F32),
        ],
        name="owner",
    )(arrived, observed.reshape(positions, block_rows), precision[0, 0])
    returned = lax.all_to_all(answer, ("tm", "lat"), split_axis=0, concat_axis=0, tiled=True)
    change = pl.pallas_call(
        functools.partial(backward_kernel, dims),
        out_shape=jax.ShapeDtypeStruct((times, rows, width), BF),
        in_specs=[smem] + [vmem] * 8,
        out_specs=vmem,
        scratch_shapes=[
            pltpu.VMEM((times + 2 * radius, members, chan, width), BF),
            pltpu.VMEM((times + 2 * radius, members, chan, width), F32),
        ],
        name="backward",
    )(offset, returned, received, w_in, w_mid, w_out, total, slope_one, slope_two)
    back = lax.all_to_all(change, "tm", split_axis=0, concat_axis=0, tiled=True)
    back = back.reshape(groups, parts, members, chan, width).transpose(0, 2, 3, 1, 4)
    updated = current + back.reshape(all_members, chan, pixels).astype(F32)
    return updated[:, None]


def solution(mesh):
    in_specs = (
        P(None, "tm", None, "lat"),
        P(),
        P(),
        P(),
        P("tm", "lat", None, None, None),
        P("tm", "lat", None, None),
        P("tm", "lat", None),
        P("tm", "lat", None, None),
    )
    out_specs = P(None, "tm", None, "lat")
    return jax.shard_map(body, mesh=mesh, in_specs=in_specs, out_specs=out_specs, check_vma=False)
```

time: 225 us -> 76.1 us (0.34)
  the two profiles are of different devices: /device:TPU:4 before, /device:TPU:0 now
where the time goes in v1:
time: 76.1 us; the launch traced here: 75.6 us
  blocking collectives  35.2 us (46%)
  Pallas kernels  19 us (25%)
  waiting for transfers between devices  9.65 us (13%)
  starting transfers between devices  5.2 us (7%)
  other arithmetic  4.71 us (6%)
  local copies, waits for them, and re-layouts  1.82 us (2%)
    all_to_all x1, blocking collectives, body(): back = lax.all_to_all(change, 'tm', split_axis=0, concat_axis=0, tiled=True)  13.1 us
    all_to_all x1, blocking collectives, body(): lax.all_to_all(packed, ('tm', 'lat'), split_axis=0, concat_axis=0, tiled=...  11.6 us
    all_to_all x1, blocking collectives, body(): lax.all_to_all(answer, ('tm', 'lat'), split_axis=0, concat_axis=0, tiled=...  10.5 us
    all_to_all x1, waiting for transfers between devices, body(): lax.all_to_all(payload, 'tm', split_axis=0, concat_axis=0, tiled=True)  9.65 us
    pallas_call x1, Pallas kernels, body(): pl.pallas_call(functools.partial(backward_kernel, dims), out_shape=jax.Sh...  8.83 us
    pallas_call x1, Pallas kernels, body(): pl.pallas_call(functools.partial(forward_kernel, dims), out_shape=(jax.Sh...  7.47 us
    all_to_all x1, starting transfers between devices, body(): lax.all_to_all(payload, 'tm', split_axis=0, concat_axis=0, tiled=True)  5.2 us
    pallas_call x1, Pallas kernels, body(): pl.pallas_call(functools.partial(owner_kernel, (groups, parts, members, b...  2.71 us
  transfers between devices with their start and end apart: 1, of which 1 were waited for; matrix products, arithmetic and copies ran while one was open for 1% of the time, Pallas kernels for 0%

profile of v1, /device:TPU:0, one launch (start us, length us, event | category | flops | bytes accessed | tf_op | source)
XLA Modules:
  0.0 75.6 jit_solution(6607431334922122408)
XLA Ops:
  0.0 0.0 copy-start.2
  0.0 0.7 convert_bitcast_fusion
  0.7 0.1 copy.9
  0.8 0.1 broadcast_in_dim.7
  0.9 0.7 fusion.1
  1.7 1.3 %convert_element_type.27 = bf16[16,1,64,256]{3,2,1,0:T(8,128)(2,1)S(1)} convert(f32[16,1,64,256]{3,2,1,0:T(8,128)} %param.8) | non-fusion elementwise | flops 262144 | bytes 1572864 | tf_op jit(solution)/shard_map/convert_element_type | solution.py:222
  3.0 0.9 %pad_maximum_fusion = bf16[8,144,256]{2,1,0:T(8,128)(2,1)} fusion(bf16[8,16,256]{2,1,0:T(8,128)(2,1)S(1)} %broadcast_in_dim.16, bf16[8,128,256]{2,1,0:T(8,128)(2,1)S(1)} %bitcast.11), kind=kLoop, calls=%fused_computation.1 | loop fusion | flops 1179648 | bytes 1179648 | tf_op jit(solution)/shard_map/concatenate | solution.py:224
  3.9 5.2 %all-to-all-start = ((bf16[8,144,256]{2,1,0:T(8,128)(2,1)}), bf16[8,144,256]{2,1,0:T(8,128)(2,1)S(1)}, u32[]{:S(2)}, u32[]{:S(2)}) async-start(bf16[8,144,256]{2,1,0:T(8,128)(2,1)} %pad_maximum_fusion), calls=%async_computation | async-start | bytes 1179648 | tf_op jit(solution)/shard_map/all_to_all | solution.py:225
  9.1 0.0 copy-done.2
  9.1 0.8 %copy.10.win_ref = bf16[128,320]{1,0:T(8,128)(2,1)} copy(bf16[128,320]{0,1:T(8,128)(2,1)S(1)} %copy-done.2) | data formatting | bytes 163840 | tf_op args[1]
  9.8 9.6 %all-to-all-done.recv_ref.picks_ref = bf16[8,144,256]{2,1,0:T(8,128)(2,1)S(1)} async-done(((bf16[8,144,256]{2,1,0:T(8,128)(2,1)}), bf16[8,144,256]{2,1,0:T(8,128)(2,1)S(1)}, u32[]{:S(2)}, u32[]{:S(2)}) %all-to-all-start) | async-done | bytes 589856 | tf_op jit(solution)/shard_map/all_to_all | solution.py:225
  19.5 0.0 copy-start
  19.5 0.8 %copy-done = bf16[8,144,256]{2,1,0:T(8,128)(2,1)} copy-done((bf16[8,144,256]{2,1,0:T(8,128)(2,1)}, bf16[8,144,256]{2,1,0:T(8,128)(2,1)S(1)}, u32[]{:S(2)}) %copy-start) | copy-done | bytes 589848
  20.3 7.5 %forward.1 = (bf16[32,8,128]{2,1,0:T(8,128)(2,1)}, f32[8,128,256]{2,1,0:T(8,128)}, f32[8,2,128,256]{3,2,1,0:T(8,128)}, f32[8,2,128,256]{3,2,1,0:T(8,128)}) custom-call(s32[1]{0:T(128)} %constant.40.clone.1.offset_ref, bf16[8,144,256]{2,1,0:T(8,128)(2,1)} %copy-done, bf16[128,320]{1,0:T(8,128)(2,1)} %copy.10.win_ref, bf16[128,128]{1,0:T(8,128)(2,1)} %wmid_ref.3, ...), custom_call_target="tpu_custom_call" | custom-call | tf_op jit(solution)/shard_map/forward/pallas_call | solution.py:232
  27.8 11.6 %all_to_all.20.recv_ref = bf16[32,8,128]{2,1,0:T(8,128)(2,1)} all-to-all(bf16[32,8,128]{2,1,0:T(8,128)(2,1)} %get-tuple-element.9), channel_id=1, replica_groups=mesh['tm'=8,'lat'=4] {'tm','lat'}, dimensions={0} | all-to-all | bytes 131072 | tf_op jit(solution)/shard_map/all_to_all | solution.py:248
  39.4 2.7 %owner.1 = bf16[32,4,128]{2,1,0:T(4,128)(2,1)} custom-call(bf16[32,8,128]{2,1,0:T(8,128)(2,1)} %all_to_all.20.recv_ref, f32[8,128]{1,0:T(8,128)} %bitcast.14, bf16[1024,1024]{1,0:T(8,128)(2,1)} %bitcast.13), custom_call_target="tpu_custom_call" | custom-call | tf_op jit(solution)/shard_map/owner/pallas_call | solution.py:250
  42.1 10.5 %all_to_all.21.recv_ref = bf16[32,4,128]{2,1,0:T(4,128)(2,1)} all-to-all(bf16[32,4,128]{2,1,0:T(4,128)(2,1)} %owner.1), channel_id=1, replica_groups=mesh['tm'=8,'lat'=4] {'tm','lat'}, dimensions={0} | all-to-all | bytes 65536 | tf_op jit(solution)/shard_map/all_to_all | solution.py:261
  52.6 0.0 copy-start.1
  52.6 8.8 %backward.1 = bf16[8,128,256]{2,1,0:T(8,128)(2,1)} custom-call(s32[1]{0:T(128)} %constant.40.clone.1.offset_ref, bf16[32,4,128]{2,1,0:T(4,128)(2,1)} %all_to_all.21.recv_ref, bf16[8,144,256]{2,1,0:T(8,128)(2,1)} %copy-done, bf16[128,320]{1,0:T(8,128)(2,1)} %copy.10.win_ref, bf16[128,128]{1,0:T(8,128)(2,1)} %wmid_ref.3, bf16[320,128]{1,0:T(8,128)(2,1)} %wout_ref.3, ...), custom_call_target="tpu_custom_call" | custom-call | tf_op jit(solution)/shard_map/backward/pallas_call | solution.py:262
  61.4 13.1 %all_to_all.22 = bf16[8,128,256]{2,1,0:T(8,128)(2,1)S(1)} all-to-all(bf16[8,128,256]{2,1,0:T(8,128)(2,1)} %backward.1), channel_id=1, replica_groups=mesh['tm'=8,'lat'=4] {'tm'}, dimensions={0} | all-to-all | bytes 1048576 | tf_op jit(solution)/shard_map/all_to_all | solution.py:273
  74.5 0.0 copy-done.1
  74.5 1.1 %convert_add_fusion = f32[16,1,64,256]{3,2,1,0:T(8,128)} fusion(f32[16,1,64,256]{3,2,1,0:T(8,128)S(1)} %copy-done.1, bf16[16,1,64,256]{3,2,1,0:T(8,128)(2,1)S(1)} %bitcast.12), kind=kLoop, calls=%fused_computation | loop fusion | flops 524288 | bytes 2621440 | tf_op jit(solution)/shard_map/add | solution.py:275
  (6 shorter events, 0.1 us)
Async XLA Ops:
  0.0 9.1 %copy-start.2 = (bf16[128,320]{0,1:T(8,128)(2,1)S(1)}, bf16[128,320]{0,1:T(8,128)(2,1)}, u32[]{:S(2)}) copy-start(bf16[128,320]{0,1:T(8,128)(2,1)} %param.9) | copy-start | bytes 245764
  3.9 15.6 %all-to-all-start = ((bf16[8,144,256]{2,1,0:T(8,128)(2,1)}), bf16[8,144,256]{2,1,0:T(8,128)(2,1)S(1)}, u32[]{:S(2)}, u32[]{:S(2)}) async-start(bf16[8,144,256]{2,1,0:T(8,128)(2,1)} %pad_maximum_fusion), calls=%async_computation | async-start | bytes 1179648 | tf_op jit(solution)/shard_map/all_to_all | solution.py:225
  19.5 0.8 %copy-start = (bf16[8,144,256]{2,1,0:T(8,128)(2,1)}, bf16[8,144,256]{2,1,0:T(8,128)(2,1)S(1)}, u32[]{:S(2)}) copy-start(bf16[8,144,256]{2,1,0:T(8,128)(2,1)S(1)} %all-to-all-done.recv_ref.picks_ref) | copy-start | bytes 1769476
  52.6 21.9 %copy-start.1 = (f32[16,1,64,256]{3,2,1,0:T(8,128)S(1)}, f32[16,1,64,256]{3,2,1,0:T(8,128)}, u32[]{:S(2)}) copy-start(f32[16,1,64,256]{3,2,1,0:T(8,128)} %param.8) | copy-start | bytes 3145732

commit v2 on v1

v2 whole, which is shorter than its diff:
```python
import functools

import jax
import jax.numpy as jnp
from jax import lax
from jax.experimental import pallas as pl
from jax.experimental.pallas import tpu as pltpu
from jax.sharding import PartitionSpec as P

WIN = 5
LANES = 128
BF = jnp.bfloat16
F32 = jnp.float32


def limit(mib):
    return pltpu.CompilerParams(vmem_limit_bytes=mib * 2**20)


def ceil_to(value, step):
    return -(-value // step) * step


def silu(values):
    half = 0.5 * values
    return half + half * jnp.tanh(half)


def silu_slope(values):
    half = 0.5 * values
    bend = jnp.tanh(half)
    return (0.5 + 0.5 * bend) * (1.0 + half * (1.0 - bend))


def loop(count, step):
    if count <= 8:
        for index in range(count):
            step(index)
    else:
        lax.fori_loop(0, count, lambda index, carry: (step(index), carry)[1], 0)


def pack_kernel(
    dims, state_hbm, pick_hbm, slot_hbm, win_turned_hbm, wmid_hbm, wout_hbm,
    out, win_ref, wmid_turned_ref, wout_turned_ref,
    state, pick_vmem, slot_ref, win_turned, wmid, wout, state_sems, sems
):
    groups, parts, members, chan, width, owners, pairs, extra = dims
    rows = members * chan
    per_row = width // LANES
    rows_each = owners * pairs // per_row
    chunks = state_sems.shape[0]
    step = groups // chunks
    small = []
    pairs_of = ((pick_hbm, pick_vmem), (slot_hbm, slot_ref), (win_turned_hbm, win_turned), (wmid_hbm, wmid), (wout_hbm, wout))
    for index, (source, target) in enumerate(pairs_of[:2]):
        small.append(pltpu.make_async_copy(source, target, sems.at[index]))
        small[-1].start()
    copies = []
    for c in range(chunks):
        span = pl.ds(c * step * members, step * members)
        copies.append(pltpu.make_async_copy(state_hbm.at[span], state.at[span], state_sems.at[c]))
        copies[-1].start()
    for index, (source, target) in enumerate(pairs_of):
        if index >= 2:
            small.append(pltpu.make_async_copy(source, target, sems.at[index]))
            small[-1].start()
    small[0].wait()
    small[1].wait()
    pick = pick_vmem[...].astype(F32)
    channel = jnp.floor((pick + 0.5) * (1.0 / (width * parts)))
    place = pick - channel * (width * parts)
    lines = []
    for values in (channel, place):
        for row in range(rows_each):
            cells = [divmod(row * per_row + k, pairs) for k in range(per_row)]
            lines.append(jnp.concatenate([values[o, r : r + 1] for o, r in cells], axis=1))
    for row in range(rows_each):
        cells = [divmod(row * per_row + k, pairs) for k in range(per_row)]
        lines.append(jnp.concatenate([jnp.full((1, LANES), slot_ref[r, o].astype(F32)) for o, r in cells], axis=1))
    if extra > len(lines):
        lines.append(jnp.zeros((extra - len(lines), width), F32))
    lines = jnp.concatenate(lines, axis=0).astype(BF)
    for d in range(groups * parts):
        out[d, rows:] = lines
    for c in range(chunks):
        copies[c].wait()
        for g in range(c * step, (c + 1) * step):
            block = state[g * members : (g + 1) * members].astype(BF)
            for part in range(parts):
                piece = block[:, :, part * width : (part + 1) * width]
                out[g * parts + part, 0:rows] = piece.reshape(rows, width)
    for copy in small[2:]:
        copy.wait()
    win_ref[...] = win_turned[...].T
    wmid_turned_ref[...] = wmid[...].T
    wout_turned_ref[...] = wout[...].T


def row_of(ref, time, base, block):
    per_row = ref.shape[2] // LANES
    row = base + block // per_row
    start = (block % per_row) * LANES
    return ref[time, row : row + 1, start : start + LANES].astype(F32)


def forward_kernel(
    dims, offset_ref, recv_ref, win_ref, wmid_ref, wout_ref,
    send_ref, total_ref, pre_one_ref, pre_two_ref, at_pixel_ref, padded, sums, hidden_one, hidden_two
):
    times, members, chan, width, owners, pairs, extra = dims
    radius = WIN // 2
    rows = members * chan
    rows_each = owners * pairs * LANES // width
    zero_state = jnp.zeros((radius, members, chan, width), BF)
    padded[0:radius] = zero_state
    padded[radius + times :] = zero_state
    padded[radius : radius + times] = recv_ref[:, 0:rows, :].reshape(times, members, chan, width)
    sums[...] = jnp.zeros_like(sums)

    def first(s):
        for m in range(members):
            window = padded[pl.ds(s, WIN), m].reshape(WIN * chan, width)
            pre_one = jnp.dot(win_ref[...], window, preferred_element_type=F32)
            pre_one_ref[s, m] = pre_one
            hidden_one[s, m] = silu(pre_one).astype(BF)

    def second(s):
        for m in range(members):
            pre_two = jnp.dot(wmid_ref[...], hidden_one[s, m], preferred_element_type=F32)
            pre_two_ref[s, m] = pre_two
            hidden_two[s, m] = silu(pre_two).astype(BF)

    def third(s):
        for m in range(members):
            blocks = jnp.dot(wout_ref[...], hidden_two[s, m], preferred_element_type=F32)
            sums[pl.ds(s, WIN), m] += blocks.reshape(WIN, chan, width)

    offset = offset_ref[0]
    eight = 8

    def gather(t):
        field = sums[t + radius]
        total_ref[t] = field.reshape(rows, width)
        state = (padded[t + radius].astype(F32) + field).astype(BF).reshape(rows, width)
        index = (lax.broadcasted_iota(jnp.int32, (width, LANES), 0) + offset).astype(F32)
        for o in range(owners):
            lines = []
            for r in range(pairs):
                place = row_of(recv_ref, t, rows + rows_each, o * pairs + r)
                lines.append(jnp.where(index == place, 1.0, 0.0).astype(BF))
            at_pixel = jnp.concatenate(lines, axis=1)
            at_pixel_ref[t, :, o * pairs * LANES : (o + 1) * pairs * LANES] = at_pixel
            found = jnp.dot(state, at_pixel, preferred_element_type=F32)
            pieces = []
            for r in range(pairs):
                channel = row_of(recv_ref, t, rows, o * pairs + r)
                high = jnp.floor(channel * (1.0 / eight))
                at_row = lax.broadcasted_iota(jnp.int32, (eight, LANES), 0).astype(F32) == channel - high * eight
                high = jnp.broadcast_to(high, (eight, LANES))
                span = slice(r * LANES, (r + 1) * LANES)
                picked = [found[m * chan : m * chan + eight, span] for m in range(members)]
                for c in range(1, chan // eight):
                    here = high == float(c)
                    for m in range(members):
                        start = m * chan + c * eight
                        picked[m] = jnp.where(here, found[start : start + eight, span], picked[m])
                for m in range(members):
                    pieces.append(jnp.sum(jnp.where(at_row, picked[m], 0.0), axis=0, keepdims=True))
            for r in range(pairs):
                pieces.append(row_of(recv_ref, t, rows + 2 * rows_each, o * pairs + r))
            spare = send_ref.shape[1] - len(pieces)
            if spare:
                pieces.append(jnp.zeros((spare, LANES), F32))
            send_ref[t * owners + o] = jnp.concatenate(pieces, axis=0).astype(BF)

    loop(times, first)
    loop(times, second)
    loop(times, third)
    loop(times, gather)


def owner_kernel(dims, recv_ref, observed_ref, precision_ref, send_ref, arrived, slots):
    groups, parts, members, bands, pairs, positions = dims
    for b in range(bands):
        for g in range(groups):
            tile = recv_ref[(g * parts) * bands + b].astype(F32)
            for part in range(1, parts):
                other = recv_ref[(g * parts + part) * bands + b].astype(F32)
                tile = tile + other
            for r in range(pairs):
                arrived[b * pairs + r, g * members : (g + 1) * members] = tile[r * members : (r + 1) * members]
        first = recv_ref[b].astype(F32)
        for r in range(pairs):
            row = pairs * members + r
            slots[b * pairs + r] = jnp.broadcast_to(first[row : row + 1], slots.shape[1:])
    innovation = []
    for n in range(positions):
        vector = jnp.zeros(arrived.shape[1:], F32)
        for k in range(bands * pairs):
            vector = vector + jnp.where(slots[k] == float(n), arrived[k], 0.0)
        innovation.append((observed_ref[n : n + 1] - vector).astype(BF))
    innovation = jnp.concatenate(innovation, axis=1)
    weighted = jnp.dot(innovation, precision_ref[...], preferred_element_type=F32)
    for b in range(bands):
        answers = []
        for r in range(pairs):
            slot = slots[b * pairs + r]
            answer = jnp.zeros(arrived.shape[1:], F32)
            for n in range(positions):
                answer = answer + jnp.where(slot == float(n), weighted[:, n * LANES : (n + 1) * LANES], 0.0)
            answers.append(answer)
        for g in range(groups):
            pieces = [answer[g * members : (g + 1) * members] for answer in answers]
            spare = send_ref.shape[1] - pairs * members
            if spare:
                pieces.append(jnp.zeros((spare, LANES), F32))
            tile = jnp.concatenate(pieces, axis=0).astype(BF)
            for part in range(parts):
                send_ref[(g * parts + part) * bands + b] = tile


def backward_kernel(
    dims, recv_ref, picks_ref, at_pixel_ref, win_ref, wmid_ref, wout_ref, total_ref, pre_one_ref, pre_two_ref,
    out_ref, padded, sums, grad_one, grad_two
):
    times, members, chan, width, owners, pairs, extra = dims
    radius = WIN // 2
    rows = members * chan
    zero_state = jnp.zeros((radius, members, chan, width), BF)
    padded[0:radius] = zero_state
    padded[radius + times :] = zero_state
    sums[0:radius] = jnp.zeros((radius, members, chan, width), F32)
    sums[radius + times :] = jnp.zeros((radius, members, chan, width), F32)

    def scatter(t):
        spread = []
        index = lax.broadcasted_iota(jnp.int32, (chan, LANES), 0).astype(F32)
        for o in range(owners):
            tile = recv_ref[t * owners + o].astype(F32)
            for r in range(pairs):
                at_chan = index == row_of(picks_ref, t, rows, o * pairs + r)
                pieces = []
                for m in range(members):
                    row = r * members + m
                    pieces.append(jnp.where(at_chan, tile[row : row + 1], 0.0).astype(BF))
                spread.append(jnp.concatenate(pieces, axis=0))
        spread = jnp.concatenate(spread, axis=1)
        guidance = lax.dot_general(
            spread, at_pixel_ref[t], (((1,), (1,)), ((), ())), preferred_element_type=F32
        )
        padded[t + radius] = guidance.astype(BF).reshape(members, chan, width)
        sums[t + radius] = (guidance + total_ref[t]).reshape(members, chan, width)

    def first(s):
        for m in range(members):
            window = padded[pl.ds(s, WIN), m].reshape(WIN * chan, width)
            grad = jnp.dot(wout_ref[...], window, preferred_element_type=F32)
            grad_two[s, m] = (grad * silu_slope(pre_two_ref[s, m])).astype(BF)

    def second(s):
        for m in range(members):
            grad = jnp.dot(wmid_ref[...], grad_two[s, m], preferred_element_type=F32)
            grad_one[s, m] = (grad * silu_slope(pre_one_ref[s, m])).astype(BF)

    def third(s):
        for m in range(members):
            blocks = jnp.dot(win_ref[...], grad_one[s, m], preferred_element_type=F32)
            sums[pl.ds(s, WIN), m] += blocks.reshape(WIN, chan, width)

    loop(times, scatter)
    loop(times, first)
    loop(times, second)
    loop(times, third)

    def finish(t):
        out_ref[t] = sums[t + radius].reshape(rows, width).astype(BF)

    loop(times, finish)


def body(noisy_state, w_in, w_mid, w_out, obs_pick, obs_slot, observed, precision):
    current = noisy_state[:, 0]
    all_members, chan, pixels = current.shape
    times = lax.axis_size("tm")
    bands = lax.axis_size("lat")
    owners, pairs, block_rows = obs_pick.shape[2:]
    positions = observed.shape[2] // block_rows
    parts = max(1, times // all_members)
    groups = times // parts
    members = all_members // groups
    width = pixels // parts
    radius = WIN // 2
    rows = members * chan
    hidden = w_mid.shape[0]
    extra = ceil_to(3 * owners * pairs * block_rows // width, 16)
    smem = pl.BlockSpec(memory_space=pltpu.SMEM)
    vmem = pl.BlockSpec(memory_space=pltpu.VMEM)
    hbm = pl.BlockSpec(memory_space=pltpu.HBM)
    chunks = 4 if groups % 4 == 0 else 1
    payload, win, wmid_turned, wout_turned = pl.pallas_call(
        functools.partial(pack_kernel, (groups, parts, members, chan, width, owners, pairs, extra)),
        out_shape=(
            jax.ShapeDtypeStruct((times, rows + extra, width), BF),
            jax.ShapeDtypeStruct(w_in.shape, BF),
            jax.ShapeDtypeStruct(w_mid.shape[::-1], BF),
            jax.ShapeDtypeStruct(w_out.shape[::-1], BF),
        ),
        in_specs=[hbm] * 6,
        out_specs=(vmem,) * 4,
        scratch_shapes=[
            pltpu.VMEM(current.shape, F32),
            pltpu.VMEM((owners, pairs, block_rows), jnp.int32),
            pltpu.SMEM((pairs, owners), jnp.int32),
            pltpu.VMEM(w_in.shape[::-1], BF),
            pltpu.VMEM(w_mid.shape, BF),
            pltpu.VMEM(w_out.shape, BF),
            pltpu.SemaphoreType.DMA((chunks,)),
            pltpu.SemaphoreType.DMA((5,)),
        ],
        compiler_params=limit(16),
        name="pack",
    )(*(pltpu.with_memory_space_constraint(x, pltpu.HBM) for x in (current, obs_pick[0, 0], obs_slot[0, 0].T, w_in.T, w_mid, w_out)))
    received = lax.all_to_all(payload, "tm", split_axis=0, concat_axis=0, tiled=True)

    offset = ((lax.axis_index("tm") % parts) * width).astype(jnp.int32).reshape(1)
    dims = (times, members, chan, width, owners, pairs, extra)
    rows_two = ceil_to(members * pairs + pairs, 8)
    inner = (times, members, hidden, width)
    padded_shape = (times + 2 * radius, members, chan, width)
    packed, total, pre_one, pre_two, at_pixel = pl.pallas_call(
        functools.partial(forward_kernel, dims),
        out_shape=(
            jax.ShapeDtypeStruct((times * owners, rows_two, LANES), BF),
            jax.ShapeDtypeStruct((times, rows, width), F32),
            jax.ShapeDtypeStruct(inner, F32),
            jax.ShapeDtypeStruct(inner, F32),
            jax.ShapeDtypeStruct((times, width, owners * pairs * block_rows), BF),
        ),
        in_specs=[smem, vmem, vmem, vmem, vmem],
        out_specs=(vmem,) * 5,
        scratch_shapes=[
            pltpu.VMEM(padded_shape, BF),
            pltpu.VMEM(padded_shape, F32),
            pltpu.VMEM(inner, BF),
            pltpu.VMEM(inner, BF),
        ],
        compiler_params=limit(24),
        name="forward",
    )(offset, received, win, w_mid, w_out)
    arrived = lax.all_to_all(packed, ("tm", "lat"), split_axis=0, concat_axis=0, tiled=True)
    rows_three = ceil_to(members * pairs, 2)
    answer = pl.pallas_call(
        functools.partial(owner_kernel, (groups, parts, members, bands, pairs, positions)),
        out_shape=jax.ShapeDtypeStruct((times * bands, rows_three, LANES), BF),
        in_specs=[vmem, vmem, vmem],
        out_specs=vmem,
        scratch_shapes=[
            pltpu.VMEM((bands * pairs, all_members, LANES), F32),
            pltpu.VMEM((bands * pairs, all_members, LANES), F32),
        ],
        compiler_params=limit(16),
        name="owner",
    )(arrived, observed.reshape(positions, block_rows), precision[0, 0])
    returned = lax.all_to_all(answer, ("tm", "lat"), split_axis=0, concat_axis=0, tiled=True)
    change = pl.pallas_call(
        functools.partial(backward_kernel, dims),
        out_shape=jax.ShapeDtypeStruct((times, rows, width), BF),
        in_specs=[vmem] * 9,
        out_specs=vmem,
        scratch_shapes=[
            pltpu.VMEM(padded_shape, BF),
            pltpu.VMEM(padded_shape, F32),
            pltpu.VMEM(inner, BF),
            pltpu.VMEM(inner, BF),
        ],
        compiler_params=limit(24),
        name="backward",
    )(returned, received, at_pixel, w_in.T, wmid_turned, wout_turned, total, pre_one, pre_two)
    back = lax.all_to_all(change, "tm", split_axis=0, concat_axis=0, tiled=True)
    back = back.reshape(groups, parts, members, chan, width).transpose(0, 2, 3, 1, 4)
    updated = current + back.reshape(all_members, chan, pixels).astype(F32)
    return updated[:, None]


def solution(mesh):
    in_specs = (
        P(None, "tm", None, "lat"),
        P(),
        P(),
        P(),
        P("tm", "lat", None, None, None),
        P("tm", "lat", None, None),
        P("tm", "lat", None),
        P("tm", "lat", None, None),
    )
    out_specs = P(None, "tm", None, "lat")
    return jax.shard_map(body, mesh=mesh, in_specs=in_specs, out_specs=out_specs, check_vma=False)
```

time: 76.1 us -> 58.4 us (0.77)
  blocking collectives: 35.2 us -> 48 us
  Pallas kernels: 19 us -> 9.07 us
  waiting for transfers between devices: 9.65 us -> 0 us
  starting transfers between devices: 5.2 us -> 0 us
  other arithmetic: 4.71 us -> 1.08 us
  local copies, waits for them, and re-layouts: 1.82 us -> 0.02 us
    all_to_all x0 -> x1, blocking collectives: none -> 15.6 us  [body(): lax.all_to_all(payload, 'tm', split_axis=0, concat_axis=0, tiled=True)]
    all_to_all x1 -> x0, waiting for transfers between devices: 9.65 us -> none  [body(): lax.all_to_all(payload, 'tm', split_axis=0, concat_axis=0, tiled=True)]
    all_to_all x1 -> x0, starting transfers between devices: 5.2 us -> none  [body(): lax.all_to_all(payload, 'tm', split_axis=0, concat_axis=0, tiled=True)]
    pallas_call x1, Pallas kernels: 8.83 us -> 3.74 us  [body(): pl.pallas_call(functools.partial(backward_kernel, dims), out_shape=jax.Sh...]
    pallas_call x1, Pallas kernels: 7.47 us -> 3.28 us  [body(): pl.pallas_call(functools.partial(forward_kernel, dims), out_shape=(jax.Sh...]
    pallas_call x1, Pallas kernels: 2.71 us -> 0.45 us  [body(): pl.pallas_call(functools.partial(owner_kernel, (groups, parts, members, b...]
    pallas_call x0 -> x1, Pallas kernels: none -> 1.61 us  [body(): pl.pallas_call(functools.partial(pack_kernel, (groups, parts, members, ch...]
    unnamed x7 -> x12, local copies, waits for them, and re-layouts: 1.59 us -> 0.02 us
  transfers between devices with their start and end apart: 1 -> 0, of which waited for: 1 -> 0; matrix products, arithmetic and copies ran while one was open for 1% -> 0% of each run, Pallas kernels for 0% -> 0%
where the time goes in v2:
time: 58.4 us; the launch traced here: 58.2 us
  blocking collectives  48 us (82%)
  Pallas kernels  9.07 us (16%)
  other arithmetic  1.08 us (2%)
    all_to_all x1, blocking collectives, body(): lax.all_to_all(payload, 'tm', split_axis=0, concat_axis=0, tiled=True)  15.6 us
    all_to_all x1, blocking collectives, body(): back = lax.all_to_all(change, 'tm', split_axis=0, concat_axis=0, tiled=True)  12.1 us
    all_to_all x1, blocking collectives, body(): lax.all_to_all(packed, ('tm', 'lat'), split_axis=0, concat_axis=0, tiled=...  11.3 us
    all_to_all x1, blocking collectives, body(): lax.all_to_all(answer, ('tm', 'lat'), split_axis=0, concat_axis=0, tiled=...  8.99 us
    pallas_call x1, Pallas kernels, body(): pl.pallas_call(functools.partial(backward_kernel, dims), out_shape=jax.Sh...  3.74 us
    pallas_call x1, Pallas kernels, body(): pl.pallas_call(functools.partial(forward_kernel, dims), out_shape=(jax.Sh...  3.28 us
    pallas_call x1, Pallas kernels, body(): pl.pallas_call(functools.partial(pack_kernel, (groups, parts, members, ch...  1.61 us

profile of v2, /device:TPU:0, one launch (start us, length us, event | category | flops | bytes accessed | tf_op | source)
XLA Modules:
  0.0 58.2 jit_solution(13374110908761678396)
XLA Ops:
  0.0 0.0 copy-start.2
  0.0 0.0 copy-start.3
  0.0 0.0 copy-start
  0.0 0.0 copy-start.4
  0.0 1.6 %pack.1 = (bf16[8,144,256]{2,1,0:T(8,128)(2,1)S(1)}, bf16[128,320]{1,0:T(8,128)(2,1)S(1)}, bf16[128,128]{1,0:T(8,128)(2,1)S(1)}, bf16[128,320]{1,0:T(8,128)(2,1)S(1)}) custom-call(f32[16,64,256]{2,1,0:T(8,128)} %bitcast.17, s32[4,2,128]{2,1,0:T(2,128)} %bitcast.19, s32[2,4]{1,0:T(2,128)} %bitcast.20, bf16[320,128]{1,0:T(8,128)(2,1)} %bitcast.14, ...), custom_call_target="tpu_custom_call" | custom-call | tf_op jit(solution)/shard_map/pack/pallas_call | solution.py:301
  1.6 0.0 copy-start.1
  1.6 15.6 %all_to_all.20.recv_ref.picks_ref = bf16[8,144,256]{2,1,0:T(8,128)(2,1)S(1)} all-to-all(bf16[8,144,256]{2,1,0:T(8,128)(2,1)S(1)} %get-tuple-element.14), channel_id=1, replica_groups=mesh['tm'=8,'lat'=4] {'tm'}, dimensions={0} | all-to-all | bytes 1179648 | tf_op jit(solution)/shard_map/all_to_all | solution.py:324
  17.2 0.0 copy-done.2
  17.2 0.0 copy-done.3
  17.2 3.3 %forward.1 = (bf16[32,8,128]{2,1,0:T(8,128)(2,1)S(1)}, f32[8,128,256]{2,1,0:T(8,128)S(1)}, f32[8,2,128,256]{3,2,1,0:T(8,128)S(1)}, f32[8,2,128,256]{3,2,1,0:T(8,128)S(1)}, bf16[8,256,1024]{2,1,0:T(8,128)(2,1)S(1)}) custom-call(s32[1]{0:T(128)} %constant.17.clone.1.offset_ref, bf16[8,144,256]{2,1,0:T(8,128)(2,1)S(1)} %all_to_all.20.recv_ref.picks_ref, ...), custom_call_target="tpu_custom_call" | custom-call | tf_op jit(solution)/shard_map/forward/pallas_call | solution.py:331
  20.5 11.3 %all_to_all.21.recv_ref = bf16[32,8,128]{2,1,0:T(8,128)(2,1)S(1)} all-to-all(bf16[32,8,128]{2,1,0:T(8,128)(2,1)S(1)} %get-tuple-element.16), channel_id=1, replica_groups=mesh['tm'=8,'lat'=4] {'tm','lat'}, dimensions={0} | all-to-all | bytes 131072 | tf_op jit(solution)/shard_map/all_to_all | solution.py:351
  31.8 0.0 copy-done
  31.8 0.0 copy-done.4
  31.8 0.4 owner.1
  32.2 9.0 %all_to_all.22.recv_ref = bf16[32,4,128]{2,1,0:T(4,128)(2,1)S(1)} all-to-all(bf16[32,4,128]{2,1,0:T(4,128)(2,1)S(1)} %owner.1), channel_id=1, replica_groups=mesh['tm'=8,'lat'=4] {'tm','lat'}, dimensions={0} | all-to-all | bytes 65536 | tf_op jit(solution)/shard_map/all_to_all | solution.py:365
  41.2 0.0 copy-done.1
  41.2 0.0 copy-start.5
  41.2 3.7 %backward.1 = bf16[8,128,256]{2,1,0:T(8,128)(2,1)S(1)} custom-call(bf16[32,4,128]{2,1,0:T(4,128)(2,1)S(1)} %all_to_all.22.recv_ref, bf16[8,144,256]{2,1,0:T(8,128)(2,1)S(1)} %all_to_all.20.recv_ref.picks_ref, bf16[8,256,1024]{2,1,0:T(8,128)(2,1)S(1)} %get-tuple-element.17.at_pixel_ref, bf16[320,128]{1,0:T(8,128)(2,1)S(1)} %bitcast.15, ...), custom_call_target="tpu_custom_call" | custom-call | tf_op jit(solution)/shard_map/backward/pallas_call | solution.py:366
  45.0 12.1 %all_to_all.23 = bf16[8,128,256]{2,1,0:T(8,128)(2,1)S(1)} all-to-all(bf16[8,128,256]{2,1,0:T(8,128)(2,1)S(1)} %backward.1), channel_id=1, replica_groups=mesh['tm'=8,'lat'=4] {'tm'}, dimensions={0} | all-to-all | bytes 1048576 | tf_op jit(solution)/shard_map/all_to_all | solution.py:380
  57.1 0.0 copy-done.5
  57.1 1.1 %convert_add_fusion = f32[16,1,64,256]{3,2,1,0:T(8,128)} fusion(f32[16,1,64,256]{3,2,1,0:T(8,128)S(1)} %copy-done.5, bf16[16,1,64,256]{3,2,1,0:T(8,128)(2,1)S(1)} %bitcast.18), kind=kLoop, calls=%fused_computation | loop fusion | flops 524288 | bytes 2621440 | tf_op jit(solution)/shard_map/add | solution.py:382
Async XLA Ops:
  0.0 17.2 %copy-start.2 = (bf16[320,128]{1,0:T(8,128)(2,1)S(1)}, bf16[320,128]{1,0:T(8,128)(2,1)}, u32[]{:S(2)}) copy-start(bf16[320,128]{1,0:T(8,128)(2,1)} %wout_ref.1) | copy-start | bytes 245764
  0.0 17.2 %copy-start.3 = (bf16[128,128]{1,0:T(8,128)(2,1)S(1)}, bf16[128,128]{1,0:T(8,128)(2,1)}, u32[]{:S(2)}) copy-start(bf16[128,128]{1,0:T(8,128)(2,1)} %wmid_ref.1) | copy-start | bytes 98308
  0.0 31.8 %copy-start = (bf16[1,1,1024,1024]{3,2,1,0:T(8,128)(2,1)S(1)}, bf16[1,1,1024,1024]{3,2,1,0:T(8,128)(2,1)}, u32[]{:S(2)}) copy-start(bf16[1,1,1024,1024]{3,2,1,0:T(8,128)(2,1)} %param.15) | copy-start | bytes 6291460
  0.0 31.8 %copy-start.4 = (f32[1,1,1024]{2,1,0:T(1,128)S(1)}, f32[1,1,1024]{2,1,0:T(1,128)}, u32[]{:S(2)}) copy-start(f32[1,1,1024]{2,1,0:T(1,128)} %param.14) | copy-start | bytes 12292
  1.6 39.6 %copy-start.1 = (bf16[128,320]{0,1:T(8,128)(2,1)S(1)}, bf16[128,320]{0,1:T(8,128)(2,1)}, u32[]{:S(2)}) copy-start(bf16[128,320]{0,1:T(8,128)(2,1)} %param.9) | copy-start | bytes 245764
  41.2 15.9 %copy-start.5 = (f32[16,1,64,256]{3,2,1,0:T(8,128)S(1)}, f32[16,1,64,256]{3,2,1,0:T(8,128)}, u32[]{:S(2)}) copy-start(f32[16,1,64,256]{3,2,1,0:T(8,128)} %param.8) | copy-start | bytes 3145732

commit v3 on v2

--- a/solution.py
+++ b/solution.py
@@ -21,15 +21,13 @@
     return -(-value // step) * step
 
 
-def silu(values):
-    half = 0.5 * values
+def silu_of_half(half):
     return half + half * jnp.tanh(half)
 
 
-def silu_slope(values):
-    half = 0.5 * values
+def twice_slope_of_half(half):
     bend = jnp.tanh(half)
-    return (0.5 + 0.5 * bend) * (1.0 + half * (1.0 - bend))
+    return (1.0 + bend) * (1.0 + half * (1.0 - bend))
 
 
 def loop(count, step):
@@ -42,7 +40,7 @@
 
 def pack_kernel(
     dims, state_hbm, pick_hbm, slot_hbm, win_turned_hbm, wmid_hbm, wout_hbm,
-    out, win_ref, wmid_turned_ref, wout_turned_ref,
+    out, win_ref, wmid_ref, wmid_turned_ref, wout_turned_ref,
     state, pick_vmem, slot_ref, win_turned, wmid, wout, state_sems, sems
 ):
     groups, parts, members, chan, width, owners, pairs, extra = dims
@@ -92,9 +90,11 @@
                 out[g * parts + part, 0:rows] = piece.reshape(rows, width)
     for copy in small[2:]:
         copy.wait()
-    win_ref[...] = win_turned[...].T
-    wmid_turned_ref[...] = wmid[...].T
-    wout_turned_ref[...] = wout[...].T
+    half = jnp.asarray(0.5, BF)
+    win_ref[...] = win_turned[...].T * half
+    wmid_ref[...] = wmid[...] * half
+    wmid_turned_ref[...] = wmid[...].T * half
+    wout_turned_ref[...] = wout[...].T * half
 
 
 def row_of(ref, time, base, block):
@@ -123,13 +123,13 @@
             window = padded[pl.ds(s, WIN), m].reshape(WIN * chan, width)
             pre_one = jnp.dot(win_ref[...], window, preferred_element_type=F32)
             pre_one_ref[s, m] = pre_one
-            hidden_one[s, m] = silu(pre_one).astype(BF)
+            hidden_one[s, m] = silu_of_half(pre_one).astype(BF)
 
     def second(s):
         for m in range(members):
             pre_two = jnp.dot(wmid_ref[...], hidden_one[s, m], preferred_element_type=F32)
             pre_two_ref[s, m] = pre_two
-            hidden_two[s, m] = silu(pre_two).astype(BF)
+            hidden_two[s, m] = silu_of_half(pre_two).astype(BF)
 
     def third(s):
         for m in range(members):
@@ -143,14 +143,15 @@
         field = sums[t + radius]
         total_ref[t] = field.reshape(rows, width)
         state = (padded[t + radius].astype(F32) + field).astype(BF).reshape(rows, width)
-        index = (lax.broadcasted_iota(jnp.int32, (width, LANES), 0) + offset).astype(F32)
+        index = (lax.broadcasted_iota(jnp.int32, (width, LANES), 0) + offset).astype(BF)
         for o in range(owners):
             lines = []
             for r in range(pairs):
                 place = row_of(recv_ref, t, rows + rows_each, o * pairs + r)
-                lines.append(jnp.where(index == place, 1.0, 0.0).astype(BF))
+                here = index == place.astype(BF)
+                lines.append(jnp.where(here, jnp.ones_like(index), jnp.zeros_like(index)))
             at_pixel = jnp.concatenate(lines, axis=1)
-            at_pixel_ref[t, :, o * pairs * LANES : (o + 1) * pairs * LANES] = at_pixel
+            at_pixel_ref[t, o * pairs * LANES : (o + 1) * pairs * LANES] = at_pixel.T
             found = jnp.dot(state, at_pixel, preferred_element_type=F32)
             pieces = []
             for r in range(pairs):
@@ -235,20 +236,19 @@
 
     def scatter(t):
         spread = []
-        index = lax.broadcasted_iota(jnp.int32, (chan, LANES), 0).astype(F32)
+        index = lax.broadcasted_iota(jnp.int32, (chan, LANES), 0).astype(BF)
         for o in range(owners):
-            tile = recv_ref[t * owners + o].astype(F32)
-            for r in range(pairs):
-                at_chan = index == row_of(picks_ref, t, rows, o * pairs + r)
+            tile = recv_ref[t * owners + o]
+            for r in range(pairs):
+                at_chan = index == row_of(picks_ref, t, rows, o * pairs + r).astype(BF)
                 pieces = []
                 for m in range(members):
                     row = r * members + m
-                    pieces.append(jnp.where(at_chan, tile[row : row + 1], 0.0).astype(BF))
+                    value = jnp.broadcast_to(tile[row : row + 1], (chan, LANES))
+                    pieces.append(jnp.where(at_chan, value, jnp.zeros_like(value)))
                 spread.append(jnp.concatenate(pieces, axis=0))
         spread = jnp.concatenate(spread, axis=1)
-        guidance = lax.dot_general(
-            spread, at_pixel_ref[t], (((1,), (1,)), ((), ())), preferred_element_type=F32
-        )
+        guidance = jnp.dot(spread, at_pixel_ref[t], preferred_element_type=F32)
         padded[t + radius] = guidance.astype(BF).reshape(members, chan, width)
         sums[t + radius] = (guidance + total_ref[t]).reshape(members, chan, width)
 
@@ -256,12 +256,12 @@
         for m in range(members):
             window = padded[pl.ds(s, WIN), m].reshape(WIN * chan, width)
             grad = jnp.dot(wout_ref[...], window, preferred_element_type=F32)
-            grad_two[s, m] = (grad * silu_slope(pre_two_ref[s, m])).astype(BF)
+            grad_two[s, m] = (grad * twice_slope_of_half(pre_two_ref[s, m])).astype(BF)
 
     def second(s):
         for m in range(members):
             grad = jnp.dot(wmid_ref[...], grad_two[s, m], preferred_element_type=F32)
-            grad_one[s, m] = (grad * silu_slope(pre_one_ref[s, m])).astype(BF)
+            grad_one[s, m] = (grad * twice_slope_of_half(pre_one_ref[s, m])).astype(BF)
 
     def third(s):
         for m in range(members):
@@ -298,16 +298,17 @@
     vmem = pl.BlockSpec(memory_space=pltpu.VMEM)
     hbm = pl.BlockSpec(memory_space=pltpu.HBM)
     chunks = 4 if groups % 4 == 0 else 1
-    payload, win, wmid_turned, wout_turned = pl.pallas_call(
+    payload, win, wmid, wmid_turned, wout_turned = pl.pallas_call(
         functools.partial(pack_kernel, (groups, parts, members, chan, width, owners, pairs, extra)),
         out_shape=(
             jax.ShapeDtypeStruct((times, rows + extra, width), BF),
             jax.ShapeDtypeStruct(w_in.shape, BF),
+            jax.ShapeDtypeStruct(w_mid.shape, BF),
             jax.ShapeDtypeStruct(w_mid.shape[::-1], BF),
             jax.ShapeDtypeStruct(w_out.shape[::-1], BF),
         ),
         in_specs=[hbm] * 6,
-        out_specs=(vmem,) * 4,
+        out_specs=(vmem,) * 5,
         scratch_shapes=[
             pltpu.VMEM(current.shape, F32),
             pltpu.VMEM((owners, pairs, block_rows), jnp.int32),
@@ -335,7 +336,7 @@
             jax.ShapeDtypeStruct((times, rows, width), F32),
             jax.ShapeDtypeStruct(inner, F32),
             jax.ShapeDtypeStruct(inner, F32),
-            jax.ShapeDtypeStruct((times, width, owners * pairs * block_rows), BF),
+            jax.ShapeDtypeStruct((times, owners * pairs * block_rows, width), BF),
         ),
         in_specs=[smem, vmem, vmem, vmem, vmem],
         out_specs=(vmem,) * 5,
@@ -347,7 +348,7 @@
         ],
         compiler_params=limit(24),
         name="forward",
-    )(offset, received, win, w_mid, w_out)
+    )(offset, received, win, wmid, w_out)
     arrived = lax.all_to_all(packed, ("tm", "lat"), split_axis=0, concat_axis=0, tiled=True)
     rows_three = ceil_to(members * pairs, 2)
     answer = pl.pallas_call(

time: 58.4 us -> 56.3 us (0.964)
  Pallas kernels: 9.07 us -> 6.91 us
    pallas_call x1, Pallas kernels: 3.74 us -> 2.45 us  [body(): pl.pallas_call(functools.partial(backward_kernel, dims), out_shape=jax.Sh...]
    pallas_call x1, Pallas kernels: 3.28 us -> 2.4 us  [body(): pl.pallas_call(functools.partial(forward_kernel, dims), out_shape=(jax.Sh...]
where the time goes in v3:
time: 56.3 us; the launch traced here: 56 us
  blocking collectives  47.9 us (85%)
  Pallas kernels  6.91 us (12%)
  other arithmetic  1.08 us (2%)
    all_to_all x1, blocking collectives, body(): lax.all_to_all(payload, 'tm', split_axis=0, concat_axis=0, tiled=True)  15.5 us
    all_to_all x1, blocking collectives, body(): back = lax.all_to_all(change, 'tm', split_axis=0, concat_axis=0, tiled=True)  12.1 us
    all_to_all x1, blocking collectives, body(): lax.all_to_all(packed, ('tm', 'lat'), split_axis=0, concat_axis=0, tiled=...  11.3 us
    all_to_all x1, blocking collectives, body(): lax.all_to_all(answer, ('tm', 'lat'), split_axis=0, concat_axis=0, tiled=...  8.99 us
    pallas_call x1, Pallas kernels, body(): pl.pallas_call(functools.partial(backward_kernel, dims), out_shape=jax.Sh...  2.45 us
    pallas_call x1, Pallas kernels, body(): pl.pallas_call(functools.partial(forward_kernel, dims), out_shape=(jax.Sh...  2.4 us
    pallas_call x1, Pallas kernels, body(): pl.pallas_call(functools.partial(pack_kernel, (groups, parts, members, ch...  1.61 us

profile of v3, /device:TPU:0, one launch (start us, length us, event | category | flops | bytes accessed | tf_op | source)
XLA Modules:
  0.0 56.0 jit_solution(2810627308472337217)
XLA Ops:
  0.0 0.0 copy-start.2
  0.0 0.0 copy-start
  0.0 0.0 copy-start.3
  0.0 1.6 %pack.1 = (bf16[8,144,256]{2,1,0:T(8,128)(2,1)S(1)}, bf16[128,320]{1,0:T(8,128)(2,1)S(1)}, bf16[128,128]{1,0:T(8,128)(2,1)S(1)}, bf16[128,128]{1,0:T(8,128)(2,1)S(1)}, bf16[128,320]{1,0:T(8,128)(2,1)S(1)}) custom-call(f32[16,64,256]{2,1,0:T(8,128)} %bitcast.17, s32[4,2,128]{2,1,0:T(2,128)} %bitcast.19, s32[2,4]{1,0:T(2,128)} %bitcast.20, ...), custom_call_target="tpu_custom_call" | custom-call | tf_op jit(solution)/shard_map/pack/pallas_call | solution.py:301
  1.6 0.0 copy-start.1
  1.6 15.5 %all_to_all.20.recv_ref.picks_ref = bf16[8,144,256]{2,1,0:T(8,128)(2,1)S(1)} all-to-all(bf16[8,144,256]{2,1,0:T(8,128)(2,1)S(1)} %get-tuple-element.15), channel_id=1, replica_groups=mesh['tm'=8,'lat'=4] {'tm'}, dimensions={0} | all-to-all | bytes 1179648 | tf_op jit(solution)/shard_map/all_to_all | solution.py:325
  17.2 0.0 copy-done.2
  17.2 2.4 %forward.1 = (bf16[32,8,128]{2,1,0:T(8,128)(2,1)S(1)}, f32[8,128,256]{2,1,0:T(8,128)S(1)}, f32[8,2,128,256]{3,2,1,0:T(8,128)S(1)}, f32[8,2,128,256]{3,2,1,0:T(8,128)S(1)}, bf16[8,1024,256]{2,1,0:T(8,128)(2,1)S(1)}) custom-call(s32[1]{0:T(128)} %constant.17.clone.1.offset_ref, bf16[8,144,256]{2,1,0:T(8,128)(2,1)S(1)} %all_to_all.20.recv_ref.picks_ref, ...), custom_call_target="tpu_custom_call" | custom-call | tf_op jit(solution)/shard_map/forward/pallas_call | solution.py:332
  19.6 11.3 %all_to_all.21.recv_ref = bf16[32,8,128]{2,1,0:T(8,128)(2,1)S(1)} all-to-all(bf16[32,8,128]{2,1,0:T(8,128)(2,1)S(1)} %get-tuple-element.18), channel_id=1, replica_groups=mesh['tm'=8,'lat'=4] {'tm','lat'}, dimensions={0} | all-to-all | bytes 131072 | tf_op jit(solution)/shard_map/all_to_all | solution.py:352
  30.9 0.0 copy-done
  30.9 0.0 copy-done.3
  30.9 0.4 owner.1
  31.3 9.0 %all_to_all.22.recv_ref = bf16[32,4,128]{2,1,0:T(4,128)(2,1)S(1)} all-to-all(bf16[32,4,128]{2,1,0:T(4,128)(2,1)S(1)} %owner.1), channel_id=1, replica_groups=mesh['tm'=8,'lat'=4] {'tm','lat'}, dimensions={0} | all-to-all | bytes 65536 | tf_op jit(solution)/shard_map/all_to_all | solution.py:366
  40.3 0.0 copy-done.1
  40.3 0.0 copy-start.4
  40.3 2.4 %backward.1 = bf16[8,128,256]{2,1,0:T(8,128)(2,1)S(1)} custom-call(bf16[32,4,128]{2,1,0:T(4,128)(2,1)S(1)} %all_to_all.22.recv_ref, bf16[8,144,256]{2,1,0:T(8,128)(2,1)S(1)} %all_to_all.20.recv_ref.picks_ref, bf16[8,1024,256]{2,1,0:T(8,128)(2,1)S(1)} %get-tuple-element.19.at_pixel_ref, bf16[320,128]{1,0:T(8,128)(2,1)S(1)} %bitcast.15, ...), custom_call_target="tpu_custom_call" | custom-call | tf_op jit(solution)/shard_map/backward/pallas_call | solution.py:367
  42.8 12.1 %all_to_all.23 = bf16[8,128,256]{2,1,0:T(8,128)(2,1)S(1)} all-to-all(bf16[8,128,256]{2,1,0:T(8,128)(2,1)S(1)} %backward.1), channel_id=1, replica_groups=mesh['tm'=8,'lat'=4] {'tm'}, dimensions={0} | all-to-all | bytes 1048576 | tf_op jit(solution)/shard_map/all_to_all | solution.py:381
  54.9 0.0 copy-done.4
  54.9 1.1 %convert_add_fusion = f32[16,1,64,256]{3,2,1,0:T(8,128)} fusion(f32[16,1,64,256]{3,2,1,0:T(8,128)S(1)} %copy-done.4, bf16[16,1,64,256]{3,2,1,0:T(8,128)(2,1)S(1)} %bitcast.18), kind=kLoop, calls=%fused_computation | loop fusion | flops 524288 | bytes 2621440 | tf_op jit(solution)/shard_map/add | solution.py:383
Async XLA Ops:
  0.0 17.2 %copy-start.2 = (bf16[320,128]{1,0:T(8,128)(2,1)S(1)}, bf16[320,128]{1,0:T(8,128)(2,1)}, u32[]{:S(2)}) copy-start(bf16[320,128]{1,0:T(8,128)(2,1)} %wout_ref.1) | copy-start | bytes 245764
  0.0 30.9 %copy-start = (bf16[1,1,1024,1024]{3,2,1,0:T(8,128)(2,1)S(1)}, bf16[1,1,1024,1024]{3,2,1,0:T(8,128)(2,1)}, u32[]{:S(2)}) copy-start(bf16[1,1,1024,1024]{3,2,1,0:T(8,128)(2,1)} %param.15) | copy-start | bytes 6291460
  0.0 30.9 %copy-start.3 = (f32[1,1,1024]{2,1,0:T(1,128)S(1)}, f32[1,1,1024]{2,1,0:T(1,128)}, u32[]{:S(2)}) copy-start(f32[1,1,1024]{2,1,0:T(1,128)} %param.14) | copy-start | bytes 12292
  1.6 38.7 %copy-start.1 = (bf16[128,320]{0,1:T(8,128)(2,1)S(1)}, bf16[128,320]{0,1:T(8,128)(2,1)}, u32[]{:S(2)}) copy-start(bf16[128,320]{0,1:T(8,128)(2,1)} %param.9) | copy-start | bytes 245764
  40.3 14.6 %copy-start.4 = (f32[16,1,64,256]{3,2,1,0:T(8,128)S(1)}, f32[16,1,64,256]{3,2,1,0:T(8,128)}, u32[]{:S(2)}) copy-start(f32[16,1,64,256]{3,2,1,0:T(8,128)} %param.8) | copy-start | bytes 3145732

commit v4 on v3

--- a/solution.py
+++ b/solution.py
@@ -38,31 +38,60 @@
         lax.fori_loop(0, count, lambda index, carry: (step(index), carry)[1], 0)
 
 
-def pack_kernel(
-    dims, state_hbm, pick_hbm, slot_hbm, win_turned_hbm, wmid_hbm, wout_hbm,
-    out, win_ref, wmid_ref, wmid_turned_ref, wout_turned_ref,
-    state, pick_vmem, slot_ref, win_turned, wmid, wout, state_sems, sems
-):
+def exchange(pieces):
+    size = lax.axis_size("tm")
+    if len(pieces) == 1:
+        return [lax.all_to_all(pieces[0], "tm", split_axis=0, concat_axis=0, tiled=True)]
+
+    def swap(values, distance):
+        return lax.ppermute(values, "tm", [(k, k ^ distance) for k in range(size)])
+
+    arrived = [pieces[0]] + [swap(piece, 2 * s) for s, piece in enumerate(pieces) if s]
+    return arrived + [swap(piece, 1) for piece in arrived]
+
+
+def departures(refs, times):
+    if len(refs) == 1:
+        return [(t, refs[0], t) for t in range(times)]
+    me = lax.axis_index("tm")
+    return [(((me // 2) ^ s) * 2 + ((me % 2) ^ k), ref, k) for s, ref in enumerate(refs) for k in range(2)]
+
+
+def arrivals(refs, times):
+    if len(refs) == 1:
+        return [(t, refs[0], t) for t in range(times)]
+    me = lax.axis_index("tm")
+    chips = len(refs) // 2
+    return [(((me // 2) ^ s) * 2 + ((me % 2) ^ k), refs[k * chips + s], k) for s in range(chips) for k in range(2)]
+
+
+def pack_kernel(dims, sends, state_hbm, pick_hbm, slot_hbm, win_turned_hbm, wmid_hbm, wout_hbm, observed_hbm, *refs):
     groups, parts, members, chan, width, owners, pairs, extra = dims
+    outs = refs[:sends]
+    win_ref, wmid_ref, wmid_turned_ref, wout_turned_ref, win_turned, wout, observed = refs[sends : sends + 7]
+    state, pick_vmem, slot_ref, wmid, state_sems, sems = refs[sends + 7 :]
+    times = groups * parts
     rows = members * chan
     per_row = width // LANES
     rows_each = owners * pairs // per_row
-    chunks = state_sems.shape[0]
-    step = groups // chunks
+    targets = departures(outs, times)
     small = []
-    pairs_of = ((pick_hbm, pick_vmem), (slot_hbm, slot_ref), (win_turned_hbm, win_turned), (wmid_hbm, wmid), (wout_hbm, wout))
-    for index, (source, target) in enumerate(pairs_of[:2]):
+    pairs_of = (
+        (pick_hbm, pick_vmem), (slot_hbm, slot_ref), (win_turned_hbm, win_turned), (wmid_hbm, wmid), (wout_hbm, wout),
+        (observed_hbm, observed),
+    )
+    for index, (source, target) in enumerate(pairs_of):
         small.append(pltpu.make_async_copy(source, target, sems.at[index]))
-        small[-1].start()
+    small[0].start()
+    small[1].start()
     copies = []
-    for c in range(chunks):
-        span = pl.ds(c * step * members, step * members)
-        copies.append(pltpu.make_async_copy(state_hbm.at[span], state.at[span], state_sems.at[c]))
-        copies[-1].start()
-    for index, (source, target) in enumerate(pairs_of):
-        if index >= 2:
-            small.append(pltpu.make_async_copy(source, target, sems.at[index]))
-            small[-1].start()
+    for index, (t, _, _) in enumerate(targets):
+        if index % parts == 0:
+            span = pl.ds((t // parts) * members, members)
+            copies.append(pltpu.make_async_copy(state_hbm.at[span], state.at[index // parts], state_sems.at[index // parts]))
+            copies[-1].start()
+    for copy in small[2:]:
+        copy.start()
     small[0].wait()
     small[1].wait()
     pick = pick_vmem[...].astype(F32)
@@ -79,15 +108,14 @@
     if extra > len(lines):
         lines.append(jnp.zeros((extra - len(lines), width), F32))
     lines = jnp.concatenate(lines, axis=0).astype(BF)
-    for d in range(groups * parts):
-        out[d, rows:] = lines
-    for c in range(chunks):
-        copies[c].wait()
-        for g in range(c * step, (c + 1) * step):
-            block = state[g * members : (g + 1) * members].astype(BF)
-            for part in range(parts):
-                piece = block[:, :, part * width : (part + 1) * width]
-                out[g * parts + part, 0:rows] = piece.reshape(rows, width)
+    for _, out, row in targets:
+        out[row, rows:] = lines
+    for index, (t, out, row) in enumerate(targets):
+        if index % parts == 0:
+            copies[index // parts].wait()
+            block = state[index // parts].astype(BF)
+        part = index % parts
+        out[row, 0:rows] = block[:, :, part * width : (part + 1) * width].reshape(rows, width)
     for copy in small[2:]:
         copy.wait()
     half = jnp.asarray(0.5, BF)
@@ -104,10 +132,9 @@
     return ref[time, row : row + 1, start : start + LANES].astype(F32)
 
 
-def forward_kernel(
-    dims, offset_ref, recv_ref, win_ref, wmid_ref, wout_ref,
-    send_ref, total_ref, pre_one_ref, pre_two_ref, at_pixel_ref, padded, sums, hidden_one, hidden_two
-):
+def forward_kernel(dims, offset_ref, win_ref, wmid_ref, wout_ref, *refs):
+    send_ref, total_ref, pre_one_ref, pre_two_ref, at_pixel_ref, lines_ref = refs[-10:-4]
+    padded, sums, hidden_one, hidden_two = refs[-4:]
     times, members, chan, width, owners, pairs, extra = dims
     radius = WIN // 2
     rows = members * chan
@@ -115,7 +142,9 @@
     zero_state = jnp.zeros((radius, members, chan, width), BF)
     padded[0:radius] = zero_state
     padded[radius + times :] = zero_state
-    padded[radius : radius + times] = recv_ref[:, 0:rows, :].reshape(times, members, chan, width)
+    for t, ref, row in arrivals(refs[:-10], times):
+        padded[t + radius] = ref[row, 0:rows].reshape(members, chan, width)
+        lines_ref[t] = ref[row, rows:]
     sums[...] = jnp.zeros_like(sums)
 
     def first(s):
@@ -147,7 +176,7 @@
         for o in range(owners):
             lines = []
             for r in range(pairs):
-                place = row_of(recv_ref, t, rows + rows_each, o * pairs + r)
+                place = row_of(lines_ref, t, rows_each, o * pairs + r)
                 here = index == place.astype(BF)
                 lines.append(jnp.where(here, jnp.ones_like(index), jnp.zeros_like(index)))
             at_pixel = jnp.concatenate(lines, axis=1)
@@ -155,7 +184,7 @@
             found = jnp.dot(state, at_pixel, preferred_element_type=F32)
             pieces = []
             for r in range(pairs):
-                channel = row_of(recv_ref, t, rows, o * pairs + r)
+                channel = row_of(lines_ref, t, 0, o * pairs + r)
                 high = jnp.floor(channel * (1.0 / eight))
                 at_row = lax.broadcasted_iota(jnp.int32, (eight, LANES), 0).astype(F32) == channel - high * eight
                 high = jnp.broadcast_to(high, (eight, LANES))
@@ -169,7 +198,7 @@
                 for m in range(members):
                     pieces.append(jnp.sum(jnp.where(at_row, picked[m], 0.0), axis=0, keepdims=True))
             for r in range(pairs):
-                pieces.append(row_of(recv_ref, t, rows + 2 * rows_each, o * pairs + r))
+                pieces.append(row_of(lines_ref, t, 2 * rows_each, o * pairs + r))
             spare = send_ref.shape[1] - len(pieces)
             if spare:
                 pieces.append(jnp.zeros((spare, LANES), F32))
@@ -222,9 +251,9 @@
 
 
 def backward_kernel(
-    dims, recv_ref, picks_ref, at_pixel_ref, win_ref, wmid_ref, wout_ref, total_ref, pre_one_ref, pre_two_ref,
-    out_ref, padded, sums, grad_one, grad_two
+    dims, recv_ref, lines_ref, at_pixel_ref, win_ref, wmid_ref, wout_ref, total_ref, pre_one_ref, pre_two_ref, *refs
 ):
+    padded, sums, grad_one, grad_two = refs[-4:]
     times, members, chan, width, owners, pairs, extra = dims
     radius = WIN // 2
     rows = members * chan
@@ -240,7 +269,7 @@
         for o in range(owners):
             tile = recv_ref[t * owners + o]
             for r in range(pairs):
-                at_chan = index == row_of(picks_ref, t, rows, o * pairs + r).astype(BF)
+                at_chan = index == row_of(lines_ref, t, 0, o * pairs + r).astype(BF)
                 pieces = []
                 for m in range(members):
                     row = r * members + m
@@ -273,10 +302,25 @@
     loop(times, second)
     loop(times, third)
 
-    def finish(t):
-        out_ref[t] = sums[t + radius].reshape(rows, width).astype(BF)
-
-    loop(times, finish)
+    for t, ref, row in departures(refs[:-4], times):
+        ref[row] = sums[t + radius].reshape(rows, width).astype(BF)
+
+
+def update_kernel(dims, state_ref, *refs):
+    times, parts, members, chan, width = dims
+    out_hbm, out, sems = refs[-3:]
+    copies = []
+    for index, (t, ref, row) in enumerate(arrivals(refs[:-3], times)):
+        span = pl.ds((t // parts) * members, members)
+        part = index % parts
+        change = ref[row].reshape(members, chan, width).astype(F32)
+        columns = slice(part * width, (part + 1) * width)
+        out[span, :, columns] = state_ref[span, :, columns] + change
+        if part == parts - 1:
+            copies.append(pltpu.make_async_copy(out.at[span], out_hbm.at[span], sems.at[index // parts]))
+            copies[-1].start()
+    for copy in copies:
+        copy.wait()
 
 
 def body(noisy_state, w_in, w_mid, w_out, obs_pick, obs_slot, observed, precision):
@@ -297,39 +341,42 @@
     smem = pl.BlockSpec(memory_space=pltpu.SMEM)
     vmem = pl.BlockSpec(memory_space=pltpu.VMEM)
     hbm = pl.BlockSpec(memory_space=pltpu.HBM)
-    chunks = 4 if groups % 4 == 0 else 1
-    payload, win, wmid, wmid_turned, wout_turned = pl.pallas_call(
-        functools.partial(pack_kernel, (groups, parts, members, chan, width, owners, pairs, extra)),
+    sends = times // 2 if parts == 1 and times in (4, 8) else 1
+    each = times // sends
+    sources = (current, obs_pick[0, 0], obs_slot[0, 0].T, w_in.T, w_mid, w_out, observed.reshape(positions, block_rows))
+    *payload, win, wmid, wmid_turned, wout_turned, win_turned, wout, seen = pl.pallas_call(
+        functools.partial(pack_kernel, (groups, parts, members, chan, width, owners, pairs, extra), sends),
         out_shape=(
-            jax.ShapeDtypeStruct((times, rows + extra, width), BF),
+            *(jax.ShapeDtypeStruct((each, rows + extra, width), BF) for _ in range(sends)),
             jax.ShapeDtypeStruct(w_in.shape, BF),
             jax.ShapeDtypeStruct(w_mid.shape, BF),
             jax.ShapeDtypeStruct(w_mid.shape[::-1], BF),
             jax.ShapeDtypeStruct(w_out.shape[::-1], BF),
+            jax.ShapeDtypeStruct(w_in.shape[::-1], BF),
+            jax.ShapeDtypeStruct(w_out.shape, BF),
+            jax.ShapeDtypeStruct((positions, block_rows), F32),
         ),
-        in_specs=[hbm] * 6,
-        out_specs=(vmem,) * 5,
+        in_specs=[hbm] * 7,
+        out_specs=(vmem,) * (sends + 7),
         scratch_shapes=[
-            pltpu.VMEM(current.shape, F32),
+            pltpu.VMEM((groups, members, chan, pixels), F32),
             pltpu.VMEM((owners, pairs, block_rows), jnp.int32),
             pltpu.SMEM((pairs, owners), jnp.int32),
-            pltpu.VMEM(w_in.shape[::-1], BF),
             pltpu.VMEM(w_mid.shape, BF),
-            pltpu.VMEM(w_out.shape, BF),
-            pltpu.SemaphoreType.DMA((chunks,)),
-            pltpu.SemaphoreType.DMA((5,)),
+            pltpu.SemaphoreType.DMA((groups,)),
+            pltpu.SemaphoreType.DMA((6,)),
         ],
         compiler_params=limit(16),
         name="pack",
-    )(*(pltpu.with_memory_space_constraint(x, pltpu.HBM) for x in (current, obs_pick[0, 0], obs_slot[0, 0].T, w_in.T, w_mid, w_out)))
-    received = lax.all_to_all(payload, "tm", split_axis=0, concat_axis=0, tiled=True)
+    )(*(pltpu.with_memory_space_constraint(x, pltpu.HBM) for x in sources))
+    received = exchange(payload)
 
     offset = ((lax.axis_index("tm") % parts) * width).astype(jnp.int32).reshape(1)
     dims = (times, members, chan, width, owners, pairs, extra)
     rows_two = ceil_to(members * pairs + pairs, 8)
     inner = (times, members, hidden, width)
     padded_shape = (times + 2 * radius, members, chan, width)
-    packed, total, pre_one, pre_two, at_pixel = pl.pallas_call(
+    packed, total, pre_one, pre_two, at_pixel, lines = pl.pallas_call(
         functools.partial(forward_kernel, dims),
         out_shape=(
             jax.ShapeDtypeStruct((times * owners, rows_two, LANES), BF),
@@ -337,9 +384,10 @@
             jax.ShapeDtypeStruct(inner, F32),
             jax.ShapeDtypeStruct(inner, F32),
             jax.ShapeDtypeStruct((times, owners * pairs * block_rows, width), BF),
+            jax.ShapeDtypeStruct((times, extra, width), BF),
         ),
-        in_specs=[smem, vmem, vmem, vmem, vmem],
-        out_specs=(vmem,) * 5,
+        in_specs=[smem] + [vmem] * (3 + len(received)),
+        out_specs=(vmem,) * 6,
         scratch_shapes=[
             pltpu.VMEM(padded_shape, BF),
             pltpu.VMEM(padded_shape, F32),
@@ -348,7 +396,7 @@
         ],
         compiler_params=limit(24),
         name="forward",
-    )(offset, received, win, wmid, w_out)
+    )(offset, win, wmid, wout, *received)
     arrived = lax.all_to_all(packed, ("tm", "lat"), split_axis=0, concat_axis=0, tiled=True)
     rows_three = ceil_to(members * pairs, 2)
     answer = pl.pallas_call(
@@ -362,13 +410,13 @@
         ],
         compiler_params=limit(16),
         name="owner",
-    )(arrived, observed.reshape(positions, block_rows), precision[0, 0])
+    )(arrived, seen, precision[0, 0])
     returned = lax.all_to_all(answer, ("tm", "lat"), split_axis=0, concat_axis=0, tiled=True)
     change = pl.pallas_call(
         functools.partial(backward_kernel, dims),
-        out_shape=jax.ShapeDtypeStruct((times, rows, width), BF),
+        out_shape=tuple(jax.ShapeDtypeStruct((each, rows, width), BF) for _ in range(sends)),
         in_specs=[vmem] * 9,
-        out_specs=vmem,
+        out_specs=(vmem,) * sends,
         scratch_shapes=[
             pltpu.VMEM(padded_shape, BF),
             pltpu.VMEM(padded_shape, F32),
@@ -377,10 +425,17 @@
         ],
         compiler_params=limit(24),
         name="backward",
-    )(returned, received, at_pixel, w_in.T, wmid_turned, wout_turned, total, pre_one, pre_two)
-    back = lax.all_to_all(change, "tm", split_axis=0, concat_axis=0, tiled=True)
-    back = back.reshape(groups, parts, members, chan, width).transpose(0, 2, 3, 1, 4)
-    updated = current + back.reshape(all_members, chan, pixels).astype(F32)
+    )(returned, lines, at_pixel, win_turned, wmid_turned, wout_turned, total, pre_one, pre_two)
+    back = exchange(change)
+    updated = pl.pallas_call(
+        functools.partial(update_kernel, (times, parts, members, chan, width)),
+        out_shape=jax.ShapeDtypeStruct(current.shape, F32),
+        in_specs=[vmem] * (1 + len(back)),
+        out_specs=hbm,
+        scratch_shapes=[pltpu.VMEM(current.shape, F32), pltpu.SemaphoreType.DMA((groups,))],
+        compiler_params=limit(16),
+        name="update",
+    )(current, *back)
     return updated[:, None]
 
 

time: 56.3 us -> 53 us (0.941)
  blocking collectives: 47.9 us -> 21.2 us
  waiting for transfers between devices: 0 us -> 14 us
  starting transfers between devices: 0 us -> 9.16 us
  Pallas kernels: 6.91 us -> 8.32 us
  other arithmetic: 1.08 us -> 0 us
    all_to_all x2 -> x0, blocking collectives: 27.7 us -> none  [the longest x1 15.5 us: body(): lax.all_to_all(payload, 'tm', split_axis=0, concat_axis=0, tiled=True)]
    ppermute x0 -> x14, waiting for transfers between devices: none -> 14 us  [swap(): return lax.ppermute(values, 'tm', [(k, k ^ distance) for k in range(size)])]
    ppermute x0 -> x14, starting transfers between devices: none -> 9.16 us  [swap(): return lax.ppermute(values, 'tm', [(k, k ^ distance) for k in range(size)])]
    pallas_call x1 -> x2, Pallas kernels: 2.45 us -> 3.64 us  [the longest x1 2.59 us: body(): pl.pallas_call(functools.partial(backward_kernel, dims), out_shape=tuple(...]
    add x1 -> x0, other arithmetic: 1.08 us -> none  [body(): updated = current + back.reshape(all_members, chan, pixels).astype(F32)]
    all_to_all x1, blocking collectives: 11.3 us -> 12.2 us  [body(): lax.all_to_all(packed, ('tm', 'lat'), split_axis=0, concat_axis=0, tiled=...]
  transfers between devices with their start and end apart: 0 -> 14, of which waited for: 0 -> 8; matrix products, arithmetic and copies ran while one was open for 0% -> 0% of each run, Pallas kernels for 0% -> 0%
where the time goes in v4:
time: 53 us; the launch traced here: 52.8 us
  blocking collectives  21.2 us (40%)
  waiting for transfers between devices  14 us (26%)
  starting transfers between devices  9.16 us (17%)
  Pallas kernels  8.32 us (16%)
    ppermute x14, waiting for transfers between devices, swap(): return lax.ppermute(values, 'tm', [(k, k ^ distance) for k in range(size)])  14 us
    all_to_all x1, blocking collectives, body(): lax.all_to_all(packed, ('tm', 'lat'), split_axis=0, concat_axis=0, tiled=...  12.2 us
    ppermute x14, starting transfers between devices, swap(): return lax.ppermute(values, 'tm', [(k, k ^ distance) for k in range(size)])  9.16 us
    all_to_all x1, blocking collectives, body(): lax.all_to_all(answer, ('tm', 'lat'), split_axis=0, concat_axis=0, tiled=...  8.99 us
    pallas_call x1, Pallas kernels, body(): pl.pallas_call(functools.partial(backward_kernel, dims), out_shape=tuple(...  2.59 us
    pallas_call x1, Pallas kernels, body(): pl.pallas_call(functools.partial(forward_kernel, dims), out_shape=(jax.Sh...  2.46 us
    pallas_call x1, Pallas kernels, body(): pl.pallas_call(functools.partial(pack_kernel, (groups, parts, members, ch...  1.76 us
  transfers between devices with their start and end apart: 14, of which 8 were waited for; matrix products, arithmetic and copies ran while one was open for 0% of the time, Pallas kernels for 0%

profile of v4, /device:TPU:0, one launch (start us, length us, event | category | flops | bytes accessed | tf_op | source)
XLA Modules:
  0.0 52.8 jit_solution(11437427825961733478)
XLA Ops:
  0.0 0.0 copy-start.1
  0.0 1.8 %pack.1 = (bf16[2,144,256]{2,1,0:T(8,128)(2,1)S(1)}, bf16[2,144,256]{2,1,0:T(8,128)(2,1)S(1)}, bf16[2,144,256]{2,1,0:T(8,128)(2,1)S(1)}, bf16[2,144,256]{2,1,0:T...) custom-call(f32[16,64,256]{2,1,0:T(8,128)} %bitcast.11, ...), custom_call_target="tpu_custom_call" | custom-call | tf_op jit(solution)/shard_map/pack/pallas_call | solution.py:347
  1.8 3.0 %collective-permute-start = (bf16[2,144,256]{2,1,0:T(8,128)(2,1)S(1)}, bf16[2,144,256]{2,1,0:T(8,128)(2,1)S(1)}, u32[]{:S(2)}, u32[]{:S(2)}) collective-permute-start(bf16[2,144,256]{2,1,0:T(8,128)(2,1)S(1)} %get-tuple-element.30), channel_id=1, source_target_pairs={{0,8},{4,12},{8,0},{12,4},{16,24},{20,28},{24,16},{28,20},{1,9},{5... | collective-permute-start | bytes 442376 | tf_op jit(solution)/shard_map/ppermute | solution.py:47
  4.8 1.5 %collective-permute-start.1 = (bf16[2,144,256]{2,1,0:T(8,128)(2,1)S(1)}, bf16[2,144,256]{2,1,0:T(8,128)(2,1)S(1)}, u32[]{:S(2)}, u32[]{:S(2)}) collective-permute-start(bf16[2,144,256]{2,1,0:T(8,128)(2,1)S(1)} %get-tuple-element.31), channel_id=1, source_target_pairs={{0,16},{4,20},{8,24},{12,28},{16,0},{20,4},{24,8},{28,12},{1,17},{... | collective-permute-start | bytes 442376 | tf_op jit(solution)/shard_map/ppermute | solution.py:47
  6.3 0.0 collective-permute-start.2
  6.3 0.0 collective-permute-start.3
  6.4 2.8 %collective-permute-done.refs_1_ = bf16[2,144,256]{2,1,0:T(8,128)(2,1)S(1)} collective-permute-done((bf16[2,144,256]{2,1,0:T(8,128)(2,1)S(1)}, bf16[2,144,256]{2,1,0:T(8,128)(2,1)S(1)}, u32[]{:S(2)}, u32[]{:S(2)}) %collective-permute-start) | collective-permute-done | bytes 147488 | tf_op jit(solution)/shard_map/ppermute | solution.py:47
  9.2 0.0 collective-permute-start.4
  9.2 4.1 %collective-permute-done.1.refs_2_ = bf16[2,144,256]{2,1,0:T(8,128)(2,1)S(1)} collective-permute-done((bf16[2,144,256]{2,1,0:T(8,128)(2,1)S(1)}, bf16[2,144,256]{2,1,0:T(8,128)(2,1)S(1)}, u32[]{:S(2)}, u32[]{:S(2)}) %collective-permute-start.1) | collective-permute-done | bytes 147488 | tf_op jit(solution)/shard_map/ppermute | solution.py:47
  13.3 0.0 collective-permute-start.5
  13.3 0.0 collective-permute-done.2.refs_3_
  13.3 0.5 collective-permute-start.6
  13.8 0.0 collective-permute-done.3.refs_4_
  13.8 0.0 collective-permute-done.4.refs_5_
  13.8 0.9 %collective-permute-done.5.refs_6_ = bf16[2,144,256]{2,1,0:T(8,128)(2,1)S(1)} collective-permute-done((bf16[2,144,256]{2,1,0:T(8,128)(2,1)S(1)}, bf16[2,144,256]{2,1,0:T(8,128)(2,1)S(1)}, u32[]{:S(2)}, u32[]{:S(2)}) %collective-permute-start.5) | collective-permute-done | bytes 147488 | tf_op jit(solution)/shard_map/ppermute | solution.py:47
  14.6 0.2 collective-permute-done.6.refs_7_
  14.9 2.5 %forward.1 = (bf16[32,8,128]{2,1,0:T(8,128)(2,1)S(1)}, f32[8,128,256]{2,1,0:T(8,128)S(1)}, f32[8,2,128,256]{3,2,1,0:T(8,128)S(1)}, f32[8,2,128,256]{3,2,1,0:T(8,...) custom-call(s32[1]{0:T(128)} %constant.17.clone.1.offset_ref, ...), custom_call_target="tpu_custom_call" | custom-call | tf_op jit(solution)/shard_map/forward/pallas_call | solution.py:379
  17.3 12.2 %all_to_all.10.recv_ref = bf16[32,8,128]{2,1,0:T(8,128)(2,1)S(1)} all-to-all(bf16[32,8,128]{2,1,0:T(8,128)(2,1)S(1)} %get-tuple-element.33), channel_id=1, replica_groups=mesh['tm'=8,'lat'=4] {'tm','lat'}, dimensions={0} | all-to-all | bytes 131072 | tf_op jit(solution)/shard_map/all_to_all | solution.py:400
  29.6 0.0 copy-done.1
  29.6 0.4 owner.1
  30.0 9.0 %all_to_all.11.recv_ref = bf16[32,4,128]{2,1,0:T(4,128)(2,1)S(1)} all-to-all(bf16[32,4,128]{2,1,0:T(4,128)(2,1)S(1)} %owner.1), channel_id=1, replica_groups=mesh['tm'=8,'lat'=4] {'tm','lat'}, dimensions={0} | all-to-all | bytes 65536 | tf_op jit(solution)/shard_map/all_to_all | solution.py:414
  39.0 0.0 copy-start
  39.0 2.6 %backward.1 = (bf16[2,128,256]{2,1,0:T(8,128)(2,1)S(1)}, bf16[2,128,256]{2,1,0:T(8,128)(2,1)S(1)}, bf16[2,128,256]{2,1,0:T(8,128)(2,1)S(1)}, bf16[2,128,256]{2,1,0:T(8,128)(2,1)S(1)}) custom-call(bf16[32,4,128]{2,1,0:T(4,128)(2,1)S(1)} %all_to_all.11.recv_ref, bf16[8,16,256]{2,1,0:T(8,128)(2,1)S(1)} %get-tuple-element.35.lines_ref, ...), custom_call_target="tpu_custom_call" | custom-call | tf_op jit(solution)/shard_map/backward/pallas_call | solution.py:415
  41.6 0.7 %collective-permute-start.7 = (bf16[2,128,256]{2,1,0:T(8,128)(2,1)S(1)}, bf16[2,128,256]{2,1,0:T(8,128)(2,1)S(1)}, u32[]{:S(2)}, u32[]{:S(2)}) collective-permute-start(bf16[2,128,256]{2,1,0:T(8,128)(2,1)S(1)} %get-tuple-element.44), channel_id=1, source_target_pairs={{0,8},{4,12},{8,0},{12,4},{16,24},{20,28},{24,16},{28,20},{1,9},{5... | collective-permute-start | bytes 393224 | tf_op jit(solution)/shard_map/ppermute | solution.py:47
  42.3 0.5 collective-permute-start.8
  42.8 2.4 %collective-permute-start.9 = (bf16[2,128,256]{2,1,0:T(8,128)(2,1)S(1)}, bf16[2,128,256]{2,1,0:T(8,128)(2,1)S(1)}, u32[]{:S(2)}, u32[]{:S(2)}) collective-permute-start(bf16[2,128,256]{2,1,0:T(8,128)(2,1)S(1)} %get-tuple-element.46), channel_id=1, source_target_pairs={{0,24},{4,28},{8,16},{12,20},{16,8},{20,12},{24,0},{28,4},{1,25},{... | collective-permute-start | bytes 393224 | tf_op jit(solution)/shard_map/ppermute | solution.py:47
  45.2 0.0 collective-permute-start.10
  45.2 2.6 %collective-permute-done.7.refs_1_ = bf16[2,128,256]{2,1,0:T(8,128)(2,1)S(1)} collective-permute-done((bf16[2,128,256]{2,1,0:T(8,128)(2,1)S(1)}, bf16[2,128,256]{2,1,0:T(8,128)(2,1)S(1)}, u32[]{:S(2)}, u32[]{:S(2)}) %collective-permute-start.7) | collective-permute-done | bytes 131104 | tf_op jit(solution)/shard_map/ppermute | solution.py:47
  47.8 0.0 collective-permute-start.11
  47.8 2.4 %collective-permute-done.8.refs_2_ = bf16[2,128,256]{2,1,0:T(8,128)(2,1)S(1)} collective-permute-done((bf16[2,128,256]{2,1,0:T(8,128)(2,1)S(1)}, bf16[2,128,256]{2,1,0:T(8,128)(2,1)S(1)}, u32[]{:S(2)}, u32[]{:S(2)}) %collective-permute-start.8) | collective-permute-done | bytes 131104 | tf_op jit(solution)/shard_map/ppermute | solution.py:47
  50.2 0.0 collective-permute-start.12
  50.2 0.0 collective-permute-done.9.refs_3_
  50.2 0.5 collective-permute-start.13
  50.7 0.0 collective-permute-done.10.refs_4_
  50.7 0.0 collective-permute-done.11.refs_5_
  50.7 0.8 %collective-permute-done.12.refs_6_ = bf16[2,128,256]{2,1,0:T(8,128)(2,1)S(1)} collective-permute-done((bf16[2,128,256]{2,1,0:T(8,128)(2,1)S(1)}, bf16[2,128,256]{2,1,0:T(8,128)(2,1)S(1)}, u32[]{:S(2)}, u32[]{:S(2)}) %collective-permute-start.12) | collective-permute-done | bytes 131104 | tf_op jit(solution)/shard_map/ppermute | solution.py:47
  51.5 0.2 collective-permute-done.13.refs_7_
  51.7 0.0 copy-done
  51.7 1.1 %update.1 = f32[16,64,256]{2,1,0:T(8,128)} custom-call(f32[16,64,256]{2,1,0:T(8,128)S(1)} %bitcast.12, bf16[2,128,256]{2,1,0:T(8,128)(2,1)S(1)} %get-tuple-element.43.refs_0_, bf16[2,128,256]{2,1,0:T(8,128)(2,1)S(1)} %collective-permute-done.7.refs_1_, bf16[2,128,256]{2,1,0:T(8,128)(2,1)S(1)} %collective-permute-done.8.refs_2_, ...), custom_call_target="tpu_custom_call" | custom-call | tf_op jit(solution)/shard_map/update/pallas_call | solution.py:430
Async XLA Ops:
  0.0 29.6 %copy-start.1 = (bf16[1,1,1024,1024]{3,2,1,0:T(8,128)(2,1)S(1)}, bf16[1,1,1024,1024]{3,2,1,0:T(8,128)(2,1)}, u32[]{:S(2)}) copy-start(bf16[1,1,1024,1024]{3,2,1,0:T(8,128)(2,1)} %param.15) | copy-start | bytes 6291460
  1.8 7.4 %collective-permute-start = (bf16[2,144,256]{2,1,0:T(8,128)(2,1)S(1)}, bf16[2,144,256]{2,1,0:T(8,128)(2,1)S(1)}, u32[]{:S(2)}, u32[]{:S(2)}) collective-permute-start(bf16[2,144,256]{2,1,0:T(8,128)(2,1)S(1)} %get-tuple-element.30), channel_id=1, source_target_pairs={{0,8},{4,12},{8,0},{12,4},{16,24},{20,28},{24,16},{28,20},{1,9},{5... | collective-permute-start | bytes 442376 | tf_op jit(solution)/shard_map/ppermute | solution.py:47
  4.8 8.5 %collective-permute-start.1 = (bf16[2,144,256]{2,1,0:T(8,128)(2,1)S(1)}, bf16[2,144,256]{2,1,0:T(8,128)(2,1)S(1)}, u32[]{:S(2)}, u32[]{:S(2)}) collective-permute-start(bf16[2,144,256]{2,1,0:T(8,128)(2,1)S(1)} %get-tuple-element.31), channel_id=1, source_target_pairs={{0,16},{4,20},{8,24},{12,28},{16,0},{20,4},{24,8},{28,12},{1,17},{... | collective-permute-start | bytes 442376 | tf_op jit(solution)/shard_map/ppermute | solution.py:47
  6.3 7.0 %collective-permute-start.2 = (bf16[2,144,256]{2,1,0:T(8,128)(2,1)S(1)}, bf16[2,144,256]{2,1,0:T(8,128)(2,1)S(1)}, u32[]{:S(2)}, u32[]{:S(2)}) collective-permute-start(bf16[2,144,256]{2,1,0:T(8,128)(2,1)S(1)} %get-tuple-element.32), channel_id=1, source_target_pairs={{0,24},{4,28},{8,16},{12,20},{16,8},{20,12},{24,0},{28,4},{1,25},{... | collective-permute-start | bytes 442376 | tf_op jit(solution)/shard_map/ppermute | solution.py:47
  6.3 7.4 %collective-permute-start.3 = (bf16[2,144,256]{2,1,0:T(8,128)(2,1)S(1)}, bf16[2,144,256]{2,1,0:T(8,128)(2,1)S(1)}, u32[]{:S(2)}, u32[]{:S(2)}) collective-permute-start(bf16[2,144,256]{2,1,0:T(8,128)(2,1)S(1)} %get-tuple-element.29.refs_0_), channel_id=1, source_target_pairs={{0,4},{4,0},{8,12},{12,8},{16,20},{20,16},{24,28},{28,24},{1,5},{5... | collective-permute-start | bytes 442376 | tf_op jit(solution)/shard_map/ppermute | solution.py:47
  9.2 4.6 %collective-permute-start.4 = (bf16[2,144,256]{2,1,0:T(8,128)(2,1)S(1)}, bf16[2,144,256]{2,1,0:T(8,128)(2,1)S(1)}, u32[]{:S(2)}, u32[]{:S(2)}) collective-permute-start(bf16[2,144,256]{2,1,0:T(8,128)(2,1)S(1)} %collective-permute-done.refs_1_), channel_id=1, source_target_pairs={{0,4},{4,0},{8,12},{12,8},{16,20},{20,16},{24,28},{28,24},{1,5},{5... | collective-permute-start | bytes 442376 | tf_op jit(solution)/shard_map/ppermute | solution.py:47
  13.3 1.4 %collective-permute-start.5 = (bf16[2,144,256]{2,1,0:T(8,128)(2,1)S(1)}, bf16[2,144,256]{2,1,0:T(8,128)(2,1)S(1)}, u32[]{:S(2)}, u32[]{:S(2)}) collective-permute-start(bf16[2,144,256]{2,1,0:T(8,128)(2,1)S(1)} %collective-permute-done.1.refs_2_), channel_id=1, source_target_pairs={{0,4},{4,0},{8,12},{12,8},{16,20},{20,16},{24,28},{28,24},{1,5},{5... | collective-permute-start | bytes 442376 | tf_op jit(solution)/shard_map/ppermute | solution.py:47
  13.3 1.6 %collective-permute-start.6 = (bf16[2,144,256]{2,1,0:T(8,128)(2,1)S(1)}, bf16[2,144,256]{2,1,0:T(8,128)(2,1)S(1)}, u32[]{:S(2)}, u32[]{:S(2)}) collective-permute-start(bf16[2,144,256]{2,1,0:T(8,128)(2,1)S(1)} %collective-permute-done.2.refs_3_), channel_id=1, source_target_pairs={{0,4},{4,0},{8,12},{12,8},{16,20},{20,16},{24,28},{28,24},{1,5},{5... | collective-permute-start | bytes 442376 | tf_op jit(solution)/shard_map/ppermute | solution.py:47
  39.0 12.7 %copy-start = (f32[16,1,64,256]{3,2,1,0:T(8,128)S(1)}, f32[16,1,64,256]{3,2,1,0:T(8,128)}, u32[]{:S(2)}) copy-start(f32[16,1,64,256]{3,2,1,0:T(8,128)} %param.8) | copy-start | bytes 3145732
  41.6 6.2 %collective-permute-start.7 = (bf16[2,128,256]{2,1,0:T(8,128)(2,1)S(1)}, bf16[2,128,256]{2,1,0:T(8,128)(2,1)S(1)}, u32[]{:S(2)}, u32[]{:S(2)}) collective-permute-start(bf16[2,128,256]{2,1,0:T(8,128)(2,1)S(1)} %get-tuple-element.44), channel_id=1, source_target_pairs={{0,8},{4,12},{8,0},{12,4},{16,24},{20,28},{24,16},{28,20},{1,9},{5... | collective-permute-start | bytes 393224 | tf_op jit(solution)/shard_map/ppermute | solution.py:47
  42.3 7.9 %collective-permute-start.8 = (bf16[2,128,256]{2,1,0:T(8,128)(2,1)S(1)}, bf16[2,128,256]{2,1,0:T(8,128)(2,1)S(1)}, u32[]{:S(2)}, u32[]{:S(2)}) collective-permute-start(bf16[2,128,256]{2,1,0:T(8,128)(2,1)S(1)} %get-tuple-element.45), channel_id=1, source_target_pairs={{0,16},{4,20},{8,24},{12,28},{16,0},{20,4},{24,8},{28,12},{1,17},{... | collective-permute-start | bytes 393224 | tf_op jit(solution)/shard_map/ppermute | solution.py:47
  42.8 7.4 %collective-permute-start.9 = (bf16[2,128,256]{2,1,0:T(8,128)(2,1)S(1)}, bf16[2,128,256]{2,1,0:T(8,128)(2,1)S(1)}, u32[]{:S(2)}, u32[]{:S(2)}) collective-permute-start(bf16[2,128,256]{2,1,0:T(8,128)(2,1)S(1)} %get-tuple-element.46), channel_id=1, source_target_pairs={{0,24},{4,28},{8,16},{12,20},{16,8},{20,12},{24,0},{28,4},{1,25},{... | collective-permute-start | bytes 393224 | tf_op jit(solution)/shard_map/ppermute | solution.py:47
  45.2 5.6 %collective-permute-start.10 = (bf16[2,128,256]{2,1,0:T(8,128)(2,1)S(1)}, bf16[2,128,256]{2,1,0:T(8,128)(2,1)S(1)}, u32[]{:S(2)}, u32[]{:S(2)}) collective-permute-start(bf16[2,128,256]{2,1,0:T(8,128)(2,1)S(1)} %get-tuple-element.43.refs_0_), channel_id=1, source_target_pairs={{0,4},{4,0},{8,12},{12,8},{16,20},{20,16},{24,28},{28,24},{1,5},{5... | collective-permute-start | bytes 393224 | tf_op jit(solution)/shard_map/ppermute | solution.py:47
  47.8 2.9 %collective-permute-start.11 = (bf16[2,128,256]{2,1,0:T(8,128)(2,1)S(1)}, bf16[2,128,256]{2,1,0:T(8,128)(2,1)S(1)}, u32[]{:S(2)}, u32[]{:S(2)}) collective-permute-start(bf16[2,128,256]{2,1,0:T(8,128)(2,1)S(1)} %collective-permute-done.7.refs_1_), channel_id=1, source_target_pairs={{0,4},{4,0},{8,12},{12,8},{16,20},{20,16},{24,28},{28,24},{1,5},{5... | collective-permute-start | bytes 393224 | tf_op jit(solution)/shard_map/ppermute | solution.py:47
  50.2 1.3 %collective-permute-start.12 = (bf16[2,128,256]{2,1,0:T(8,128)(2,1)S(1)}, bf16[2,128,256]{2,1,0:T(8,128)(2,1)S(1)}, u32[]{:S(2)}, u32[]{:S(2)}) collective-permute-start(bf16[2,128,256]{2,1,0:T(8,128)(2,1)S(1)} %collective-permute-done.8.refs_2_), channel_id=1, source_target_pairs={{0,4},{4,0},{8,12},{12,8},{16,20},{20,16},{24,28},{28,24},{1,5},{5... | collective-permute-start | bytes 393224 | tf_op jit(solution)/shard_map/ppermute | solution.py:47
  50.2 1.5 %collective-permute-start.13 = (bf16[2,128,256]{2,1,0:T(8,128)(2,1)S(1)}, bf16[2,128,256]{2,1,0:T(8,128)(2,1)S(1)}, u32[]{:S(2)}, u32[]{:S(2)}) collective-permute-start(bf16[2,128,256]{2,1,0:T(8,128)(2,1)S(1)} %collective-permute-done.9.refs_3_), channel_id=1, source_target_pairs={{0,4},{4,0},{8,12},{12,8},{16,20},{20,16},{24,28},{28,24},{1,5},{5... | collective-permute-start | bytes 393224 | tf_op jit(solution)/shard_map/ppermute | solution.py:47

commit v5 on v4

--- a/solution.py
+++ b/solution.py
@@ -38,62 +38,68 @@
         lax.fori_loop(0, count, lambda index, carry: (step(index), carry)[1], 0)
 
 
-def exchange(pieces):
-    size = lax.axis_size("tm")
-    if len(pieces) == 1:
+def swap(values, distance):
+    return lax.ppermute(values, "tm", [(k, k ^ distance) for k in range(lax.axis_size("tm"))])
+
+
+def exchange(pieces, shifts):
+    if shifts is None:
         return [lax.all_to_all(pieces[0], "tm", split_axis=0, concat_axis=0, tiled=True)]
-
-    def swap(values, distance):
-        return lax.ppermute(values, "tm", [(k, k ^ distance) for k in range(size)])
-
-    arrived = [pieces[0]] + [swap(piece, 2 * s) for s, piece in enumerate(pieces) if s]
+    arrived = [swap(piece, 2 * s) if s else piece for piece, s in zip(pieces, shifts)]
     return arrived + [swap(piece, 1) for piece in arrived]
 
 
-def departures(refs, times):
-    if len(refs) == 1:
+def departures(refs, times, shifts):
+    if shifts is None:
         return [(t, refs[0], t) for t in range(times)]
     me = lax.axis_index("tm")
-    return [(((me // 2) ^ s) * 2 + ((me % 2) ^ k), ref, k) for s, ref in enumerate(refs) for k in range(2)]
-
-
-def arrivals(refs, times):
-    if len(refs) == 1:
+    return [(((me // 2) ^ s) * 2 + ((me % 2) ^ k), ref, k) for s, ref in zip(shifts, refs) for k in range(2)]
+
+
+def arrivals(refs, times, shifts):
+    if shifts is None:
         return [(t, refs[0], t) for t in range(times)]
     me = lax.axis_index("tm")
-    chips = len(refs) // 2
-    return [(((me // 2) ^ s) * 2 + ((me % 2) ^ k), refs[k * chips + s], k) for s in range(chips) for k in range(2)]
-
-
-def pack_kernel(dims, sends, state_hbm, pick_hbm, slot_hbm, win_turned_hbm, wmid_hbm, wout_hbm, observed_hbm, *refs):
+    halves = (refs[: len(shifts)], refs[len(shifts) :])
+    return [(((me // 2) ^ s) * 2 + ((me % 2) ^ k), halves[k][i], k) for i, s in enumerate(shifts) for k in range(2)]
+
+
+def put(ref, row, state, lines):
+    rows, extra = state.shape[0], lines.shape[0]
+    if len(ref.shape) == 3:
+        ref[row, 0:rows] = state
+        ref[row, rows:] = lines
+    else:
+        ref[row * (rows + extra) : row * (rows + extra) + rows] = state
+        if row == 0:
+            ref[rows : rows + extra] = lines
+
+
+def take(ref, row, rows, extra):
+    if len(ref.shape) == 3:
+        return ref[row, 0:rows], ref[row, rows:]
+    return ref[row * (rows + extra) : row * (rows + extra) + rows], ref[rows : rows + extra]
+
+
+def pack_kernel(dims, shifts, state_hbm, pick_hbm, slot_hbm, *refs):
     groups, parts, members, chan, width, owners, pairs, extra = dims
-    outs = refs[:sends]
-    win_ref, wmid_ref, wmid_turned_ref, wout_turned_ref, win_turned, wout, observed = refs[sends : sends + 7]
-    state, pick_vmem, slot_ref, wmid, state_sems, sems = refs[sends + 7 :]
+    outs, (lines_ref, state, pick_vmem, slot_ref, state_sems, sems) = refs[:-6], refs[-6:]
     times = groups * parts
     rows = members * chan
     per_row = width // LANES
     rows_each = owners * pairs // per_row
-    targets = departures(outs, times)
-    small = []
-    pairs_of = (
-        (pick_hbm, pick_vmem), (slot_hbm, slot_ref), (win_turned_hbm, win_turned), (wmid_hbm, wmid), (wout_hbm, wout),
-        (observed_hbm, observed),
-    )
-    for index, (source, target) in enumerate(pairs_of):
-        small.append(pltpu.make_async_copy(source, target, sems.at[index]))
-    small[0].start()
-    small[1].start()
+    targets = departures(outs, times, shifts)
+    small = [pltpu.make_async_copy(pick_hbm, pick_vmem, sems.at[0]), pltpu.make_async_copy(slot_hbm, slot_ref, sems.at[1])]
+    for copy in small:
+        copy.start()
     copies = []
     for index, (t, _, _) in enumerate(targets):
         if index % parts == 0:
             span = pl.ds((t // parts) * members, members)
             copies.append(pltpu.make_async_copy(state_hbm.at[span], state.at[index // parts], state_sems.at[index // parts]))
             copies[-1].start()
-    for copy in small[2:]:
-        copy.start()
-    small[0].wait()
-    small[1].wait()
+    for copy in small:
+        copy.wait()
     pick = pick_vmem[...].astype(F32)
     channel = jnp.floor((pick + 0.5) * (1.0 / (width * parts)))
     place = pick - channel * (width * parts)
@@ -108,21 +114,38 @@
     if extra > len(lines):
         lines.append(jnp.zeros((extra - len(lines), width), F32))
     lines = jnp.concatenate(lines, axis=0).astype(BF)
-    for _, out, row in targets:
-        out[row, rows:] = lines
+    lines_ref[...] = lines
     for index, (t, out, row) in enumerate(targets):
         if index % parts == 0:
             copies[index // parts].wait()
             block = state[index // parts].astype(BF)
         part = index % parts
-        out[row, 0:rows] = block[:, :, part * width : (part + 1) * width].reshape(rows, width)
-    for copy in small[2:]:
+        put(out, row, block[:, :, part * width : (part + 1) * width].reshape(rows, width), lines)
+
+
+def prepare_kernel(dims, shifts, lines_ref, state_hbm, win_turned_hbm, wmid_hbm, wout_hbm, observed_hbm, *refs):
+    members, chan = dims
+    outs, refs = refs[:-9], refs[-9:]
+    state, win_ref, wmid_ref, wmid_turned_ref, wout_turned_ref, win_turned, wout, observed, sems = refs[:9]
+    rows = members * chan
+    moves = (
+        (wmid_hbm, wmid_ref), (win_turned_hbm, win_turned), (wout_hbm, wout), (observed_hbm, observed), (state_hbm, state),
+    )
+    copies = [pltpu.make_async_copy(source, target, sems.at[index]) for index, (source, target) in enumerate(moves)]
+    for copy in copies:
+        copy.start()
+    for copy in copies[:-1]:
         copy.wait()
     half = jnp.asarray(0.5, BF)
+    wmid = wmid_ref[...]
     win_ref[...] = win_turned[...].T * half
-    wmid_ref[...] = wmid[...] * half
-    wmid_turned_ref[...] = wmid[...].T * half
+    wmid_turned_ref[...] = wmid.T * half
     wout_turned_ref[...] = wout[...].T * half
+    wmid_ref[...] = wmid * half
+    copies[-1].wait()
+    if outs:
+        for t, out, row in departures(outs, 0, shifts):
+            put(out, row, state[pl.ds(t * members, members)].astype(BF).reshape(rows, -1), lines_ref[...])
 
 
 def row_of(ref, time, base, block):
@@ -132,7 +155,7 @@
     return ref[time, row : row + 1, start : start + LANES].astype(F32)
 
 
-def forward_kernel(dims, offset_ref, win_ref, wmid_ref, wout_ref, *refs):
+def forward_kernel(dims, shifts, offset_ref, win_ref, wmid_ref, wout_ref, *refs):
     send_ref, total_ref, pre_one_ref, pre_two_ref, at_pixel_ref, lines_ref = refs[-10:-4]
     padded, sums, hidden_one, hidden_two = refs[-4:]
     times, members, chan, width, owners, pairs, extra = dims
@@ -142,9 +165,9 @@
     zero_state = jnp.zeros((radius, members, chan, width), BF)
     padded[0:radius] = zero_state
     padded[radius + times :] = zero_state
-    for t, ref, row in arrivals(refs[:-10], times):
-        padded[t + radius] = ref[row, 0:rows].reshape(members, chan, width)
-        lines_ref[t] = ref[row, rows:]
+    for t, ref, row in arrivals(refs[:-10], times, shifts):
+        state, lines_ref[t] = take(ref, row, rows, extra)
+        padded[t + radius] = state.reshape(members, chan, width)
     sums[...] = jnp.zeros_like(sums)
 
     def first(s):
@@ -251,7 +274,7 @@
 
 
 def backward_kernel(
-    dims, recv_ref, lines_ref, at_pixel_ref, win_ref, wmid_ref, wout_ref, total_ref, pre_one_ref, pre_two_ref, *refs
+    dims, shifts, recv_ref, lines_ref, at_pixel_ref, win_ref, wmid_ref, wout_ref, total_ref, pre_one_ref, pre_two_ref, *refs
 ):
     padded, sums, grad_one, grad_two = refs[-4:]
     times, members, chan, width, owners, pairs, extra = dims
@@ -302,15 +325,15 @@
     loop(times, second)
     loop(times, third)
 
-    for t, ref, row in departures(refs[:-4], times):
+    for t, ref, row in departures(refs[:-4], times, shifts):
         ref[row] = sums[t + radius].reshape(rows, width).astype(BF)
 
 
-def update_kernel(dims, state_ref, *refs):
+def update_kernel(dims, shifts, state_ref, *refs):
     times, parts, members, chan, width = dims
     out_hbm, out, sems = refs[-3:]
     copies = []
-    for index, (t, ref, row) in enumerate(arrivals(refs[:-3], times)):
+    for index, (t, ref, row) in enumerate(arrivals(refs[:-3], times, shifts)):
         span = pl.ds((t // parts) * members, members)
         part = index % parts
         change = ref[row].reshape(members, chan, width).astype(F32)
@@ -321,6 +344,10 @@
             copies[-1].start()
     for copy in copies:
         copy.wait()
+
+
+def update_rest_kernel(dims, shifts, written_hbm, state_ref, *refs):
+    update_kernel(dims, shifts, state_ref, *refs)
 
 
 def body(noisy_state, w_in, w_mid, w_out, obs_pick, obs_slot, observed, precision):
@@ -341,13 +368,34 @@
     smem = pl.BlockSpec(memory_space=pltpu.SMEM)
     vmem = pl.BlockSpec(memory_space=pltpu.VMEM)
     hbm = pl.BlockSpec(memory_space=pltpu.HBM)
-    sends = times // 2 if parts == 1 and times in (4, 8) else 1
+    shifts = range(times // 2) if parts == 1 and times in (4, 8) else None
+    sends = len(shifts) if shifts else 1
     each = times // sends
-    sources = (current, obs_pick[0, 0], obs_slot[0, 0].T, w_in.T, w_mid, w_out, observed.reshape(positions, block_rows))
-    *payload, win, wmid, wmid_turned, wout_turned, win_turned, wout, seen = pl.pallas_call(
-        functools.partial(pack_kernel, (groups, parts, members, chan, width, owners, pairs, extra), sends),
+    first = 1 if shifts else 0
+    here = lambda *arrays: [pltpu.with_memory_space_constraint(x, pltpu.HBM) for x in arrays]
+    piece = jax.ShapeDtypeStruct((2 * rows + extra, width) if shifts else (times, rows + extra, width), BF)
+    *payload, lines = pl.pallas_call(
+        functools.partial(
+            pack_kernel, (groups, parts, members, chan, width, owners, pairs, extra), shifts and shifts[1:]
+        ),
+        out_shape=(*[piece] * (sends - first), jax.ShapeDtypeStruct((extra, width), BF)),
+        in_specs=[hbm] * 3,
+        out_specs=(vmem,) * (sends - first + 1),
+        scratch_shapes=[
+            pltpu.VMEM((groups, members, chan, pixels), F32),
+            pltpu.VMEM((owners, pairs, block_rows), jnp.int32),
+            pltpu.SMEM((pairs, owners), jnp.int32),
+            pltpu.SemaphoreType.DMA((groups,)),
+            pltpu.SemaphoreType.DMA((2,)),
+        ],
+        compiler_params=limit(16),
+        name="pack",
+    )(*here(current, obs_pick[0, 0], obs_slot[0, 0].T))
+    *own, state, win, wmid, wmid_turned, wout_turned, win_turned, wout, seen = pl.pallas_call(
+        functools.partial(prepare_kernel, (members, chan), shifts and shifts[:1]),
         out_shape=(
-            *(jax.ShapeDtypeStruct((each, rows + extra, width), BF) for _ in range(sends)),
+            *[piece] * first,
+            jax.ShapeDtypeStruct(current.shape, F32),
             jax.ShapeDtypeStruct(w_in.shape, BF),
             jax.ShapeDtypeStruct(w_mid.shape, BF),
             jax.ShapeDtypeStruct(w_mid.shape[::-1], BF),
@@ -356,20 +404,13 @@
             jax.ShapeDtypeStruct(w_out.shape, BF),
             jax.ShapeDtypeStruct((positions, block_rows), F32),
         ),
-        in_specs=[hbm] * 7,
-        out_specs=(vmem,) * (sends + 7),
-        scratch_shapes=[
-            pltpu.VMEM((groups, members, chan, pixels), F32),
-            pltpu.VMEM((owners, pairs, block_rows), jnp.int32),
-            pltpu.SMEM((pairs, owners), jnp.int32),
-            pltpu.VMEM(w_mid.shape, BF),
-            pltpu.SemaphoreType.DMA((groups,)),
-            pltpu.SemaphoreType.DMA((6,)),
-        ],
+        in_specs=[vmem] + [hbm] * 5,
+        out_specs=(vmem,) * (first + 8),
+        scratch_shapes=[pltpu.SemaphoreType.DMA((5,))],
         compiler_params=limit(16),
-        name="pack",
-    )(*(pltpu.with_memory_space_constraint(x, pltpu.HBM) for x in sources))
-    received = exchange(payload)
+        name="prepare",
+    )(lines, *here(current, w_in.T, w_mid, w_out, observed.reshape(positions, block_rows)))
+    received = exchange(own + payload, shifts)
 
     offset = ((lax.axis_index("tm") % parts) * width).astype(jnp.int32).reshape(1)
     dims = (times, members, chan, width, owners, pairs, extra)
@@ -377,7 +418,7 @@
     inner = (times, members, hidden, width)
     padded_shape = (times + 2 * radius, members, chan, width)
     packed, total, pre_one, pre_two, at_pixel, lines = pl.pallas_call(
-        functools.partial(forward_kernel, dims),
+        functools.partial(forward_kernel, dims, shifts),
         out_shape=(
             jax.ShapeDtypeStruct((times * owners, rows_two, LANES), BF),
             jax.ShapeDtypeStruct((times, rows, width), F32),
@@ -413,7 +454,7 @@
     )(arrived, seen, precision[0, 0])
     returned = lax.all_to_all(answer, ("tm", "lat"), split_axis=0, concat_axis=0, tiled=True)
     change = pl.pallas_call(
-        functools.partial(backward_kernel, dims),
+        functools.partial(backward_kernel, dims, shifts),
         out_shape=tuple(jax.ShapeDtypeStruct((each, rows, width), BF) for _ in range(sends)),
         in_specs=[vmem] * 9,
         out_specs=(vmem,) * sends,
@@ -426,16 +467,24 @@
         compiler_params=limit(24),
         name="backward",
     )(returned, lines, at_pixel, win_turned, wmid_turned, wout_turned, total, pre_one, pre_two)
-    back = exchange(change)
-    updated = pl.pallas_call(
-        functools.partial(update_kernel, (times, parts, members, chan, width)),
-        out_shape=jax.ShapeDtypeStruct(current.shape, F32),
-        in_specs=[vmem] * (1 + len(back)),
-        out_specs=hbm,
-        scratch_shapes=[pltpu.VMEM(current.shape, F32), pltpu.SemaphoreType.DMA((groups,))],
-        compiler_params=limit(16),
-        name="update",
-    )(current, *back)
+    back = exchange(change, shifts)
+    early = sends // 2
+    mates = back[sends:]
+    stages = ((back[:early] + mates[:early], shifts[:early]), (back[early:sends] + mates[early:], shifts[early:])) if shifts else ((back, None),)
+    updated = None
+    for arrays, part_of in stages:
+        kernel = update_kernel if updated is None else update_rest_kernel
+        written = [] if updated is None else [updated]
+        updated = pl.pallas_call(
+            functools.partial(kernel, (times, parts, members, chan, width), part_of),
+            out_shape=jax.ShapeDtypeStruct(current.shape, F32),
+            in_specs=[hbm] * len(written) + [vmem] * (1 + len(arrays)),
+            out_specs=hbm,
+            scratch_shapes=[pltpu.VMEM(current.shape, F32), pltpu.SemaphoreType.DMA((groups,))],
+            input_output_aliases={0: 0} if written else {},
+            compiler_params=limit(16),
+            name="update",
+        )(*written, state, *arrays)
     return updated[:, None]
 
 

time: 53 us -> 52.2 us (0.985)
  waiting for transfers between devices: 14 us -> 11.3 us
  Pallas kernels: 8.32 us -> 10.2 us
    ppermute x14, waiting for transfers between devices: 14 us -> 11.3 us  [swap(): lax.ppermute(values, 'tm', [(k, k ^ distance) for k in range(lax.axis_siz...]
    pallas_call x3 -> x5, Pallas kernels: 6.11 us -> 8.26 us  [the longest x1 2.61 us: body(): pl.pallas_call(functools.partial(backward_kernel, dims, shifts), out_shap...]
  transfers between devices with their start and end apart: 14 -> 14, of which waited for: 8 -> 7; matrix products, arithmetic and copies ran while one was open for 0% -> 0% of each run, Pallas kernels for 0% -> 4%
where the time goes in v5:
time: 52.2 us; the launch traced here: 52 us
  blocking collectives  21.2 us (41%)
  waiting for transfers between devices  11.3 us (22%)
  Pallas kernels  10.2 us (20%)
  starting transfers between devices  9.23 us (18%)
    all_to_all x1, blocking collectives, body(): lax.all_to_all(packed, ('tm', 'lat'), split_axis=0, concat_axis=0, tiled=...  12.2 us
    ppermute x14, waiting for transfers between devices, swap(): lax.ppermute(values, 'tm', [(k, k ^ distance) for k in range(lax.axis_siz...  11.3 us
    ppermute x14, starting transfers between devices, swap(): lax.ppermute(values, 'tm', [(k, k ^ distance) for k in range(lax.axis_siz...  9.23 us
    all_to_all x1, blocking collectives, body(): lax.all_to_all(answer, ('tm', 'lat'), split_axis=0, concat_axis=0, tiled=...  8.99 us
    pallas_call x1, Pallas kernels, body(): pl.pallas_call(functools.partial(backward_kernel, dims, shifts), out_shap...  2.61 us
    pallas_call x1, Pallas kernels, body(): pl.pallas_call(functools.partial(forward_kernel, dims, shifts), out_shape...  2.49 us
    pallas_call x2, Pallas kernels, body(): pl.pallas_call(functools.partial(kernel, (times, parts, members, chan, wi...  1.76 us
    pallas_call x1, Pallas kernels, body(): pl.pallas_call(functools.partial(pack_kernel, (groups, parts, members, ch...  1.45 us
  transfers between devices with their start and end apart: 14, of which 7 were waited for; matrix products, arithmetic and copies ran while one was open for 0% of the time, Pallas kernels for 4%

profile of v5, /device:TPU:0, one launch (start us, length us, event | category | flops | bytes accessed | tf_op | source)
XLA Modules:
  0.0 52.0 jit_solution(9061161431057053533)
XLA Ops:
  0.0 0.0 copy-start
  0.0 1.5 %pack.1 = (bf16[272,256]{1,0:T(8,128)(2,1)S(1)}, bf16[272,256]{1,0:T(8,128)(2,1)S(1)}, bf16[272,256]{1,0:T(8,128)(2,1)S(1)}, bf16[16,256]{1,0:T(8,128)(2,1)S(1)}) custom-call(f32[16,64,256]{2,1,0:T(8,128)} %bitcast.12, s32[4,2,128]{2,1,0:T(2,128)} %bitcast.15, s32[2,4]{1,0:T(2,128)} %bitcast.17), custom_call_target="tpu_custom_call" | custom-call | tf_op jit(solution)/shard_map/pack/pallas_call | solution.py:377
  1.5 3.0 %collective-permute-start = (bf16[272,256]{1,0:T(8,128)(2,1)S(1)}, bf16[272,256]{1,0:T(8,128)(2,1)S(1)}, u32[]{:S(2)}, u32[]{:S(2)}) collective-permute-start(bf16[272,256]{1,0:T(8,128)(2,1)S(1)} %get-tuple-element.34), channel_id=1, source_target_pairs={{0,8},{4,12},{8,0},{12,4},{16,24},{20,28},{24,16},{28,20},{1,9},{5... | collective-permute-start | bytes 417800 | tf_op jit(solution)/shard_map/ppermute | solution.py:42
  4.5 1.5 %collective-permute-start.1 = (bf16[272,256]{1,0:T(8,128)(2,1)S(1)}, bf16[272,256]{1,0:T(8,128)(2,1)S(1)}, u32[]{:S(2)}, u32[]{:S(2)}) collective-permute-start(bf16[272,256]{1,0:T(8,128)(2,1)S(1)} %get-tuple-element.35), channel_id=1, source_target_pairs={{0,16},{4,20},{8,24},{12,28},{16,0},{20,4},{24,8},{28,12},{1,17},{... | collective-permute-start | bytes 417800 | tf_op jit(solution)/shard_map/ppermute | solution.py:42
  6.0 0.0 collective-permute-start.2
  6.0 1.4 %prepare.1 = (bf16[272,256]{1,0:T(8,128)(2,1)S(1)}, f32[16,64,256]{2,1,0:T(8,128)S(1)}, bf16[128,320]{1,0:T(8,128)(2,1)S(1)}, bf16[128,128]{1,0:T(8,128)(2,1)S(1...) custom-call(bf16[16,256]{1,0:T(8,128)(2,1)S(1)} %get-tuple-element.2, ...), custom_call_target="tpu_custom_call" | custom-call | tf_op jit(solution)/shard_map/prepare/pallas_call | solution.py:394
  7.5 0.1 collective-permute-start.3
  7.5 1.0 %collective-permute-done.refs_1_ = bf16[272,256]{1,0:T(8,128)(2,1)S(1)} collective-permute-done((bf16[272,256]{1,0:T(8,128)(2,1)S(1)}, bf16[272,256]{1,0:T(8,128)(2,1)S(1)}, u32[]{:S(2)}, u32[]{:S(2)}) %collective-permute-start) | collective-permute-done | bytes 139296 | tf_op jit(solution)/shard_map/ppermute | solution.py:42
  8.6 0.0 collective-permute-start.4
  8.6 4.1 %collective-permute-done.1.refs_2_ = bf16[272,256]{1,0:T(8,128)(2,1)S(1)} collective-permute-done((bf16[272,256]{1,0:T(8,128)(2,1)S(1)}, bf16[272,256]{1,0:T(8,128)(2,1)S(1)}, u32[]{:S(2)}, u32[]{:S(2)}) %collective-permute-start.1) | collective-permute-done | bytes 139296 | tf_op jit(solution)/shard_map/ppermute | solution.py:42
  12.6 0.0 collective-permute-start.5
  12.6 0.0 collective-permute-done.2.refs_3_
  12.6 0.5 collective-permute-start.6
  13.1 0.0 collective-permute-done.3.refs_4_
  13.1 0.0 collective-permute-done.4.refs_5_
  13.1 0.8 %collective-permute-done.5.refs_6_ = bf16[272,256]{1,0:T(8,128)(2,1)S(1)} collective-permute-done((bf16[272,256]{1,0:T(8,128)(2,1)S(1)}, bf16[272,256]{1,0:T(8,128)(2,1)S(1)}, u32[]{:S(2)}, u32[]{:S(2)}) %collective-permute-start.5) | collective-permute-done | bytes 139296 | tf_op jit(solution)/shard_map/ppermute | solution.py:42
  14.0 0.2 collective-permute-done.6.refs_7_
  14.2 2.5 %forward.1 = (bf16[32,8,128]{2,1,0:T(8,128)(2,1)S(1)}, f32[8,128,256]{2,1,0:T(8,128)S(1)}, f32[8,2,128,256]{3,2,1,0:T(8,128)S(1)}, f32[8,2,128,256]{3,2,1,0:T(8,...) custom-call(s32[1]{0:T(128)} %constant.17.clone.1.offset_ref, ...), custom_call_target="tpu_custom_call" | custom-call | tf_op jit(solution)/shard_map/forward/pallas_call | solution.py:420
  16.7 12.2 %all_to_all.10.recv_ref = bf16[32,8,128]{2,1,0:T(8,128)(2,1)S(1)} all-to-all(bf16[32,8,128]{2,1,0:T(8,128)(2,1)S(1)} %get-tuple-element.37), channel_id=1, replica_groups=mesh['tm'=8,'lat'=4] {'tm','lat'}, dimensions={0} | all-to-all | bytes 131072 | tf_op jit(solution)/shard_map/all_to_all | solution.py:441
  28.9 0.0 copy-done
  28.9 0.4 owner.1
  29.4 9.0 %all_to_all.11.recv_ref = bf16[32,4,128]{2,1,0:T(4,128)(2,1)S(1)} all-to-all(bf16[32,4,128]{2,1,0:T(4,128)(2,1)S(1)} %owner.1), channel_id=1, replica_groups=mesh['tm'=8,'lat'=4] {'tm','lat'}, dimensions={0} | all-to-all | bytes 65536 | tf_op jit(solution)/shard_map/all_to_all | solution.py:455
  38.4 2.6 %backward.1 = (bf16[2,128,256]{2,1,0:T(8,128)(2,1)S(1)}, bf16[2,128,256]{2,1,0:T(8,128)(2,1)S(1)}, bf16[2,128,256]{2,1,0:T(8,128)(2,1)S(1)}, bf16[2,128,256]{2,1,0:T(8,128)(2,1)S(1)}) custom-call(bf16[32,4,128]{2,1,0:T(4,128)(2,1)S(1)} %all_to_all.11.recv_ref, bf16[8,16,256]{2,1,0:T(8,128)(2,1)S(1)} %get-tuple-element.39.lines_ref, ...), custom_call_target="tpu_custom_call" | custom-call | tf_op jit(solution)/shard_map/backward/pallas_call | solution.py:456
  41.0 0.7 %collective-permute-start.7 = (bf16[2,128,256]{2,1,0:T(8,128)(2,1)S(1)}, bf16[2,128,256]{2,1,0:T(8,128)(2,1)S(1)}, u32[]{:S(2)}, u32[]{:S(2)}) collective-permute-start(bf16[2,128,256]{2,1,0:T(8,128)(2,1)S(1)} %get-tuple-element.48), channel_id=1, source_target_pairs={{0,8},{4,12},{8,0},{12,4},{16,24},{20,28},{24,16},{28,20},{1,9},{5... | collective-permute-start | bytes 393224 | tf_op jit(solution)/shard_map/ppermute | solution.py:42
  41.6 0.5 %collective-permute-start.10 = (bf16[2,128,256]{2,1,0:T(8,128)(2,1)S(1)}, bf16[2,128,256]{2,1,0:T(8,128)(2,1)S(1)}, u32[]{:S(2)}, u32[]{:S(2)}) collective-permute-start(bf16[2,128,256]{2,1,0:T(8,128)(2,1)S(1)} %get-tuple-element.49), channel_id=1, source_target_pairs={{0,16},{4,20},{8,24},{12,28},{16,0},{20,4},{24,8},{28,12},{1,17},{... | collective-permute-start | bytes 393224 | tf_op jit(solution)/shard_map/ppermute | solution.py:42
  42.2 2.3 %collective-permute-start.11 = (bf16[2,128,256]{2,1,0:T(8,128)(2,1)S(1)}, bf16[2,128,256]{2,1,0:T(8,128)(2,1)S(1)}, u32[]{:S(2)}, u32[]{:S(2)}) collective-permute-start(bf16[2,128,256]{2,1,0:T(8,128)(2,1)S(1)} %get-tuple-element.50), channel_id=1, source_target_pairs={{0,24},{4,28},{8,16},{12,20},{16,8},{20,12},{24,0},{28,4},{1,25},{... | collective-permute-start | bytes 393224 | tf_op jit(solution)/shard_map/ppermute | solution.py:42
  44.5 0.0 collective-permute-start.8
  44.5 2.6 %collective-permute-done.7.refs_1_ = bf16[2,128,256]{2,1,0:T(8,128)(2,1)S(1)} collective-permute-done((bf16[2,128,256]{2,1,0:T(8,128)(2,1)S(1)}, bf16[2,128,256]{2,1,0:T(8,128)(2,1)S(1)}, u32[]{:S(2)}, u32[]{:S(2)}) %collective-permute-start.7) | collective-permute-done | bytes 131104 | tf_op jit(solution)/shard_map/ppermute | solution.py:42
  47.2 0.0 collective-permute-start.9
  47.2 2.4 %collective-permute-done.10.refs_0_ = bf16[2,128,256]{2,1,0:T(8,128)(2,1)S(1)} collective-permute-done((bf16[2,128,256]{2,1,0:T(8,128)(2,1)S(1)}, bf16[2,128,256]{2,1,0:T(8,128)(2,1)S(1)}, u32[]{:S(2)}, u32[]{:S(2)}) %collective-permute-start.10) | collective-permute-done | bytes 131104 | tf_op jit(solution)/shard_map/ppermute | solution.py:42
  49.6 0.0 collective-permute-start.12
  49.6 0.0 collective-permute-done.11.refs_1_
  49.6 0.5 collective-permute-start.13
  50.1 0.0 collective-permute-done.8.refs_2_
  50.1 0.0 collective-permute-done.9.refs_3_
  50.1 0.9 %update.2.written_hbm = f32[16,64,256]{2,1,0:T(8,128)} custom-call(f32[16,64,256]{2,1,0:T(8,128)S(1)} %get-tuple-element.29.state_ref, bf16[2,128,256]{2,1,0:T(8,128)(2,1)S(1)} %get-tuple-element.47.refs_0_, bf16[2,128,256]{2,1,0:T(8,128)(2,1)S(1)} %collective-permute-done.7.refs_1_, bf16[2,128,256]{2,1,0:T(8,128)(2,1)S(1)} %collective-permute-done.8.refs_2_, ...), custom_call_target="tpu_custom_call" | custom-call | tf_op jit(solution)/shard_map/update/pallas_call | solution.py:478
  51.0 0.0 collective-permute-done.12.refs_2_
  51.0 0.1 collective-permute-done.13.refs_3_
  51.1 0.9 %update.3 = f32[16,64,256]{2,1,0:T(8,128)} custom-call(f32[16,64,256]{2,1,0:T(8,128)} %update.2.written_hbm, f32[16,64,256]{2,1,0:T(8,128)S(1)} %get-tuple-element.29.state_ref, bf16[2,128,256]{2,1,0:T(8,128)(2,1)S(1)} %collective-permute-done.10.refs_0_, bf16[2,128,256]{2,1,0:T(8,128)(2,1)S(1)} %collective-permute-done.11.refs_1_, ...), custom_call_target="tpu_custom_call", output_to_operand_aliasing={{}: (0, {})} | custom-call | tf_op jit(solution)/shard_map/update/pallas_call | solution.py:478
Async XLA Ops:
  0.0 28.9 %copy-start = (bf16[1,1,1024,1024]{3,2,1,0:T(8,128)(2,1)S(1)}, bf16[1,1,1024,1024]{3,2,1,0:T(8,128)(2,1)}, u32[]{:S(2)}) copy-start(bf16[1,1,1024,1024]{3,2,1,0:T(8,128)(2,1)} %param.15) | copy-start | bytes 6291460
  1.5 7.1 %collective-permute-start = (bf16[272,256]{1,0:T(8,128)(2,1)S(1)}, bf16[272,256]{1,0:T(8,128)(2,1)S(1)}, u32[]{:S(2)}, u32[]{:S(2)}) collective-permute-start(bf16[272,256]{1,0:T(8,128)(2,1)S(1)} %get-tuple-element.34), channel_id=1, source_target_pairs={{0,8},{4,12},{8,0},{12,4},{16,24},{20,28},{24,16},{28,20},{1,9},{5... | collective-permute-start | bytes 417800 | tf_op jit(solution)/shard_map/ppermute | solution.py:42
  4.5 8.1 %collective-permute-start.1 = (bf16[272,256]{1,0:T(8,128)(2,1)S(1)}, bf16[272,256]{1,0:T(8,128)(2,1)S(1)}, u32[]{:S(2)}, u32[]{:S(2)}) collective-permute-start(bf16[272,256]{1,0:T(8,128)(2,1)S(1)} %get-tuple-element.35), channel_id=1, source_target_pairs={{0,16},{4,20},{8,24},{12,28},{16,0},{20,4},{24,8},{28,12},{1,17},{... | collective-permute-start | bytes 417800 | tf_op jit(solution)/shard_map/ppermute | solution.py:42
  6.0 6.6 %collective-permute-start.2 = (bf16[272,256]{1,0:T(8,128)(2,1)S(1)}, bf16[272,256]{1,0:T(8,128)(2,1)S(1)}, u32[]{:S(2)}, u32[]{:S(2)}) collective-permute-start(bf16[272,256]{1,0:T(8,128)(2,1)S(1)} %get-tuple-element.36), channel_id=1, source_target_pairs={{0,24},{4,28},{8,16},{12,20},{16,8},{20,12},{24,0},{28,4},{1,25},{... | collective-permute-start | bytes 417800 | tf_op jit(solution)/shard_map/ppermute | solution.py:42
  7.5 5.7 %collective-permute-start.3 = (bf16[272,256]{1,0:T(8,128)(2,1)S(1)}, bf16[272,256]{1,0:T(8,128)(2,1)S(1)}, u32[]{:S(2)}, u32[]{:S(2)}) collective-permute-start(bf16[272,256]{1,0:T(8,128)(2,1)S(1)} %get-tuple-element.33.refs_0_), channel_id=1, source_target_pairs={{0,4},{4,0},{8,12},{12,8},{16,20},{20,16},{24,28},{28,24},{1,5},{5... | collective-permute-start | bytes 417800 | tf_op jit(solution)/shard_map/ppermute | solution.py:42
  8.6 4.6 %collective-permute-start.4 = (bf16[272,256]{1,0:T(8,128)(2,1)S(1)}, bf16[272,256]{1,0:T(8,128)(2,1)S(1)}, u32[]{:S(2)}, u32[]{:S(2)}) collective-permute-start(bf16[272,256]{1,0:T(8,128)(2,1)S(1)} %collective-permute-done.refs_1_), channel_id=1, source_target_pairs={{0,4},{4,0},{8,12},{12,8},{16,20},{20,16},{24,28},{28,24},{1,5},{5... | collective-permute-start | bytes 417800 | tf_op jit(solution)/shard_map/ppermute | solution.py:42
  12.6 1.4 %collective-permute-start.5 = (bf16[272,256]{1,0:T(8,128)(2,1)S(1)}, bf16[272,256]{1,0:T(8,128)(2,1)S(1)}, u32[]{:S(2)}, u32[]{:S(2)}) collective-permute-start(bf16[272,256]{1,0:T(8,128)(2,1)S(1)} %collective-permute-done.1.refs_2_), channel_id=1, source_target_pairs={{0,4},{4,0},{8,12},{12,8},{16,20},{20,16},{24,28},{28,24},{1,5},{5... | collective-permute-start | bytes 417800 | tf_op jit(solution)/shard_map/ppermute | solution.py:42
  12.6 1.6 %collective-permute-start.6 = (bf16[272,256]{1,0:T(8,128)(2,1)S(1)}, bf16[272,256]{1,0:T(8,128)(2,1)S(1)}, u32[]{:S(2)}, u32[]{:S(2)}) collective-permute-start(bf16[272,256]{1,0:T(8,128)(2,1)S(1)} %collective-permute-done.2.refs_3_), channel_id=1, source_target_pairs={{0,4},{4,0},{8,12},{12,8},{16,20},{20,16},{24,28},{28,24},{1,5},{5... | collective-permute-start | bytes 417800 | tf_op jit(solution)/shard_map/ppermute | solution.py:42
  41.0 6.2 %collective-permute-start.7 = (bf16[2,128,256]{2,1,0:T(8,128)(2,1)S(1)}, bf16[2,128,256]{2,1,0:T(8,128)(2,1)S(1)}, u32[]{:S(2)}, u32[]{:S(2)}) collective-permute-start(bf16[2,128,256]{2,1,0:T(8,128)(2,1)S(1)} %get-tuple-element.48), channel_id=1, source_target_pairs={{0,8},{4,12},{8,0},{12,4},{16,24},{20,28},{24,16},{28,20},{1,9},{5... | collective-permute-start | bytes 393224 | tf_op jit(solution)/shard_map/ppermute | solution.py:42
  41.6 7.9 %collective-permute-start.10 = (bf16[2,128,256]{2,1,0:T(8,128)(2,1)S(1)}, bf16[2,128,256]{2,1,0:T(8,128)(2,1)S(1)}, u32[]{:S(2)}, u32[]{:S(2)}) collective-permute-start(bf16[2,128,256]{2,1,0:T(8,128)(2,1)S(1)} %get-tuple-element.49), channel_id=1, source_target_pairs={{0,16},{4,20},{8,24},{12,28},{16,0},{20,4},{24,8},{28,12},{1,17},{... | collective-permute-start | bytes 393224 | tf_op jit(solution)/shard_map/ppermute | solution.py:42
  42.2 7.4 %collective-permute-start.11 = (bf16[2,128,256]{2,1,0:T(8,128)(2,1)S(1)}, bf16[2,128,256]{2,1,0:T(8,128)(2,1)S(1)}, u32[]{:S(2)}, u32[]{:S(2)}) collective-permute-start(bf16[2,128,256]{2,1,0:T(8,128)(2,1)S(1)} %get-tuple-element.50), channel_id=1, source_target_pairs={{0,24},{4,28},{8,16},{12,20},{16,8},{20,12},{24,0},{28,4},{1,25},{... | collective-permute-start | bytes 393224 | tf_op jit(solution)/shard_map/ppermute | solution.py:42
  44.5 5.5 %collective-permute-start.8 = (bf16[2,128,256]{2,1,0:T(8,128)(2,1)S(1)}, bf16[2,128,256]{2,1,0:T(8,128)(2,1)S(1)}, u32[]{:S(2)}, u32[]{:S(2)}) collective-permute-start(bf16[2,128,256]{2,1,0:T(8,128)(2,1)S(1)} %get-tuple-element.47.refs_0_), channel_id=1, source_target_pairs={{0,4},{4,0},{8,12},{12,8},{16,20},{20,16},{24,28},{28,24},{1,5},{5... | collective-permute-start | bytes 393224 | tf_op jit(solution)/shard_map/ppermute | solution.py:42
  47.2 2.9 %collective-permute-start.9 = (bf16[2,128,256]{2,1,0:T(8,128)(2,1)S(1)}, bf16[2,128,256]{2,1,0:T(8,128)(2,1)S(1)}, u32[]{:S(2)}, u32[]{:S(2)}) collective-permute-start(bf16[2,128,256]{2,1,0:T(8,128)(2,1)S(1)} %collective-permute-done.7.refs_1_), channel_id=1, source_target_pairs={{0,4},{4,0},{8,12},{12,8},{16,20},{20,16},{24,28},{28,24},{1,5},{5... | collective-permute-start | bytes 393224 | tf_op jit(solution)/shard_map/ppermute | solution.py:42
  49.6 1.4 %collective-permute-start.12 = (bf16[2,128,256]{2,1,0:T(8,128)(2,1)S(1)}, bf16[2,128,256]{2,1,0:T(8,128)(2,1)S(1)}, u32[]{:S(2)}, u32[]{:S(2)}) collective-permute-start(bf16[2,128,256]{2,1,0:T(8,128)(2,1)S(1)} %collective-permute-done.10.refs_0_), channel_id=1, source_target_pairs={{0,4},{4,0},{8,12},{12,8},{16,20},{20,16},{24,28},{28,24},{1,5},{5... | collective-permute-start | bytes 393224 | tf_op jit(solution)/shard_map/ppermute | solution.py:42
  49.6 1.5 %collective-permute-start.13 = (bf16[2,128,256]{2,1,0:T(8,128)(2,1)S(1)}, bf16[2,128,256]{2,1,0:T(8,128)(2,1)S(1)}, u32[]{:S(2)}, u32[]{:S(2)}) collective-permute-start(bf16[2,128,256]{2,1,0:T(8,128)(2,1)S(1)} %collective-permute-done.11.refs_1_), channel_id=1, source_target_pairs={{0,4},{4,0},{8,12},{12,8},{16,20},{20,16},{24,28},{28,24},{1,5},{5... | collective-permute-start | bytes 393224 | tf_op jit(solution)/shard_map/ppermute | solution.py:42

commit v6 on v5

--- a/solution.py
+++ b/solution.py
@@ -123,10 +123,18 @@
         put(out, row, block[:, :, part * width : (part + 1) * width].reshape(rows, width), lines)
 
 
-def prepare_kernel(dims, shifts, lines_ref, state_hbm, win_turned_hbm, wmid_hbm, wout_hbm, observed_hbm, *refs):
+def two_windows(weights, chan):
+    spare = jnp.zeros((chan, weights.shape[1]), weights.dtype)
+    return jnp.concatenate(
+        [jnp.concatenate([weights, spare], axis=0), jnp.concatenate([spare, weights], axis=0)], axis=1
+    )
+
+
+def prepare_kernel(dims, shifts, lines_ref, state_hbm, win_turned_hbm, wmid_hbm, wout_hbm, observed_hbm, *refs_all):
     members, chan = dims
-    outs, refs = refs[:-9], refs[-9:]
-    state, win_ref, wmid_ref, wmid_turned_ref, wout_turned_ref, win_turned, wout, observed, sems = refs[:9]
+    outs = refs_all[:-10]
+    state, win_ref, wmid_ref, wmid_turned_ref, wout_turned_ref, win_turned_ref, wout, observed = refs_all[-10:-2]
+    win_turned, sems = refs_all[-2:]
     rows = members * chan
     moves = (
         (wmid_hbm, wmid_ref), (win_turned_hbm, win_turned), (wout_hbm, wout), (observed_hbm, observed), (state_hbm, state),
@@ -138,9 +146,10 @@
         copy.wait()
     half = jnp.asarray(0.5, BF)
     wmid = wmid_ref[...]
+    win_turned_ref[...] = two_windows(win_turned[...], chan)
     win_ref[...] = win_turned[...].T * half
+    wout_turned_ref[...] = two_windows(wout[...], chan).T * half
     wmid_turned_ref[...] = wmid.T * half
-    wout_turned_ref[...] = wout[...].T * half
     wmid_ref[...] = wmid * half
     copies[-1].wait()
     if outs:
@@ -304,36 +313,43 @@
         padded[t + radius] = guidance.astype(BF).reshape(members, chan, width)
         sums[t + radius] = (guidance + total_ref[t]).reshape(members, chan, width)
 
-    def first(s):
+    def first(pair):
+        s = 2 * pair
         for m in range(members):
-            window = padded[pl.ds(s, WIN), m].reshape(WIN * chan, width)
-            grad = jnp.dot(wout_ref[...], window, preferred_element_type=F32)
-            grad_two[s, m] = (grad * twice_slope_of_half(pre_two_ref[s, m])).astype(BF)
+            fields = padded[pl.ds(s, WIN + 1), m].reshape((WIN + 1) * chan, width)
+            grad = jnp.dot(wout_ref[...], fields, preferred_element_type=F32).reshape(2, -1, width)
+            grad_two[pl.ds(s, 2), m] = (grad * twice_slope_of_half(pre_two_ref[pl.ds(s, 2), m])).astype(BF)
 
     def second(s):
         for m in range(members):
             grad = jnp.dot(wmid_ref[...], grad_two[s, m], preferred_element_type=F32)
             grad_one[s, m] = (grad * twice_slope_of_half(pre_one_ref[s, m])).astype(BF)
 
-    def third(s):
+    def third(pair):
+        s = 2 * pair
         for m in range(members):
-            blocks = jnp.dot(win_ref[...], grad_one[s, m], preferred_element_type=F32)
-            sums[pl.ds(s, WIN), m] += blocks.reshape(WIN, chan, width)
+            grad = grad_one[pl.ds(s, 2), m].reshape(-1, width)
+            blocks = jnp.dot(win_ref[...], grad, preferred_element_type=F32)
+            sums[pl.ds(s, WIN + 1), m] += blocks.reshape(WIN + 1, chan, width)
 
     loop(times, scatter)
-    loop(times, first)
+    loop(times // 2, first)
     loop(times, second)
-    loop(times, third)
+    loop(times // 2, third)
 
     for t, ref, row in departures(refs[:-4], times, shifts):
         ref[row] = sums[t + radius].reshape(rows, width).astype(BF)
 
 
-def update_kernel(dims, shifts, state_ref, *refs):
+def update_kernel(dims, places, state_ref, *refs):
     times, parts, members, chan, width = dims
     out_hbm, out, sems = refs[-3:]
     copies = []
-    for index, (t, ref, row) in enumerate(arrivals(refs[:-3], times, shifts)):
+    sources = arrivals(refs[:-3], times, None)
+    if places is not None:
+        me = lax.axis_index("tm")
+        sources = [(((me // 2) ^ s) * 2 + ((me % 2) ^ k), ref, k) for (s, k), ref in zip(places, refs)]
+    for index, (t, ref, row) in enumerate(sources):
         span = pl.ds((t // parts) * members, members)
         part = index % parts
         change = ref[row].reshape(members, chan, width).astype(F32)
@@ -346,8 +362,8 @@
         copy.wait()
 
 
-def update_rest_kernel(dims, shifts, written_hbm, state_ref, *refs):
-    update_kernel(dims, shifts, state_ref, *refs)
+def update_rest_kernel(dims, places, written_hbm, state_ref, *refs):
+    update_kernel(dims, places, state_ref, *refs)
 
 
 def body(noisy_state, w_in, w_mid, w_out, obs_pick, obs_slot, observed, precision):
@@ -391,6 +407,7 @@
         compiler_params=limit(16),
         name="pack",
     )(*here(current, obs_pick[0, 0], obs_slot[0, 0].T))
+    paired = ((WIN + 1) * chan, 2 * hidden)
     *own, state, win, wmid, wmid_turned, wout_turned, win_turned, wout, seen = pl.pallas_call(
         functools.partial(prepare_kernel, (members, chan), shifts and shifts[:1]),
         out_shape=(
@@ -399,14 +416,17 @@
             jax.ShapeDtypeStruct(w_in.shape, BF),
             jax.ShapeDtypeStruct(w_mid.shape, BF),
             jax.ShapeDtypeStruct(w_mid.shape[::-1], BF),
-            jax.ShapeDtypeStruct(w_out.shape[::-1], BF),
-            jax.ShapeDtypeStruct(w_in.shape[::-1], BF),
+            jax.ShapeDtypeStruct(paired[::-1], BF),
+            jax.ShapeDtypeStruct(paired, BF),
             jax.ShapeDtypeStruct(w_out.shape, BF),
             jax.ShapeDtypeStruct((positions, block_rows), F32),
         ),
         in_specs=[vmem] + [hbm] * 5,
         out_specs=(vmem,) * (first + 8),
-        scratch_shapes=[pltpu.SemaphoreType.DMA((5,))],
+        scratch_shapes=[
+            pltpu.VMEM(w_in.shape[::-1], BF),
+            pltpu.SemaphoreType.DMA((5,)),
+        ],
         compiler_params=limit(16),
         name="prepare",
     )(lines, *here(current, w_in.T, w_mid, w_out, observed.reshape(positions, block_rows)))
@@ -468,9 +488,11 @@
         name="backward",
     )(returned, lines, at_pixel, win_turned, wmid_turned, wout_turned, total, pre_one, pre_two)
     back = exchange(change, shifts)
-    early = sends // 2
-    mates = back[sends:]
-    stages = ((back[:early] + mates[:early], shifts[:early]), (back[early:sends] + mates[early:], shifts[early:])) if shifts else ((back, None),)
+    stages = ((back, None),)
+    if shifts:
+        places = [(s, k) for k in range(2) for s in shifts]
+        early = sends + sends // 2
+        stages = ((back[:early], places[:early]), (back[early:], places[early:]))
     updated = None
     for arrays, part_of in stages:
         kernel = update_kernel if updated is None else update_rest_kernel

time: 52.2 us -> 51.9 us (level)
  transfers between devices with their start and end apart: 14 -> 14, of which waited for: 7 -> 6; matrix products, arithmetic and copies ran while one was open for 0% -> 0% of each run, Pallas kernels for 4% -> 5%
where the time goes in v6:
time: 51.9 us; the launch traced here: 51.7 us
  blocking collectives  21.2 us (41%)
  waiting for transfers between devices  11.2 us (22%)
  Pallas kernels  10 us (19%)
  starting transfers between devices  9.23 us (18%)
    all_to_all x1, blocking collectives, body(): lax.all_to_all(packed, ('tm', 'lat'), split_axis=0, concat_axis=0, tiled=...  12.2 us
    ppermute x14, waiting for transfers between devices, swap(): lax.ppermute(values, 'tm', [(k, k ^ distance) for k in range(lax.axis_siz...  11.2 us
    ppermute x14, starting transfers between devices, swap(): lax.ppermute(values, 'tm', [(k, k ^ distance) for k in range(lax.axis_siz...  9.23 us
    all_to_all x1, blocking collectives, body(): lax.all_to_all(answer, ('tm', 'lat'), split_axis=0, concat_axis=0, tiled=...  8.99 us
    pallas_call x1, Pallas kernels, body(): pl.pallas_call(functools.partial(forward_kernel, dims, shifts), out_shape...  2.5 us
    pallas_call x1, Pallas kernels, body(): pl.pallas_call(functools.partial(backward_kernel, dims, shifts), out_shap...  2.46 us
    pallas_call x2, Pallas kernels, body(): pl.pallas_call(functools.partial(kernel, (times, parts, members, chan, wi...  1.75 us
    pallas_call x1, Pallas kernels, body(): pl.pallas_call(functools.partial(pack_kernel, (groups, parts, members, ch...  1.45 us
  transfers between devices with their start and end apart: 14, of which 6 were waited for; matrix products, arithmetic and copies ran while one was open for 0% of the time, Pallas kernels for 5%

profile of v6, /device:TPU:0, one launch (start us, length us, event | category | flops | bytes accessed | tf_op | source)
XLA Modules:
  0.0 51.7 jit_solution(17026936786778072510)
XLA Ops:
  0.0 0.0 copy-start
  0.0 1.5 %pack.1 = (bf16[272,256]{1,0:T(8,128)(2,1)S(1)}, bf16[272,256]{1,0:T(8,128)(2,1)S(1)}, bf16[272,256]{1,0:T(8,128)(2,1)S(1)}, bf16[16,256]{1,0:T(8,128)(2,1)S(1)}) custom-call(f32[16,64,256]{2,1,0:T(8,128)} %bitcast.12, s32[4,2,128]{2,1,0:T(2,128)} %bitcast.15, s32[2,4]{1,0:T(2,128)} %bitcast.17), custom_call_target="tpu_custom_call" | custom-call | tf_op jit(solution)/shard_map/pack/pallas_call | solution.py:393
  1.5 3.0 %collective-permute-start = (bf16[272,256]{1,0:T(8,128)(2,1)S(1)}, bf16[272,256]{1,0:T(8,128)(2,1)S(1)}, u32[]{:S(2)}, u32[]{:S(2)}) collective-permute-start(bf16[272,256]{1,0:T(8,128)(2,1)S(1)} %get-tuple-element.34), channel_id=1, source_target_pairs={{0,8},{4,12},{8,0},{12,4},{16,24},{20,28},{24,16},{28,20},{1,9},{5... | collective-permute-start | bytes 417800 | tf_op jit(solution)/shard_map/ppermute | solution.py:42
  4.5 1.5 %collective-permute-start.1 = (bf16[272,256]{1,0:T(8,128)(2,1)S(1)}, bf16[272,256]{1,0:T(8,128)(2,1)S(1)}, u32[]{:S(2)}, u32[]{:S(2)}) collective-permute-start(bf16[272,256]{1,0:T(8,128)(2,1)S(1)} %get-tuple-element.35), channel_id=1, source_target_pairs={{0,16},{4,20},{8,24},{12,28},{16,0},{20,4},{24,8},{28,12},{1,17},{... | collective-permute-start | bytes 417800 | tf_op jit(solution)/shard_map/ppermute | solution.py:42
  6.0 0.0 collective-permute-start.2
  6.0 1.4 %prepare.1 = (bf16[272,256]{1,0:T(8,128)(2,1)S(1)}, f32[16,64,256]{2,1,0:T(8,128)S(1)}, bf16[128,320]{1,0:T(8,128)(2,1)S(1)}, bf16[128,128]{1,0:T(8,128)(2,1)S(1...) custom-call(bf16[16,256]{1,0:T(8,128)(2,1)S(1)} %get-tuple-element.2, ...), custom_call_target="tpu_custom_call" | custom-call | tf_op jit(solution)/shard_map/prepare/pallas_call | solution.py:411
  7.5 0.1 collective-permute-start.3
  7.5 1.0 %collective-permute-done.refs_1_ = bf16[272,256]{1,0:T(8,128)(2,1)S(1)} collective-permute-done((bf16[272,256]{1,0:T(8,128)(2,1)S(1)}, bf16[272,256]{1,0:T(8,128)(2,1)S(1)}, u32[]{:S(2)}, u32[]{:S(2)}) %collective-permute-start) | collective-permute-done | bytes 139296 | tf_op jit(solution)/shard_map/ppermute | solution.py:42
  8.6 0.0 collective-permute-start.4
  8.6 4.1 %collective-permute-done.1.refs_2_ = bf16[272,256]{1,0:T(8,128)(2,1)S(1)} collective-permute-done((bf16[272,256]{1,0:T(8,128)(2,1)S(1)}, bf16[272,256]{1,0:T(8,128)(2,1)S(1)}, u32[]{:S(2)}, u32[]{:S(2)}) %collective-permute-start.1) | collective-permute-done | bytes 139296 | tf_op jit(solution)/shard_map/ppermute | solution.py:42
  12.6 0.0 collective-permute-start.5
  12.6 0.0 collective-permute-done.2.refs_3_
  12.6 0.5 collective-permute-start.6
  13.1 0.0 collective-permute-done.3.refs_4_
  13.1 0.0 collective-permute-done.4.refs_5_
  13.1 0.8 %collective-permute-done.5.refs_6_ = bf16[272,256]{1,0:T(8,128)(2,1)S(1)} collective-permute-done((bf16[272,256]{1,0:T(8,128)(2,1)S(1)}, bf16[272,256]{1,0:T(8,128)(2,1)S(1)}, u32[]{:S(2)}, u32[]{:S(2)}) %collective-permute-start.5) | collective-permute-done | bytes 139296 | tf_op jit(solution)/shard_map/ppermute | solution.py:42
  14.0 0.2 collective-permute-done.6.refs_7_
  14.2 2.5 %forward.1 = (bf16[32,8,128]{2,1,0:T(8,128)(2,1)S(1)}, f32[8,128,256]{2,1,0:T(8,128)S(1)}, f32[8,2,128,256]{3,2,1,0:T(8,128)S(1)}, f32[8,2,128,256]{3,2,1,0:T(8,...) custom-call(s32[1]{0:T(128)} %constant.17.clone.1.offset_ref, ...), custom_call_target="tpu_custom_call" | custom-call | tf_op jit(solution)/shard_map/forward/pallas_call | solution.py:440
  16.7 12.2 %all_to_all.10.recv_ref = bf16[32,8,128]{2,1,0:T(8,128)(2,1)S(1)} all-to-all(bf16[32,8,128]{2,1,0:T(8,128)(2,1)S(1)} %get-tuple-element.37), channel_id=1, replica_groups=mesh['tm'=8,'lat'=4] {'tm','lat'}, dimensions={0} | all-to-all | bytes 131072 | tf_op jit(solution)/shard_map/all_to_all | solution.py:461
  28.9 0.0 copy-done
  28.9 0.4 owner.1
  29.4 9.0 %all_to_all.11.recv_ref = bf16[32,4,128]{2,1,0:T(4,128)(2,1)S(1)} all-to-all(bf16[32,4,128]{2,1,0:T(4,128)(2,1)S(1)} %owner.1), channel_id=1, replica_groups=mesh['tm'=8,'lat'=4] {'tm','lat'}, dimensions={0} | all-to-all | bytes 65536 | tf_op jit(solution)/shard_map/all_to_all | solution.py:475
  38.4 2.5 %backward.1 = (bf16[2,128,256]{2,1,0:T(8,128)(2,1)S(1)}, bf16[2,128,256]{2,1,0:T(8,128)(2,1)S(1)}, bf16[2,128,256]{2,1,0:T(8,128)(2,1)S(1)}, bf16[2,128,256]{2,1,0:T(8,128)(2,1)S(1)}) custom-call(bf16[32,4,128]{2,1,0:T(4,128)(2,1)S(1)} %all_to_all.11.recv_ref, bf16[8,16,256]{2,1,0:T(8,128)(2,1)S(1)} %get-tuple-element.39.lines_ref, ...), custom_call_target="tpu_custom_call" | custom-call | tf_op jit(solution)/shard_map/backward/pallas_call | solution.py:476
  40.8 0.7 %collective-permute-start.7 = (bf16[2,128,256]{2,1,0:T(8,128)(2,1)S(1)}, bf16[2,128,256]{2,1,0:T(8,128)(2,1)S(1)}, u32[]{:S(2)}, u32[]{:S(2)}) collective-permute-start(bf16[2,128,256]{2,1,0:T(8,128)(2,1)S(1)} %get-tuple-element.48), channel_id=1, source_target_pairs={{0,8},{4,12},{8,0},{12,4},{16,24},{20,28},{24,16},{28,20},{1,9},{5... | collective-permute-start | bytes 393224 | tf_op jit(solution)/shard_map/ppermute | solution.py:42
  41.5 0.5 %collective-permute-start.8 = (bf16[2,128,256]{2,1,0:T(8,128)(2,1)S(1)}, bf16[2,128,256]{2,1,0:T(8,128)(2,1)S(1)}, u32[]{:S(2)}, u32[]{:S(2)}) collective-permute-start(bf16[2,128,256]{2,1,0:T(8,128)(2,1)S(1)} %get-tuple-element.49), channel_id=1, source_target_pairs={{0,16},{4,20},{8,24},{12,28},{16,0},{20,4},{24,8},{28,12},{1,17},{... | collective-permute-start | bytes 393224 | tf_op jit(solution)/shard_map/ppermute | solution.py:42
  42.0 2.4 %collective-permute-start.9 = (bf16[2,128,256]{2,1,0:T(8,128)(2,1)S(1)}, bf16[2,128,256]{2,1,0:T(8,128)(2,1)S(1)}, u32[]{:S(2)}, u32[]{:S(2)}) collective-permute-start(bf16[2,128,256]{2,1,0:T(8,128)(2,1)S(1)} %get-tuple-element.50), channel_id=1, source_target_pairs={{0,24},{4,28},{8,16},{12,20},{16,8},{20,12},{24,0},{28,4},{1,25},{... | collective-permute-start | bytes 393224 | tf_op jit(solution)/shard_map/ppermute | solution.py:42
  44.4 0.0 collective-permute-start.10
  44.4 2.6 %collective-permute-done.7.refs_1_ = bf16[2,128,256]{2,1,0:T(8,128)(2,1)S(1)} collective-permute-done((bf16[2,128,256]{2,1,0:T(8,128)(2,1)S(1)}, bf16[2,128,256]{2,1,0:T(8,128)(2,1)S(1)}, u32[]{:S(2)}, u32[]{:S(2)}) %collective-permute-start.7) | collective-permute-done | bytes 131104 | tf_op jit(solution)/shard_map/ppermute | solution.py:42
  47.0 0.0 collective-permute-start.11
  47.0 2.4 %collective-permute-done.8.refs_2_ = bf16[2,128,256]{2,1,0:T(8,128)(2,1)S(1)} collective-permute-done((bf16[2,128,256]{2,1,0:T(8,128)(2,1)S(1)}, bf16[2,128,256]{2,1,0:T(8,128)(2,1)S(1)}, u32[]{:S(2)}, u32[]{:S(2)}) %collective-permute-start.8) | collective-permute-done | bytes 131104 | tf_op jit(solution)/shard_map/ppermute | solution.py:42
  49.4 0.0 collective-permute-start.12
  49.4 0.0 collective-permute-done.9.refs_3_
  49.4 0.5 collective-permute-start.13
  49.9 0.0 collective-permute-done.10.refs_4_
  49.9 0.0 collective-permute-done.11.refs_5_
  49.9 1.0 %update.2.written_hbm = f32[16,64,256]{2,1,0:T(8,128)} custom-call(f32[16,64,256]{2,1,0:T(8,128)S(1)} %get-tuple-element.29.state_ref, bf16[2,128,256]{2,1,0:T(8,128)(2,1)S(1)} %get-tuple-element.47.refs_0_, bf16[2,128,256]{2,1,0:T(8,128)(2,1)S(1)} %collective-permute-done.7.refs_1_, bf16[2,128,256]{2,1,0:T(8,128)(2,1)S(1)} %collective-permute-done.8.refs_2_, ...), custom_call_target="tpu_custom_call" | custom-call | tf_op jit(solution)/shard_map/update/pallas_call | solution.py:500
  50.9 0.0 collective-permute-done.12.refs_0_
  50.9 0.0 collective-permute-done.13.refs_1_
  51.0 0.8 %update.3 = f32[16,64,256]{2,1,0:T(8,128)} custom-call(f32[16,64,256]{2,1,0:T(8,128)} %update.2.written_hbm, f32[16,64,256]{2,1,0:T(8,128)S(1)} %get-tuple-element.29.state_ref, bf16[2,128,256]{2,1,0:T(8,128)(2,1)S(1)} %collective-permute-done.12.refs_0_, bf16[2,128,256]{2,1,0:T(8,128)(2,1)S(1)} %collective-permute-done.13.refs_1_), custom_call_target="tpu_custom_call", output_to_operand_aliasing={{}: (0, {})} | custom-call | tf_op jit(solution)/shard_map/update/pallas_call | solution.py:500
Async XLA Ops:
  0.0 28.9 %copy-start = (bf16[1,1,1024,1024]{3,2,1,0:T(8,128)(2,1)S(1)}, bf16[1,1,1024,1024]{3,2,1,0:T(8,128)(2,1)}, u32[]{:S(2)}) copy-start(bf16[1,1,1024,1024]{3,2,1,0:T(8,128)(2,1)} %param.15) | copy-start | bytes 6291460
  1.5 7.1 %collective-permute-start = (bf16[272,256]{1,0:T(8,128)(2,1)S(1)}, bf16[272,256]{1,0:T(8,128)(2,1)S(1)}, u32[]{:S(2)}, u32[]{:S(2)}) collective-permute-start(bf16[272,256]{1,0:T(8,128)(2,1)S(1)} %get-tuple-element.34), channel_id=1, source_target_pairs={{0,8},{4,12},{8,0},{12,4},{16,24},{20,28},{24,16},{28,20},{1,9},{5... | collective-permute-start | bytes 417800 | tf_op jit(solution)/shard_map/ppermute | solution.py:42
  4.5 8.1 %collective-permute-start.1 = (bf16[272,256]{1,0:T(8,128)(2,1)S(1)}, bf16[272,256]{1,0:T(8,128)(2,1)S(1)}, u32[]{:S(2)}, u32[]{:S(2)}) collective-permute-start(bf16[272,256]{1,0:T(8,128)(2,1)S(1)} %get-tuple-element.35), channel_id=1, source_target_pairs={{0,16},{4,20},{8,24},{12,28},{16,0},{20,4},{24,8},{28,12},{1,17},{... | collective-permute-start | bytes 417800 | tf_op jit(solution)/shard_map/ppermute | solution.py:42
  6.0 6.6 %collective-permute-start.2 = (bf16[272,256]{1,0:T(8,128)(2,1)S(1)}, bf16[272,256]{1,0:T(8,128)(2,1)S(1)}, u32[]{:S(2)}, u32[]{:S(2)}) collective-permute-start(bf16[272,256]{1,0:T(8,128)(2,1)S(1)} %get-tuple-element.36), channel_id=1, source_target_pairs={{0,24},{4,28},{8,16},{12,20},{16,8},{20,12},{24,0},{28,4},{1,25},{... | collective-permute-start | bytes 417800 | tf_op jit(solution)/shard_map/ppermute | solution.py:42
  7.5 5.7 %collective-permute-start.3 = (bf16[272,256]{1,0:T(8,128)(2,1)S(1)}, bf16[272,256]{1,0:T(8,128)(2,1)S(1)}, u32[]{:S(2)}, u32[]{:S(2)}) collective-permute-start(bf16[272,256]{1,0:T(8,128)(2,1)S(1)} %get-tuple-element.33.refs_0_), channel_id=1, source_target_pairs={{0,4},{4,0},{8,12},{12,8},{16,20},{20,16},{24,28},{28,24},{1,5},{5... | collective-permute-start | bytes 417800 | tf_op jit(solution)/shard_map/ppermute | solution.py:42
  8.6 4.6 %collective-permute-start.4 = (bf16[272,256]{1,0:T(8,128)(2,1)S(1)}, bf16[272,256]{1,0:T(8,128)(2,1)S(1)}, u32[]{:S(2)}, u32[]{:S(2)}) collective-permute-start(bf16[272,256]{1,0:T(8,128)(2,1)S(1)} %collective-permute-done.refs_1_), channel_id=1, source_target_pairs={{0,4},{4,0},{8,12},{12,8},{16,20},{20,16},{24,28},{28,24},{1,5},{5... | collective-permute-start | bytes 417800 | tf_op jit(solution)/shard_map/ppermute | solution.py:42
  12.6 1.4 %collective-permute-start.5 = (bf16[272,256]{1,0:T(8,128)(2,1)S(1)}, bf16[272,256]{1,0:T(8,128)(2,1)S(1)}, u32[]{:S(2)}, u32[]{:S(2)}) collective-permute-start(bf16[272,256]{1,0:T(8,128)(2,1)S(1)} %collective-permute-done.1.refs_2_), channel_id=1, source_target_pairs={{0,4},{4,0},{8,12},{12,8},{16,20},{20,16},{24,28},{28,24},{1,5},{5... | collective-permute-start | bytes 417800 | tf_op jit(solution)/shard_map/ppermute | solution.py:42
  12.6 1.6 %collective-permute-start.6 = (bf16[272,256]{1,0:T(8,128)(2,1)S(1)}, bf16[272,256]{1,0:T(8,128)(2,1)S(1)}, u32[]{:S(2)}, u32[]{:S(2)}) collective-permute-start(bf16[272,256]{1,0:T(8,128)(2,1)S(1)} %collective-permute-done.2.refs_3_), channel_id=1, source_target_pairs={{0,4},{4,0},{8,12},{12,8},{16,20},{20,16},{24,28},{28,24},{1,5},{5... | collective-permute-start | bytes 417800 | tf_op jit(solution)/shard_map/ppermute | solution.py:42
  40.8 6.2 %collective-permute-start.7 = (bf16[2,128,256]{2,1,0:T(8,128)(2,1)S(1)}, bf16[2,128,256]{2,1,0:T(8,128)(2,1)S(1)}, u32[]{:S(2)}, u32[]{:S(2)}) collective-permute-start(bf16[2,128,256]{2,1,0:T(8,128)(2,1)S(1)} %get-tuple-element.48), channel_id=1, source_target_pairs={{0,8},{4,12},{8,0},{12,4},{16,24},{20,28},{24,16},{28,20},{1,9},{5... | collective-permute-start | bytes 393224 | tf_op jit(solution)/shard_map/ppermute | solution.py:42
  41.5 7.9 %collective-permute-start.8 = (bf16[2,128,256]{2,1,0:T(8,128)(2,1)S(1)}, bf16[2,128,256]{2,1,0:T(8,128)(2,1)S(1)}, u32[]{:S(2)}, u32[]{:S(2)}) collective-permute-start(bf16[2,128,256]{2,1,0:T(8,128)(2,1)S(1)} %get-tuple-element.49), channel_id=1, source_target_pairs={{0,16},{4,20},{8,24},{12,28},{16,0},{20,4},{24,8},{28,12},{1,17},{... | collective-permute-start | bytes 393224 | tf_op jit(solution)/shard_map/ppermute | solution.py:42
  42.0 7.4 %collective-permute-start.9 = (bf16[2,128,256]{2,1,0:T(8,128)(2,1)S(1)}, bf16[2,128,256]{2,1,0:T(8,128)(2,1)S(1)}, u32[]{:S(2)}, u32[]{:S(2)}) collective-permute-start(bf16[2,128,256]{2,1,0:T(8,128)(2,1)S(1)} %get-tuple-element.50), channel_id=1, source_target_pairs={{0,24},{4,28},{8,16},{12,20},{16,8},{20,12},{24,0},{28,4},{1,25},{... | collective-permute-start | bytes 393224 | tf_op jit(solution)/shard_map/ppermute | solution.py:42
  44.4 5.5 %collective-permute-start.10 = (bf16[2,128,256]{2,1,0:T(8,128)(2,1)S(1)}, bf16[2,128,256]{2,1,0:T(8,128)(2,1)S(1)}, u32[]{:S(2)}, u32[]{:S(2)}) collective-permute-start(bf16[2,128,256]{2,1,0:T(8,128)(2,1)S(1)} %get-tuple-element.47.refs_0_), channel_id=1, source_target_pairs={{0,4},{4,0},{8,12},{12,8},{16,20},{20,16},{24,28},{28,24},{1,5},{5... | collective-permute-start | bytes 393224 | tf_op jit(solution)/shard_map/ppermute | solution.py:42
  47.0 2.9 %collective-permute-start.11 = (bf16[2,128,256]{2,1,0:T(8,128)(2,1)S(1)}, bf16[2,128,256]{2,1,0:T(8,128)(2,1)S(1)}, u32[]{:S(2)}, u32[]{:S(2)}) collective-permute-start(bf16[2,128,256]{2,1,0:T(8,128)(2,1)S(1)} %collective-permute-done.7.refs_1_), channel_id=1, source_target_pairs={{0,4},{4,0},{8,12},{12,8},{16,20},{20,16},{24,28},{28,24},{1,5},{5... | collective-permute-start | bytes 393224 | tf_op jit(solution)/shard_map/ppermute | solution.py:42
  49.4 1.5 %collective-permute-start.12 = (bf16[2,128,256]{2,1,0:T(8,128)(2,1)S(1)}, bf16[2,128,256]{2,1,0:T(8,128)(2,1)S(1)}, u32[]{:S(2)}, u32[]{:S(2)}) collective-permute-start(bf16[2,128,256]{2,1,0:T(8,128)(2,1)S(1)} %collective-permute-done.8.refs_2_), channel_id=1, source_target_pairs={{0,4},{4,0},{8,12},{12,8},{16,20},{20,16},{24,28},{28,24},{1,5},{5... | collective-permute-start | bytes 393224 | tf_op jit(solution)/shard_map/ppermute | solution.py:42
  49.4 1.5 %collective-permute-start.13 = (bf16[2,128,256]{2,1,0:T(8,128)(2,1)S(1)}, bf16[2,128,256]{2,1,0:T(8,128)(2,1)S(1)}, u32[]{:S(2)}, u32[]{:S(2)}) collective-permute-start(bf16[2,128,256]{2,1,0:T(8,128)(2,1)S(1)} %collective-permute-done.9.refs_3_), channel_id=1, source_target_pairs={{0,4},{4,0},{8,12},{12,8},{16,20},{20,16},{24,28},{28,24},{1,5},{5... | collective-permute-start | bytes 393224 | tf_op jit(solution)/shard_map/ppermute | solution.py:42
